TPU v7x, 128 devices: a whole 4x4x4 slice. The times are simulated.
128 devices in a mesh: gx: 16 (over y, x), gy: 8 (over z, core).
Axes of the slice: x: 4, y: 4, z: 4, core: 2. Of those that a mesh axis runs over, the one named last changes fastest.
Arguments:
- records: bfloat16 [128, 128, 64, 128], P(('gx', 'gy')), may hold values from -6 to 6
- slot_voxels: int32 [128, 128, 256], P(('gx', 'gy')), may hold values from 0 to 8192, as said below
- brick_mask: int32 [32, 16, 4], P('gx', 'gy'), may hold values 0 or 1
- lift_weight: bfloat16 [32, 64], replicated, may hold values from -1 to 1
- leaf_convs: bfloat16 [2, 3, 3, 3, 64, 64], replicated, may hold values from -0.21875 to 0.21875
- down_leaf: bfloat16 [2, 2, 2, 64, 128], replicated, may hold values from -0.375 to 0.375
- down_coarse: bfloat16 [2, 2, 2, 2, 128, 128], replicated, may hold values from -0.25 to 0.25
- coarse_convs: bfloat16 [3, 3, 3, 3, 128, 128], replicated, may hold values from -0.15625 to 0.15625
Outputs:
- leaf_features: bfloat16 [256, 128, 16, 128], P('gx', 'gy')
- top_features: bfloat16 [32, 16, 4, 128], P('gx', 'gy')
Inputs may be any that keep to these rules, and one draw needn't show every extreme that they name: `slot_voxels`: entry [s, d, j] is owner d's local voxel index of slot j of the records that device s sends to owner d, or 8192 where that slot is empty; filled slots come first in each bucket; in every draw some owner receives 256 filled slots from every device, and every bucket has an empty slot unless its owner is such a full one.
All inputs are finite; a program needn't handle non-finite values. No bound on the sum of `brick_mask` on one device may be relied on, other than what follows from the above.
Results may differ from a plain program's by a relative error of at most 0.023.
Values may be sent and summed in bfloat16 or wider, within the bound.
No kernel may reach another device: no remote copies, remote signals or barrier semaphores. Data moves between devices by JAX's collectives and lax.ppermute only.
A program may use at most 64 MiB of HBM per device.

v0:
```python
import functools

import jax
import jax.numpy as jnp
from jax import lax
from jax.experimental import pallas as pl
from jax.experimental.pallas import tpu as pltpu
from jax.sharding import PartitionSpec as P

BRICK = 8
BUCKETS = 8


def with_halo(cells, sides, width):
    for axis, dim in sides:
        count = lax.axis_size(axis)
        here = lax.axis_index(axis)
        head = lax.slice_in_dim(cells, 0, width, axis=dim)
        tail = lax.slice_in_dim(cells, cells.shape[dim] - width, cells.shape[dim], axis=dim)
        before = lax.ppermute(tail, axis, [(i, (i + 1) % count) for i in range(count)])
        after = lax.ppermute(head, axis, [((i + 1) % count, i) for i in range(count)])
        before = jnp.where(here > 0, before, jnp.zeros_like(before))
        after = jnp.where(here < count - 1, after, jnp.zeros_like(after))
        cells = jnp.concatenate([before, cells, after], axis=dim)
    return cells


def join_columns(left_block, right_block):
    return jnp.concatenate([left_block, right_block], -1)


def leaf_taps(kernel):
    zero_block = jnp.zeros_like(kernel[:, :, 0])
    tap_low = kernel[:, :, 0]
    tap_mid = kernel[:, :, 1]
    tap_high = kernel[:, :, 2]
    from_before = jnp.concatenate(
        [join_columns(zero_block, zero_block), join_columns(tap_low, zero_block)], -2
    )
    from_middle = jnp.concatenate(
        [join_columns(tap_mid, tap_low), join_columns(tap_high, tap_mid)], -2
    )
    from_after = jnp.concatenate(
        [join_columns(zero_block, tap_high), join_columns(zero_block, zero_block)], -2
    )
    return jnp.concatenate([from_before, from_middle, from_after], -2)


def leaf_sweep(padded, tap_table, extent_x, extent_y):
    shifted = jnp.pad(padded, ((0, 0), (0, 0), (1, 1), (0, 0)))
    stacked = jnp.concatenate([shifted[:, :, :-2], shifted[:, :, 1:-1], shifted[:, :, 2:]], -1)
    summed = jnp.zeros((extent_x, extent_y, padded.shape[2], tap_table.shape[-1]), jnp.float32)
    for step_x in range(3):
        for step_y in range(3):
            window = stacked[step_x : step_x + extent_x, step_y : step_y + extent_y]
            summed = summed + jnp.einsum(
                "xyzk,kc->xyzc",
                window,
                tap_table[step_x, step_y],
                preferred_element_type=jnp.float32,
            )
    return summed


def leaf_layer(values, tap_table, occupied):
    padded = with_halo(values, (("gx", 0), ("gy", 1)), 1)
    swept = leaf_sweep(padded, tap_table, values.shape[0], values.shape[1])
    return (jax.nn.relu(swept) * occupied).astype(jnp.bfloat16)


def coarse_layer(values, kernel, occupied):
    padded = with_halo(values, (("gx", 0), ("gy", 1)), 1)
    padded = jnp.pad(padded, ((0, 0), (0, 0), (1, 1), (0, 0)))
    extent_x, extent_y, extent_z, channels = values.shape
    summed = jnp.zeros((extent_x, extent_y, extent_z, kernel.shape[-1]), jnp.float32)
    for step_x in range(3):
        for step_y in range(3):
            for step_z in range(3):
                window = padded[
                    step_x : step_x + extent_x,
                    step_y : step_y + extent_y,
                    step_z : step_z + extent_z,
                ]
                summed = summed + jnp.einsum(
                    "xyzk,kc->xyzc",
                    window,
                    kernel[step_x, step_y, step_z],
                    preferred_element_type=jnp.float32,
                )
    return (jax.nn.relu(summed) * occupied).astype(jnp.bfloat16)


def shrink_paired(values, kernel):
    extent_x, extent_y, extent_z, width = values.shape
    blocks = values.reshape(extent_x // 2, 2, extent_y // 2, 2, extent_z, width)
    merged = kernel.reshape(2, 2, width, kernel.shape[-1])
    return jnp.einsum("xaybzk,abko->xyzo", blocks, merged, preferred_element_type=jnp.float32)


def spread_mask(brick_mask, factor, factor_z):
    widened_mask = jnp.repeat(jnp.repeat(brick_mask, factor, 0), factor, 1)
    return jnp.repeat(widened_mask, factor_z, 2).astype(jnp.float32)


def pack_messages(records, slot_voxels):
    fours = slot_voxels.shape[-1] // 4
    high = (slot_voxels >> 9) * 16 + ((slot_voxels & 31) >> 1)
    low = ((slot_voxels >> 5) & 15) * 2 + (slot_voxels & 1)
    parity = lax.axis_index("gy") % 2
    source = lax.broadcasted_iota(jnp.int32, (4 * fours, 4, 2, fours), 0)
    quarter = lax.broadcasted_iota(jnp.int32, (4 * fours, 4, 2, fours), 1)
    side = lax.broadcasted_iota(jnp.int32, (4 * fours, 4, 2, fours), 2)
    row = lax.broadcasted_iota(jnp.int32, (4 * fours, 4, 2, fours), 3)
    picks = ((source == 4 * row + quarter) & (side == parity)).astype(jnp.bfloat16)
    picks = picks.reshape(4 * fours, 4 * 2 * fours)
    both = jnp.stack([high, low]).astype(jnp.bfloat16)
    ids = jnp.einsum("tds,sk->dtk", both, picks, preferred_element_type=jnp.float32)
    ids = ids.astype(jnp.bfloat16).reshape(slot_voxels.shape[0], 8, 2 * fours)
    return jnp.concatenate([records, ids], 1)


def scatter_kernel(msg_ref, lift_ref, cells_ref, total_ref):
    step = pl.program_id(0)

    @pl.when(step == 0)
    def _():
        total_ref[...] = jnp.zeros_like(total_ref)

    wide = 256
    lanes = lax.broadcasted_iota(jnp.int32, (wide, wide), 0).astype(jnp.bfloat16)
    zero = jnp.zeros((32, wide), jnp.bfloat16)
    for quad in range(BUCKETS // 4):
        turned, ids = [], []
        for pair in range(2):
            first = quad * 4 + pair * 2
            rows = jnp.concatenate([msg_ref[first, 0:64], msg_ref[first + 1, 0:64]], 0)
            turned.append(jnp.transpose(rows))
            ids.append(
                msg_ref[first, 64:72].astype(jnp.float32)
                + msg_ref[first + 1, 64:72].astype(jnp.float32)
            )
        turned = jnp.concatenate(turned, 1)
        ids = jnp.concatenate(ids, 1)
        for quarter in range(4):
            features = turned[quarter * 32 : quarter * 32 + 32]
            high = jnp.broadcast_to(ids[quarter : quarter + 1], (wide, wide)).astype(jnp.bfloat16)
            low = jnp.broadcast_to(ids[quarter + 4 : quarter + 5], (32, wide)).astype(jnp.bfloat16)
            hot = jnp.where(lanes == high, 1.0, 0.0).astype(jnp.bfloat16)
            spread = jnp.concatenate(
                [jnp.where(low == jnp.bfloat16(value), features, zero) for value in range(32)], 0
            )
            total_ref[...] += lax.dot_general(
                spread, hot, (((1,), (1,)), ((), ())), preferred_element_type=jnp.float32
            )

    @pl.when(step == pl.num_programs(0) - 1)
    def _():
        for part in range(4):
            summed = jnp.transpose(total_ref[part * wide : part * wide + wide])
            coarse = summed.astype(jnp.bfloat16)
            fine = (summed - coarse.astype(jnp.float32)).astype(jnp.bfloat16)
            lifted = jnp.dot(coarse, lift_ref[...], preferred_element_type=jnp.float32)
            lifted += jnp.dot(fine, lift_ref[...], preferred_element_type=jnp.float32)
            cells_ref[:, part * 512 : part * 512 + 512] = lifted.astype(jnp.bfloat16)


def scatter_and_lift(messages, lift_weight):
    sources, rows, width = messages.shape
    lift_block = jnp.kron(jnp.eye(8, dtype=jnp.bfloat16), lift_weight)
    return pl.pallas_call(
        scatter_kernel,
        grid=(sources // BUCKETS,),
        in_specs=[
            pl.BlockSpec((BUCKETS, rows, width), lambda i: (i, 0, 0)),
            pl.BlockSpec((256, 512), lambda i: (0, 0)),
        ],
        out_specs=pl.BlockSpec((256, 2048), lambda i: (0, 0)),
        out_shape=jax.ShapeDtypeStruct((256, 2048), jnp.bfloat16),
        scratch_shapes=[pltpu.VMEM((1024, 256), jnp.float32)],
        compiler_params=pltpu.CompilerParams(vmem_limit_bytes=48 << 20),
        name="scatter",
    )(messages, lift_block)


def per_device(
    records, slot_voxels, brick_mask, lift_weight, leaf_convs, down_leaf, down_coarse, coarse_convs
):
    messages = pack_messages(records[0], slot_voxels[0])
    arrived = lax.all_to_all(messages, ("gx", "gy"), split_axis=0, concat_axis=0, tiled=True)
    cells = scatter_and_lift(arrived, lift_weight)
    voxel_cells = cells.reshape(16, 16, 16, 128).transpose(0, 2, 1, 3)
    leaf_occupied = spread_mask(brick_mask, BRICK, BRICK // 2)
    taps_first = leaf_taps(leaf_convs[0])
    taps_second = leaf_taps(leaf_convs[1])
    first_layer = leaf_layer(voxel_cells, taps_first, leaf_occupied[..., None])
    second_layer = leaf_layer(first_layer, taps_second, leaf_occupied[..., None])
    level_input = second_layer
    for level_index in range(3):
        factor = BRICK // 2 ** (level_index + 1)
        occupied = spread_mask(brick_mask, factor, factor)[..., None]
        if level_index == 0:
            kernel = down_leaf
            paired = level_input
        else:
            kernel = down_coarse[level_index - 1]
            size_x, size_y, size_z, width = level_input.shape
            paired = level_input.reshape(size_x, size_y, size_z // 2, 2 * width)
        shrunk = (jax.nn.relu(shrink_paired(paired, kernel)) * occupied).astype(jnp.bfloat16)
        level_input = coarse_layer(shrunk, coarse_convs[level_index], occupied)
    return (second_layer, level_input)


def solution(mesh):
    in_specs = (
        P(("gx", "gy"), None, None, None),
        P(("gx", "gy"), None, None),
        P("gx", "gy", None),
        P(),
        P(),
        P(),
        P(),
        P(),
    )
    out_specs = (P("gx", "gy", None, None), P("gx", "gy", None, None))
    return jax.shard_map(
        per_device, mesh=mesh, in_specs=in_specs, out_specs=out_specs, check_vma=False
    )
```

profile of v0, /device:TPU:0, one launch (start us, length us, event | category | flops | bytes accessed | tf_op | source)
XLA Modules:
  0.0 193.1 jit_solution(1230462245516610805)
XLA Ops:
  2.4 3.3 %pad_maximum_fusion.2 = bf16[128,72,128]{2,1,0:T(8,128)(2,1)} fusion(bf16[128,8,128]{2,1,0:T(8,128)(2,1)S(1)} %copy.408, bf16[128,64,128]{2,1,0:T(8,128)(2,1)} %bitcast.653), kind=kLoop, calls=%fused_computation.5 | loop fusion | flops 4718592 | bytes 4718592 | tf_op jit(solution)/shard_map/concatenate | solution.py:119
  5.7 11.1 %all-to-all-start = ((bf16[128,72,128]{2,1,0:T(8,128)(2,1)}), bf16[128,72,128]{2,1,0:T(8,128)(2,1)S(1)}, u32[]{:S(2)}, u32[]{:S(2)}) async-start(bf16[128,72,128]{2,1,0:T(8,128)(2,1)} %pad_maximum_fusion.2), calls=%async_computation | async-start | bytes 4718592 | tf_op jit(solution)/shard_map/all_to_all | solution.py:189
  22.4 27.7 %all-to-all-done.msg_ref = bf16[128,72,128]{2,1,0:T(8,128)(2,1)S(1)} async-done(((bf16[128,72,128]{2,1,0:T(8,128)(2,1)}), bf16[128,72,128]{2,1,0:T(8,128)(2,1)S(1)}, u32[]{:S(2)}, u32[]{:S(2)}) %all-to-all-start) | async-done | bytes 2359328 | tf_op jit(solution)/shard_map/all_to_all | solution.py:189
  50.1 22.1 %scatter.1 = bf16[256,2048]{1,0:T(8,128)(2,1)S(1)} custom-call(bf16[128,72,128]{2,1,0:T(8,128)(2,1)S(1)} %all-to-all-done.msg_ref, bf16[256,512]{1,0:T(8,128)(2,1)S(1)} %mul.110.lift_ref), custom_call_target="tpu_custom_call" | custom-call | tf_op jit(solution)/shard_map/scatter/pallas_call | solution.py:170
  74.3 4.6 %collective-permute-start.1 = (bf16[1,16,16,128]{3,2,1,0:T(8,128)(2,1)S(1)}, bf16[1,16,16,128]{3,2,1,0:T(8,128)(2,1)S(1)}, u32[]{:S(2)}, u32[]{:S(2)}) collective-permute-start(bf16[1,16,16,128]{3,2,1,0:T(8,128)(2,1)S(1)} %get-tuple-element.18), channel_id=1, source_target_pairs={{8,0},{16,8},{24,16},{32,24},{40,32},{48,40},{56,48},{64,56},{72,6... | collective-permute-start | bytes 196616 | tf_op jit(solution)/shard_map/ppermute | solution.py:21
  81.7 2.9 %collective-permute-start.3 = (bf16[18,1,16,128]{3,2,1,0:T(8,128)(2,1)S(1)}, bf16[18,1,16,128]{3,2,1,0:T(8,128)(2,1)S(1)}, u32[]{:S(2)}, u32[]{:S(2)}) collective-permute-start(bf16[18,1,16,128]{3,2,1,0:T(8,128)(2,1)S(1)} %get-tuple-element.14), channel_id=1, source_target_pairs={{1,0},{2,1},{3,2},{4,3},{5,4},{6,5},{7,6},{0,7},{9,8},{10,9},{11,1... | collective-permute-start | bytes 221192 | tf_op jit(solution)/shard_map/ppermute | solution.py:21
  98.2 1.9 multiply_convert_fusion.1
  100.9 5.6 %collective-permute-start.5 = (bf16[1,16,16,128]{3,2,1,0:T(8,128)(2,1)S(1)}, bf16[1,16,16,128]{3,2,1,0:T(8,128)(2,1)S(1)}, u32[]{:S(2)}, u32[]{:S(2)}) collective-permute-start(bf16[1,16,16,128]{3,2,1,0:T(8,128)(2,1)S(1)} %get-tuple-element.16), channel_id=1, source_target_pairs={{8,0},{16,8},{24,16},{32,24},{40,32},{48,40},{56,48},{64,56},{72,6... | collective-permute-start | bytes 196616 | tf_op jit(solution)/shard_map/ppermute | solution.py:21
  109.2 2.9 %collective-permute-start.7 = (bf16[18,1,16,128]{3,2,1,0:T(8,128)(2,1)S(1)}, bf16[18,1,16,128]{3,2,1,0:T(8,128)(2,1)S(1)}, u32[]{:S(2)}, u32[]{:S(2)}) collective-permute-start(bf16[18,1,16,128]{3,2,1,0:T(8,128)(2,1)S(1)} %get-tuple-element.12), channel_id=1, source_target_pairs={{1,0},{2,1},{3,2},{4,3},{5,4},{6,5},{7,6},{0,7},{9,8},{10,9},{11,1... | collective-permute-start | bytes 221192 | tf_op jit(solution)/shard_map/ppermute | solution.py:21
  117.7 1.9 fusion.134
  119.6 1.9 fusion.135
  121.4 1.9 fusion.133
  125.2 1.9 fusion.131
  127.1 1.9 fusion.130
  129.0 1.9 fusion.129
  130.8 1.9 fusion.128
  132.7 2.8 %multiply_convert_fusion = bf16[16,16,16,128]{3,2,1,0:T(8,128)(2,1)S(1)} fusion(f32[16,16,16,128]{3,2,1,0:T(8,128)S(1)} %fusion.128, f32[16,16,16,128]{3,2,1,0:T(8,128)S(1)} %fusion.129, f32[16,16,16,128]{3,2,1,0:T(8,128)S(1)} %fusion.130, f32[16,16,16,128]{3,2,1,0:T(8,128)S(1)} %fusion.131, f32[16,16,16,128]{3,2,1,0:T(8,128)S(1)} %fusion.132, ...), kind=kOutput, calls=%fused_computation.6 | convolution fusion | flops 408420352 | bytes 21921792 | tf_op jit(solution)/shard_map/xyzk,kc->xyzc/dot_general | solution.py:56
  136.2 5.8 %collective-permute-start.9 = (bf16[1,8,16,128]{3,2,0,1:T(8,128)(2,1)S(1)}, bf16[1,8,16,128]{3,2,0,1:T(8,128)(2,1)S(1)}, u32[]{:S(2)}, u32[]{:S(2)}) collective-permute-start(bf16[1,8,16,128]{3,2,0,1:T(8,128)(2,1)S(1)} %get-tuple-element.32), channel_id=1, source_target_pairs={{8,0},{16,8},{24,16},{32,24},{40,32},{48,40},{56,48},{64,56},{72,6... | collective-permute-start | bytes 98312 | tf_op jit(solution)/shard_map/ppermute | solution.py:21
  143.6 6.7 %collective-permute-done.8 = bf16[1,8,16,128]{3,2,0,1:T(8,128)(2,1)S(1)} collective-permute-done((bf16[1,8,16,128]{3,2,0,1:T(8,128)(2,1)S(1)}, bf16[1,8,16,128]{3,2,0,1:T(8,128)(2,1)S(1)}, u32[]{:S(2)}, u32[]{:S(2)}) %collective-permute-start.8) | collective-permute-done | bytes 32800 | tf_op jit(solution)/shard_map/ppermute | solution.py:20
  150.7 2.9 %collective-permute-start.11 = (bf16[10,1,16,128]{3,2,0,1:T(8,128)(2,1)S(1)}, bf16[10,1,16,128]{3,2,0,1:T(8,128)(2,1)S(1)}, u32[]{:S(2)}, u32[]{:S(2)}) collective-permute-start(bf16[10,1,16,128]{3,2,0,1:T(8,128)(2,1)S(1)} %get-tuple-element.30), channel_id=1, source_target_pairs={{1,0},{2,1},{3,2},{4,3},{5,4},{6,5},{7,6},{0,7},{9,8},{10,9},{11,1... | collective-permute-start | bytes 122888 | tf_op jit(solution)/shard_map/ppermute | solution.py:21
  162.1 5.3 %collective-permute-start.13 = (bf16[1,4,8,128]{3,2,0,1:T(8,128)(2,1)S(1)}, bf16[1,4,8,128]{3,2,0,1:T(8,128)(2,1)S(1)}, u32[]{:S(2)}, u32[]{:S(2)}) collective-permute-start(bf16[1,4,8,128]{3,2,0,1:T(8,128)(2,1)S(1)} %get-tuple-element.38), channel_id=1, source_target_pairs={{8,0},{16,8},{24,16},{32,24},{40,32},{48,40},{56,48},{64,56},{72,6... | collective-permute-start | bytes 24584 | tf_op jit(solution)/shard_map/ppermute | solution.py:21
  169.2 3.0 %collective-permute-start.15 = (bf16[6,1,8,128]{3,2,0,1:T(8,128)(2,1)S(1)}, bf16[6,1,8,128]{3,2,0,1:T(8,128)(2,1)S(1)}, u32[]{:S(2)}, u32[]{:S(2)}) collective-permute-start(bf16[6,1,8,128]{3,2,0,1:T(8,128)(2,1)S(1)} %get-tuple-element.36), channel_id=1, source_target_pairs={{1,0},{2,1},{3,2},{4,3},{5,4},{6,5},{7,6},{0,7},{9,8},{10,9},{11,1... | collective-permute-start | bytes 36872 | tf_op jit(solution)/shard_map/ppermute | solution.py:21
  177.7 5.4 %collective-permute-start.17 = (bf16[1,2,4,128]{3,2,0,1:T(4,128)(2,1)S(1)}, bf16[1,2,4,128]{3,2,0,1:T(4,128)(2,1)S(1)}, u32[]{:S(2)}, u32[]{:S(2)}) collective-permute-start(bf16[1,2,4,128]{3,2,0,1:T(4,128)(2,1)S(1)} %get-tuple-element.42), channel_id=1, source_target_pairs={{8,0},{16,8},{24,16},{32,24},{40,32},{48,40},{56,48},{64,56},{72,6... | collective-permute-start | bytes 6152 | tf_op jit(solution)/shard_map/ppermute | solution.py:21
  184.9 2.9 %collective-permute-start.19 = (bf16[4,1,4,128]{3,2,0,1:T(4,128)(2,1)S(1)}, bf16[4,1,4,128]{3,2,0,1:T(4,128)(2,1)S(1)}, u32[]{:S(2)}, u32[]{:S(2)}) collective-permute-start(bf16[4,1,4,128]{3,2,0,1:T(4,128)(2,1)S(1)} %get-tuple-element.40), channel_id=1, source_target_pairs={{1,0},{2,1},{3,2},{4,3},{5,4},{6,5},{7,6},{0,7},{9,8},{10,9},{11,1... | collective-permute-start | bytes 12296 | tf_op jit(solution)/shard_map/ppermute | solution.py:21
  (240 shorter events, 61.4 us)
Async XLA Ops:
  0.6 134.9 %copy-start = (bf16[2,2,2,64,128]{4,3,2,1,0:T(8,128)(2,1)S(1)}, bf16[2,2,2,64,128]{4,3,2,1,0:T(8,128)(2,1)}, u32[]{:S(2)}) copy-start(bf16[2,2,2,64,128]{4,3,2,1,0:T(8,128)(2,1)} %param.13) | copy-start | bytes 393220
  5.7 11.6 %copy-start.8 = (s32[2,2,4]{2,1,0:T(2,128)S(1)}, s32[2,2,4]{2,1,0:T(2,128)}, u32[]{:S(2)}) copy-start(s32[2,2,4]{2,1,0:T(2,128)} %param.10) | copy-start | bytes 196
  5.7 44.4 %all-to-all-start = ((bf16[128,72,128]{2,1,0:T(8,128)(2,1)}), bf16[128,72,128]{2,1,0:T(8,128)(2,1)S(1)}, u32[]{:S(2)}, u32[]{:S(2)}) async-start(bf16[128,72,128]{2,1,0:T(8,128)(2,1)} %pad_maximum_fusion.2), calls=%async_computation | async-start | bytes 4718592 | tf_op jit(solution)/shard_map/all_to_all | solution.py:189
  72.7 7.7 %collective-permute-start = (bf16[1,16,16,128]{3,2,1,0:T(8,128)(2,1)S(1)}, bf16[1,16,16,128]{3,2,1,0:T(8,128)(2,1)S(1)}, u32[]{:S(2)}, u32[]{:S(2)}) collective-permute-start(bf16[1,16,16,128]{3,2,1,0:T(8,128)(2,1)S(1)} %get-tuple-element.17), channel_id=1, source_target_pairs={{0,8},{8,16},{16,24},{24,32},{32,40},{40,48},{48,56},{56,64},{64,7... | collective-permute-start | bytes 196616 | tf_op jit(solution)/shard_map/ppermute | solution.py:20
  74.3 6.5 %collective-permute-start.1 = (bf16[1,16,16,128]{3,2,1,0:T(8,128)(2,1)S(1)}, bf16[1,16,16,128]{3,2,1,0:T(8,128)(2,1)S(1)}, u32[]{:S(2)}, u32[]{:S(2)}) collective-permute-start(bf16[1,16,16,128]{3,2,1,0:T(8,128)(2,1)S(1)} %get-tuple-element.18), channel_id=1, source_target_pairs={{8,0},{16,8},{24,16},{32,24},{40,32},{48,40},{56,48},{64,56},{72,6... | collective-permute-start | bytes 196616 | tf_op jit(solution)/shard_map/ppermute | solution.py:21
  80.8 5.0 %collective-permute-start.2 = (bf16[18,1,16,128]{3,2,1,0:T(8,128)(2,1)S(1)}, bf16[18,1,16,128]{3,2,1,0:T(8,128)(2,1)S(1)}, u32[]{:S(2)}, u32[]{:S(2)}) collective-permute-start(bf16[18,1,16,128]{3,2,1,0:T(8,128)(2,1)S(1)} %get-tuple-element.13), channel_id=1, source_target_pairs={{0,1},{1,2},{2,3},{3,4},{4,5},{5,6},{6,7},{7,0},{8,9},{9,10},{10,1... | collective-permute-start | bytes 221192 | tf_op jit(solution)/shard_map/ppermute | solution.py:20
  81.7 4.9 %collective-permute-start.3 = (bf16[18,1,16,128]{3,2,1,0:T(8,128)(2,1)S(1)}, bf16[18,1,16,128]{3,2,1,0:T(8,128)(2,1)S(1)}, u32[]{:S(2)}, u32[]{:S(2)}) collective-permute-start(bf16[18,1,16,128]{3,2,1,0:T(8,128)(2,1)S(1)} %get-tuple-element.14), channel_id=1, source_target_pairs={{1,0},{2,1},{3,2},{4,3},{5,4},{6,5},{7,6},{0,7},{9,8},{10,9},{11,1... | collective-permute-start | bytes 221192 | tf_op jit(solution)/shard_map/ppermute | solution.py:21
  100.1 8.0 %collective-permute-start.4 = (bf16[1,16,16,128]{3,2,1,0:T(8,128)(2,1)S(1)}, bf16[1,16,16,128]{3,2,1,0:T(8,128)(2,1)S(1)}, u32[]{:S(2)}, u32[]{:S(2)}) collective-permute-start(bf16[1,16,16,128]{3,2,1,0:T(8,128)(2,1)S(1)} %get-tuple-element.15), channel_id=1, source_target_pairs={{0,8},{8,16},{16,24},{24,32},{32,40},{40,48},{48,56},{56,64},{64,7... | collective-permute-start | bytes 196616 | tf_op jit(solution)/shard_map/ppermute | solution.py:20
  100.9 7.6 %collective-permute-start.5 = (bf16[1,16,16,128]{3,2,1,0:T(8,128)(2,1)S(1)}, bf16[1,16,16,128]{3,2,1,0:T(8,128)(2,1)S(1)}, u32[]{:S(2)}, u32[]{:S(2)}) collective-permute-start(bf16[1,16,16,128]{3,2,1,0:T(8,128)(2,1)S(1)} %get-tuple-element.16), channel_id=1, source_target_pairs={{8,0},{16,8},{24,16},{32,24},{40,32},{48,40},{56,48},{64,56},{72,6... | collective-permute-start | bytes 196616 | tf_op jit(solution)/shard_map/ppermute | solution.py:21
  108.5 5.0 %collective-permute-start.6 = (bf16[18,1,16,128]{3,2,1,0:T(8,128)(2,1)S(1)}, bf16[18,1,16,128]{3,2,1,0:T(8,128)(2,1)S(1)}, u32[]{:S(2)}, u32[]{:S(2)}) collective-permute-start(bf16[18,1,16,128]{3,2,1,0:T(8,128)(2,1)S(1)} %get-tuple-element.11), channel_id=1, source_target_pairs={{0,1},{1,2},{2,3},{3,4},{4,5},{5,6},{6,7},{7,0},{8,9},{9,10},{10,1... | collective-permute-start | bytes 221192 | tf_op jit(solution)/shard_map/ppermute | solution.py:20
  109.2 4.9 %collective-permute-start.7 = (bf16[18,1,16,128]{3,2,1,0:T(8,128)(2,1)S(1)}, bf16[18,1,16,128]{3,2,1,0:T(8,128)(2,1)S(1)}, u32[]{:S(2)}, u32[]{:S(2)}) collective-permute-start(bf16[18,1,16,128]{3,2,1,0:T(8,128)(2,1)S(1)} %get-tuple-element.12), channel_id=1, source_target_pairs={{1,0},{2,1},{3,2},{4,3},{5,4},{6,5},{7,6},{0,7},{9,8},{10,9},{11,1... | collective-permute-start | bytes 221192 | tf_op jit(solution)/shard_map/ppermute | solution.py:21
  136.2 14.2 %copy-start.6 = (bf16[2,2,2,2,128,128]{5,4,3,2,1,0:T(8,128)(2,1)S(1)}, bf16[2,2,2,2,128,128]{5,4,3,2,1,0:T(8,128)(2,1)}, u32[]{:S(2)}) copy-start(bf16[2,2,2,2,128,128]{5,4,3,2,1,0:T(8,128)(2,1)} %param.14) | copy-start | bytes 1572868
  136.2 7.4 %collective-permute-start.9 = (bf16[1,8,16,128]{3,2,0,1:T(8,128)(2,1)S(1)}, bf16[1,8,16,128]{3,2,0,1:T(8,128)(2,1)S(1)}, u32[]{:S(2)}, u32[]{:S(2)}) collective-permute-start(bf16[1,8,16,128]{3,2,0,1:T(8,128)(2,1)S(1)} %get-tuple-element.32), channel_id=1, source_target_pairs={{8,0},{16,8},{24,16},{32,24},{40,32},{48,40},{56,48},{64,56},{72,6... | collective-permute-start | bytes 98312 | tf_op jit(solution)/shard_map/ppermute | solution.py:21
  143.1 7.2 %collective-permute-start.8 = (bf16[1,8,16,128]{3,2,0,1:T(8,128)(2,1)S(1)}, bf16[1,8,16,128]{3,2,0,1:T(8,128)(2,1)S(1)}, u32[]{:S(2)}, u32[]{:S(2)}) collective-permute-start(bf16[1,8,16,128]{3,2,0,1:T(8,128)(2,1)S(1)} %get-tuple-element.31), channel_id=1, source_target_pairs={{0,8},{8,16},{16,24},{24,32},{32,40},{40,48},{48,56},{56,64},{64,7... | collective-permute-start | bytes 98312 | tf_op jit(solution)/shard_map/ppermute | solution.py:20
  150.3 4.7 %collective-permute-start.10 = (bf16[10,1,16,128]{3,2,0,1:T(8,128)(2,1)S(1)}, bf16[10,1,16,128]{3,2,0,1:T(8,128)(2,1)S(1)}, u32[]{:S(2)}, u32[]{:S(2)}) collective-permute-start(bf16[10,1,16,128]{3,2,0,1:T(8,128)(2,1)S(1)} %get-tuple-element.29), channel_id=1, source_target_pairs={{0,1},{1,2},{2,3},{3,4},{4,5},{5,6},{6,7},{7,0},{8,9},{9,10},{10,1... | collective-permute-start | bytes 122888 | tf_op jit(solution)/shard_map/ppermute | solution.py:20
  150.7 4.6 %collective-permute-start.11 = (bf16[10,1,16,128]{3,2,0,1:T(8,128)(2,1)S(1)}, bf16[10,1,16,128]{3,2,0,1:T(8,128)(2,1)S(1)}, u32[]{:S(2)}, u32[]{:S(2)}) collective-permute-start(bf16[10,1,16,128]{3,2,0,1:T(8,128)(2,1)S(1)} %get-tuple-element.30), channel_id=1, source_target_pairs={{1,0},{2,1},{3,2},{4,3},{5,4},{6,5},{7,6},{0,7},{9,8},{10,9},{11,1... | collective-permute-start | bytes 122888 | tf_op jit(solution)/shard_map/ppermute | solution.py:21
  162.0 7.0 %collective-permute-start.12 = (bf16[1,4,8,128]{3,2,0,1:T(8,128)(2,1)S(1)}, bf16[1,4,8,128]{3,2,0,1:T(8,128)(2,1)S(1)}, u32[]{:S(2)}, u32[]{:S(2)}) collective-permute-start(bf16[1,4,8,128]{3,2,0,1:T(8,128)(2,1)S(1)} %get-tuple-element.37), channel_id=1, source_target_pairs={{0,8},{8,16},{16,24},{24,32},{32,40},{40,48},{48,56},{56,64},{64,7... | collective-permute-start | bytes 24584 | tf_op jit(solution)/shard_map/ppermute | solution.py:20
  162.1 7.0 %collective-permute-start.13 = (bf16[1,4,8,128]{3,2,0,1:T(8,128)(2,1)S(1)}, bf16[1,4,8,128]{3,2,0,1:T(8,128)(2,1)S(1)}, u32[]{:S(2)}, u32[]{:S(2)}) collective-permute-start(bf16[1,4,8,128]{3,2,0,1:T(8,128)(2,1)S(1)} %get-tuple-element.38), channel_id=1, source_target_pairs={{8,0},{16,8},{24,16},{32,24},{40,32},{48,40},{56,48},{64,56},{72,6... | collective-permute-start | bytes 24584 | tf_op jit(solution)/shard_map/ppermute | solution.py:21
  169.0 4.3 %collective-permute-start.14 = (bf16[6,1,8,128]{3,2,0,1:T(8,128)(2,1)S(1)}, bf16[6,1,8,128]{3,2,0,1:T(8,128)(2,1)S(1)}, u32[]{:S(2)}, u32[]{:S(2)}) collective-permute-start(bf16[6,1,8,128]{3,2,0,1:T(8,128)(2,1)S(1)} %get-tuple-element.35), channel_id=1, source_target_pairs={{0,1},{1,2},{2,3},{3,4},{4,5},{5,6},{6,7},{7,0},{8,9},{9,10},{10,1... | collective-permute-start | bytes 36872 | tf_op jit(solution)/shard_map/ppermute | solution.py:20
  169.2 4.4 %collective-permute-start.15 = (bf16[6,1,8,128]{3,2,0,1:T(8,128)(2,1)S(1)}, bf16[6,1,8,128]{3,2,0,1:T(8,128)(2,1)S(1)}, u32[]{:S(2)}, u32[]{:S(2)}) collective-permute-start(bf16[6,1,8,128]{3,2,0,1:T(8,128)(2,1)S(1)} %get-tuple-element.36), channel_id=1, source_target_pairs={{1,0},{2,1},{3,2},{4,3},{5,4},{6,5},{7,6},{0,7},{9,8},{10,9},{11,1... | collective-permute-start | bytes 36872 | tf_op jit(solution)/shard_map/ppermute | solution.py:21
  177.6 7.0 %collective-permute-start.16 = (bf16[1,2,4,128]{3,2,0,1:T(4,128)(2,1)S(1)}, bf16[1,2,4,128]{3,2,0,1:T(4,128)(2,1)S(1)}, u32[]{:S(2)}, u32[]{:S(2)}) collective-permute-start(bf16[1,2,4,128]{3,2,0,1:T(4,128)(2,1)S(1)} %get-tuple-element.41), channel_id=1, source_target_pairs={{0,8},{8,16},{16,24},{24,32},{32,40},{40,48},{48,56},{56,64},{64,7... | collective-permute-start | bytes 6152 | tf_op jit(solution)/shard_map/ppermute | solution.py:20
  177.7 7.0 %collective-permute-start.17 = (bf16[1,2,4,128]{3,2,0,1:T(4,128)(2,1)S(1)}, bf16[1,2,4,128]{3,2,0,1:T(4,128)(2,1)S(1)}, u32[]{:S(2)}, u32[]{:S(2)}) collective-permute-start(bf16[1,2,4,128]{3,2,0,1:T(4,128)(2,1)S(1)} %get-tuple-element.42), channel_id=1, source_target_pairs={{8,0},{16,8},{24,16},{32,24},{40,32},{48,40},{56,48},{64,56},{72,6... | collective-permute-start | bytes 6152 | tf_op jit(solution)/shard_map/ppermute | solution.py:21
  184.8 4.3 %collective-permute-start.18 = (bf16[4,1,4,128]{3,2,0,1:T(4,128)(2,1)S(1)}, bf16[4,1,4,128]{3,2,0,1:T(4,128)(2,1)S(1)}, u32[]{:S(2)}, u32[]{:S(2)}) collective-permute-start(bf16[4,1,4,128]{3,2,0,1:T(4,128)(2,1)S(1)} %get-tuple-element.39), channel_id=1, source_target_pairs={{0,1},{1,2},{2,3},{3,4},{4,5},{5,6},{6,7},{7,0},{8,9},{9,10},{10,1... | collective-permute-start | bytes 12296 | tf_op jit(solution)/shard_map/ppermute | solution.py:20
  184.9 4.3 %collective-permute-start.19 = (bf16[4,1,4,128]{3,2,0,1:T(4,128)(2,1)S(1)}, bf16[4,1,4,128]{3,2,0,1:T(4,128)(2,1)S(1)}, u32[]{:S(2)}, u32[]{:S(2)}) collective-permute-start(bf16[4,1,4,128]{3,2,0,1:T(4,128)(2,1)S(1)} %get-tuple-element.40), channel_id=1, source_target_pairs={{1,0},{2,1},{3,2},{4,3},{5,4},{6,5},{7,6},{0,7},{9,8},{10,9},{11,1... | collective-permute-start | bytes 12296 | tf_op jit(solution)/shard_map/ppermute | solution.py:21
  (6 other events, 35.6 us)
where the time goes:
time: 194 us; the launch traced here: 193 us
  starting transfers between devices  53.7 us (28%)
  waiting for transfers between devices  50 us (26%)
  matrix products  41.7 us (21%)
  Pallas kernels  22.1 us (11%)
  other arithmetic  12.8 us (7%)
  local copies, waits for them, and re-layouts  11.2 us (6%)
    ppermute x10, starting transfers between devices, with_halo(): lax.ppermute(head, axis, [((i + 1) % count, i) for i in range(count)])  41.4 us
    all_to_all x1, waiting for transfers between devices, per_device(): lax.all_to_all(messages, ('gx', 'gy'), split_axis=0, concat_axis=0, tiled...  27.7 us
    dot_general x18, matrix products, leaf_sweep(): jnp.einsum('xyzk,kc->xyzc', window, tap_table[step_x, step_y], preferred_...  27.5 us
    pallas_call x1, Pallas kernels, scatter_and_lift(): pl.pallas_call(scatter_kernel, grid=(sources // BUCKETS,), in_specs=[pl.B...  22.1 us
    ppermute x10, waiting for transfers between devices, with_halo(): lax.ppermute(tail, axis, [(i, (i + 1) % count) for i in range(count)])  19 us
    dot_general x81, matrix products, coarse_layer(): jnp.einsum('xyzk,kc->xyzc', window, kernel[step_x, step_y, step_z], prefe...  13.1 us
    all_to_all x1, starting transfers between devices, per_device(): lax.all_to_all(messages, ('gx', 'gy'), split_axis=0, concat_axis=0, tiled...  11.1 us
    unnamed x26, local copies, waits for them, and re-layouts  4.28 us
  transfers between devices with their start and end apart: 21, of which 19 were waited for; matrix products, arithmetic and copies ran while one was open for 5% of the time, Pallas kernels for 0%

commit v1 on v0

v1 whole, which is shorter than its diff:
```python
import functools

import jax
import jax.numpy as jnp
from jax import lax
from jax.experimental import pallas as pl
from jax.experimental.pallas import tpu as pltpu
from jax.sharding import PartitionSpec as P

BRICK = 8
BUCKETS = 8


def pack_messages(records, slot_voxels):
    fours = slot_voxels.shape[-1] // 4
    high = (slot_voxels >> 9) * 16 + ((slot_voxels & 31) >> 1)
    low = ((slot_voxels >> 5) & 15) * 2 + (slot_voxels & 1)
    parity = lax.axis_index("gy") % 2
    source = lax.broadcasted_iota(jnp.int32, (4 * fours, 4, 2, fours), 0)
    quarter = lax.broadcasted_iota(jnp.int32, (4 * fours, 4, 2, fours), 1)
    side = lax.broadcasted_iota(jnp.int32, (4 * fours, 4, 2, fours), 2)
    row = lax.broadcasted_iota(jnp.int32, (4 * fours, 4, 2, fours), 3)
    picks = ((source == 4 * row + quarter) & (side == parity)).astype(jnp.bfloat16)
    picks = picks.reshape(4 * fours, 4 * 2 * fours)
    both = jnp.stack([high, low]).astype(jnp.bfloat16)
    ids = jnp.einsum("tds,sk->dtk", both, picks, preferred_element_type=jnp.float32)
    ids = ids.astype(jnp.bfloat16).reshape(slot_voxels.shape[0], 8, 2 * fours)
    return jnp.concatenate([records, ids], 1)


def scatter_kernel(
    msg_ref, lift_ref, cells_ref, west_ref, east_ref, south_ref, north_ref, total_ref
):
    step = pl.program_id(0)

    @pl.when(step == 0)
    def _():
        total_ref[...] = jnp.zeros_like(total_ref)

    wide = 256
    lanes = lax.broadcasted_iota(jnp.int32, (wide, wide), 0).astype(jnp.bfloat16)
    zero = jnp.zeros((32, wide), jnp.bfloat16)
    for quad in range(BUCKETS // 4):
        turned, ids = [], []
        for pair in range(2):
            first = quad * 4 + pair * 2
            rows = jnp.concatenate([msg_ref[first, 0:64], msg_ref[first + 1, 0:64]], 0)
            turned.append(jnp.transpose(rows))
            ids.append(
                msg_ref[first, 64:72].astype(jnp.float32)
                + msg_ref[first + 1, 64:72].astype(jnp.float32)
            )
        turned = jnp.concatenate(turned, 1)
        ids = jnp.concatenate(ids, 1)
        for quarter in range(4):
            features = turned[quarter * 32 : quarter * 32 + 32]
            high = jnp.broadcast_to(ids[quarter : quarter + 1], (wide, wide)).astype(jnp.bfloat16)
            low = jnp.broadcast_to(ids[quarter + 4 : quarter + 5], (32, wide)).astype(jnp.bfloat16)
            hot = jnp.where(lanes == high, 1.0, 0.0).astype(jnp.bfloat16)
            spread = jnp.concatenate(
                [jnp.where(low == jnp.bfloat16(value), features, zero) for value in range(32)], 0
            )
            total_ref[...] += lax.dot_general(
                spread, hot, (((1,), (1,)), ((), ())), preferred_element_type=jnp.float32
            )

    @pl.when(step == pl.num_programs(0) - 1)
    def _():
        for part in range(4):
            summed = jnp.transpose(total_ref[part * wide : part * wide + wide])
            coarse = summed.astype(jnp.bfloat16)
            west_ref[:, part * wide : part * wide + wide] = coarse[:64]
            east_ref[:, part * wide : part * wide + wide] = coarse[192:]
            if part == 0:
                south_ref[...] = coarse
            if part == 3:
                north_ref[...] = coarse
            fine = (summed - coarse.astype(jnp.float32)).astype(jnp.bfloat16)
            lifted = jnp.dot(coarse, lift_ref[...], preferred_element_type=jnp.float32)
            lifted += jnp.dot(fine, lift_ref[...], preferred_element_type=jnp.float32)
            cells_ref[:, part * 512 : part * 512 + 512] = lifted.astype(jnp.bfloat16)


def scatter_and_lift(messages, lift_block):
    sources, rows, width = messages.shape
    shapes = [(256, 2048), (64, 1024), (64, 1024), (256, 256), (256, 256)]
    return pl.pallas_call(
        scatter_kernel,
        grid=(sources // BUCKETS,),
        in_specs=[
            pl.BlockSpec((BUCKETS, rows, width), lambda i: (i, 0, 0)),
            pl.BlockSpec((256, 512), lambda i: (0, 0)),
        ],
        out_specs=[pl.BlockSpec(shape, lambda i: (0, 0)) for shape in shapes],
        out_shape=[jax.ShapeDtypeStruct(shape, jnp.bfloat16) for shape in shapes],
        scratch_shapes=[pltpu.VMEM((1024, 256), jnp.float32)],
        compiler_params=pltpu.CompilerParams(vmem_limit_bytes=24 << 20),
        name="scatter",
    )(messages, lift_block)


def leaf_taps_kernel(convs_ref, taps_ref):
    zero = jnp.zeros((64, 64), jnp.bfloat16)
    for layer in range(2):
        for dx in range(3):
            for kind in range(2):
                for step_y in range(4):
                    for half in range(2):
                        row = kind * 512 + step_y * 128 + half * 64
                        for out_y in range(2):
                            blocks = []
                            for out_z in range(2):
                                dy = step_y - out_y
                                if kind == 0:
                                    dz = half - out_z + 1
                                else:
                                    dz = 3 - out_z if half == 0 else -out_z
                                inside = 0 <= dy <= 2 and 0 <= dz <= 2
                                blocks.append(convs_ref[layer, dx, dy, dz] if inside else zero)
                            taps_ref[layer, dx, row : row + 64, out_y * 128 : out_y * 128 + 128] = (
                                jnp.concatenate(blocks, 1)
                            )


def leaf_taps(leaf_convs):
    return pl.pallas_call(
        leaf_taps_kernel,
        out_shape=jax.ShapeDtypeStruct((2, 3, 1024, 256), jnp.bfloat16),
        name="leaf_taps",
    )(leaf_convs)


def row_shifts(values, period):
    count = values.shape[0]
    place = lax.rem(lax.broadcasted_iota(jnp.int32, values.shape, 0), period)
    before = jnp.where(place == 0, 0.0, pltpu.roll(values, 1, 0))
    after = jnp.where(place == period - 1, 0.0, pltpu.roll(values, count - 1, 0))
    return before, after


def z_neighbours(values):
    before, after = row_shifts(values, 16)
    lane = lax.rem(lax.broadcasted_iota(jnp.int32, values.shape, 1), 128)
    return jnp.where(lane < 64, after, before).astype(jnp.bfloat16)


def leaf_kernel(
    cells_ref,
    west_ref,
    east_ref,
    south_ref,
    north_ref,
    lift_ref,
    taps_ref,
    down_leaf_ref,
    coarse_ref,
    down_ref,
    leaf_mask_ref,
    mid_mask_ref,
    features_ref,
    down_two_ref,
    cell_ref,
    cell_z_ref,
    one_ref,
    one_z_ref,
    down_one_ref,
    parts_ref,
):
    here_x = lax.axis_index("gx")
    here_y = lax.axis_index("gy")
    from_west = jnp.where(here_x > 0, 1.0, 0.0)
    from_east = jnp.where(here_x < lax.axis_size("gx") - 1, 1.0, 0.0)
    from_south = jnp.where(here_y > 0, 1.0, 0.0)
    from_north = jnp.where(here_y < lax.axis_size("gy") - 1, 1.0, 0.0)
    lift = lift_ref[...]

    def place(row, lane, values):
        rows, lanes = values.shape
        cell_ref[row : row + rows, lane : lane + lanes] = values.astype(jnp.bfloat16)

    cell_ref[64:320, 512:2560] = cells_ref[...]
    for part in range(4):
        for row, ref, flag in ((0, west_ref, from_west), (320, east_ref, from_east)):
            sums = ref[:, part * 256 : part * 256 + 256]
            lifted = jnp.dot(sums, lift, preferred_element_type=jnp.float32)
            place(row, 512 + part * 512, lifted * flag)
    for lane, ref, flag in ((0, south_ref, from_south), (2560, north_ref, from_north)):
        for row, rows, other in ((0, 64, from_west), (64, 256, 1.0), (320, 64, from_east)):
            lifted = jnp.dot(ref[row : row + rows], lift, preferred_element_type=jnp.float32)
            place(row, lane, lifted * (flag * other))

    @pl.loop(0, 12)
    def _(step):
        lanes = pl.ds(pl.multiple_of(step * 256, 256), 256)
        cell_z_ref[:, lanes] = z_neighbours(cell_ref[:, lanes].astype(jnp.float32))

    def sweep(layer, source_ref, source_z_ref, rows, step):
        lanes = pl.ds(pl.multiple_of(step * 256, 256), 512)
        pieces = []
        for dx in range(3):
            pieces.append(source_ref[dx * 16 : dx * 16 + rows, lanes])
            pieces.append(source_z_ref[dx * 16 : dx * 16 + rows, lanes])
        taps = taps_ref[layer].reshape(3072, 256)
        total = jnp.dot(jnp.concatenate(pieces, 1), taps, preferred_element_type=jnp.float32)
        return jnp.maximum(total, 0.0)

    @pl.loop(0, 11)
    def _(step):
        total = sweep(0, cell_ref, cell_z_ref, 352, step)
        masks = [leaf_mask_ref[(2 * step + half + 5) // 8, 16:368] for half in range(2)]
        values = (total * jnp.concatenate(masks, 1)).astype(jnp.bfloat16)
        lanes = pl.ds(pl.multiple_of(step * 256, 256), 256)
        one_ref[:, lanes] = values
        one_z_ref[:, lanes] = z_neighbours(values.astype(jnp.float32))

    @pl.loop(0, 10)
    def _(step):
        total = sweep(1, one_ref, one_z_ref, 320, step)
        mask = leaf_mask_ref[(2 * step + 6) // 8, 32:352]
        values = (total * jnp.concatenate([mask, mask], 1)).astype(jnp.bfloat16)

        @pl.when((step >= 1) & (step < 9))
        def _():
            for half in range(2):
                inner = values[32:288, half * 128 : half * 128 + 128]
                features_ref[:, 2 * step - 2 + half] = inner.reshape(16, 16, 128)

        pairs = values.reshape(10, 2, 16, 256)
        merged = jnp.concatenate(
            [pairs[:, 0].reshape(160, 256), pairs[:, 1].reshape(160, 256)], 1
        )
        total = jnp.dot(merged, down_leaf_ref[...], preferred_element_type=jnp.float32)
        mask = mask.reshape(10, 2, 16, 128)[:, 0].reshape(160, 128)
        down = (jnp.maximum(total, 0.0) * mask).astype(jnp.bfloat16)
        before, after = row_shifts(down.astype(jnp.float32), 16)
        lanes = pl.ds(pl.multiple_of(step * 128, 128), 128)
        down_one_ref[0, :, lanes] = before.astype(jnp.bfloat16)
        down_one_ref[1, :, lanes] = down
        down_one_ref[2, :, lanes] = after.astype(jnp.bfloat16)

    windows = []
    for y in range(8):
        windows.append(
            jnp.concatenate(
                [
                    down_one_ref[dz, dx * 16 : dx * 16 + 128, y * 128 : y * 128 + 384]
                    for dx in range(3)
                    for dz in range(3)
                ],
                1,
            )
        )
    total = jnp.dot(jnp.concatenate(windows, 0), coarse_ref[...], preferred_element_type=jnp.float32)
    total = jnp.maximum(total, 0.0).reshape(8, 128, 128)
    masks = [leaf_mask_ref[1 + y // 4, 64:320].reshape(8, 2, 16, 128)[:, 0] for y in range(8)]
    level = total * jnp.concatenate(masks, 0).reshape(8, 128, 128)
    level = level.astype(jnp.bfloat16).reshape(4, 2, 4, 2, 16, 128)
    merged = jnp.concatenate(
        [level[:, b, :, a].reshape(256, 128) for a in range(2) for b in range(2)], 1
    )
    parts = jnp.dot(merged, down_ref[...], preferred_element_type=jnp.float32)
    parts_ref[0] = parts[:, :128]
    parts_ref[1] = parts[:, 128:]
    total = parts_ref[0, pl.ds(0, 128, stride=2)] + parts_ref[1, pl.ds(1, 128, stride=2)]
    mask = mid_mask_ref[2:6, 2:6].reshape(128, 128)
    down_two_ref[...] = (jnp.maximum(total, 0.0) * mask).astype(jnp.bfloat16)


def leaf_levels(cells, halos, lift_block, taps, down_leaf, coarse, down, leaf_mask, mid_mask):
    return pl.pallas_call(
        leaf_kernel,
        out_shape=[
            jax.ShapeDtypeStruct((16, 16, 16, 128), jnp.bfloat16),
            jax.ShapeDtypeStruct((128, 128), jnp.bfloat16),
        ],
        scratch_shapes=[
            pltpu.VMEM((384, 3072), jnp.bfloat16),
            pltpu.VMEM((384, 3072), jnp.bfloat16),
            pltpu.VMEM((352, 2816), jnp.bfloat16),
            pltpu.VMEM((352, 2816), jnp.bfloat16),
            pltpu.VMEM((3, 160, 1280), jnp.bfloat16),
            pltpu.VMEM((2, 256, 128), jnp.float32),
        ],
        compiler_params=pltpu.CompilerParams(vmem_limit_bytes=40 << 20),
        name="leaf_levels",
    )(cells, *halos, lift_block, taps, down_leaf, coarse, down, leaf_mask, mid_mask)


def coarse_kernel(
    south_ref,
    middle_ref,
    north_ref,
    coarse_ref,
    down_ref,
    last_ref,
    mid_mask_ref,
    top_mask_ref,
    top_ref,
    parts_ref,
):
    here_x = lax.axis_index("gx")
    here_y = lax.axis_index("gy")
    from_west = jnp.where(here_x > 0, 1.0, 0.0)
    from_east = jnp.where(here_x < lax.axis_size("gx") - 1, 1.0, 0.0)
    from_south = jnp.where(here_y > 0, 1.0, 0.0)
    from_north = jnp.where(here_y < lax.axis_size("gy") - 1, 1.0, 0.0)

    strips = []
    for ref, first, flag in ((south_ref, 1, from_south), (middle_ref, 0, 1.0), (north_ref, 0, from_north)):
        count = 4 if ref is middle_ref else 3
        tiles = [ref[i].astype(jnp.float32).reshape(4, 4, 8, 128) for i in range(3)]
        tiles = [tile[first : first + count] for tile in tiles]
        tiles = [
            tiles[0][:, 1:] * (flag * from_west),
            tiles[1] * flag,
            tiles[2][:, :3] * (flag * from_east),
        ]
        strips.append(jnp.concatenate(tiles, 1))
    grid = jnp.concatenate(strips, 0)
    before, after = row_shifts(grid.reshape(800, 128), 8)
    grids = [before.reshape(10, 10, 8, 128), grid, after.reshape(10, 10, 8, 128)]
    pieces = [
        grids[dz][dy : dy + 8, dx : dx + 8].reshape(512, 128).astype(jnp.bfloat16)
        for dx in range(3)
        for dy in range(3)
        for dz in range(3)
    ]
    total = jnp.dot(jnp.concatenate(pieces, 1), coarse_ref[...], preferred_element_type=jnp.float32)
    level = jnp.maximum(total, 0.0) * mid_mask_ref[...].reshape(512, 128)
    level = level.reshape(4, 2, 4, 2, 8, 128)
    merged = jnp.concatenate(
        [level[:, b, :, a].reshape(128, 128) for a in range(2) for b in range(2)], 1
    ).astype(jnp.bfloat16)
    parts = jnp.dot(merged, down_ref[...], preferred_element_type=jnp.float32)
    parts_ref[0] = parts[:, :128]
    parts_ref[1] = parts[:, 128:]
    total = parts_ref[0, pl.ds(0, 64, stride=2)] + parts_ref[1, pl.ds(1, 64, stride=2)]
    down = jnp.maximum(total, 0.0) * top_mask_ref[...]
    down = down.astype(jnp.bfloat16).astype(jnp.float32)
    before, after = row_shifts(down, 4)
    shifted = [before, down, after]
    pieces = []
    for dx in range(3):
        for dy in range(3):
            for dz in range(3):
                turn = (64 - (dy - 1) * 16 - (dx - 1) * 4) % 64
                moved = pltpu.roll(shifted[dz], turn, 0) if turn else shifted[dz]
                pieces.append(moved.astype(jnp.bfloat16))
    total = jnp.dot(jnp.concatenate(pieces, 1), last_ref[...], preferred_element_type=jnp.float32)
    top = (jnp.maximum(total, 0.0) * top_mask_ref[...]).astype(jnp.bfloat16)
    for x in range(2):
        for y in range(2):
            row = (y + 1) * 16 + (x + 1) * 4
            top_ref[x, y] = top[row : row + 4]


def coarse_levels(south, middle, north, coarse, down, last, mid_mask, top_mask):
    return pl.pallas_call(
        coarse_kernel,
        out_shape=jax.ShapeDtypeStruct((2, 2, 4, 128), jnp.bfloat16),
        scratch_shapes=[pltpu.VMEM((2, 128, 128), jnp.float32)],
        compiler_params=pltpu.CompilerParams(vmem_limit_bytes=24 << 20),
        name="coarse_levels",
    )(south, middle, north, coarse, down, last, mid_mask, top_mask)


def ring(values, axis, step):
    count = lax.axis_size(axis)
    return lax.ppermute(values, axis, [(i, (i + step) % count) for i in range(count)])


def masks_of(brick_mask):
    size_x, size_y, size_z = brick_mask.shape
    count_x, count_y = lax.axis_size("gx"), lax.axis_size("gy")
    whole = lax.all_gather(brick_mask, ("gx", "gy"), axis=0, tiled=False)
    whole = whole.reshape(count_x, count_y, size_x, size_y, size_z).transpose(0, 2, 1, 3, 4)
    whole = whole.reshape(count_x * size_x, count_y * size_y, size_z).astype(jnp.float32)
    whole = jnp.pad(whole, ((1, 1), (1, 1), (0, 0)))
    start = (lax.axis_index("gx") * size_x, lax.axis_index("gy") * size_y, 0)
    near = lax.dynamic_slice(whole, start, (size_x + 2, size_y + 2, size_z))
    near = near.transpose(1, 0, 2)
    leaf = jnp.repeat(jnp.repeat(near, 8, 1)[:, 4:28], 4, 2).reshape(4, 384, 1)
    middle = jnp.repeat(jnp.repeat(jnp.repeat(near, 2, 0), 2, 1), 2, 2)[..., None]
    top = near.reshape(64, 1)
    return (
        jnp.broadcast_to(leaf, (4, 384, 128)),
        jnp.broadcast_to(middle, (8, 8, 8, 128)),
        jnp.broadcast_to(top, (64, 128)),
    )


def per_device(
    records, slot_voxels, brick_mask, lift_weight, leaf_convs, down_leaf, down_coarse, coarse_convs
):
    messages = pack_messages(records[0], slot_voxels[0])
    arrived = lax.all_to_all(messages, ("gx", "gy"), split_axis=0, concat_axis=0, tiled=True)
    leaf_mask, mid_mask, top_mask = masks_of(brick_mask)
    lift_block = jnp.kron(jnp.eye(8, dtype=jnp.bfloat16), lift_weight)
    taps = leaf_taps(leaf_convs)
    coarse_one = coarse_convs[0].transpose(0, 2, 1, 3, 4).reshape(3456, 128)
    coarse_two = coarse_convs[1].reshape(3456, 128)
    coarse_three = coarse_convs[2].reshape(3456, 128)
    downs = down_coarse.transpose(0, 1, 2, 4, 3, 5).reshape(2, 512, 256)

    cells, low_x, high_x, low_y, high_y = scatter_and_lift(arrived, lift_block)
    west = ring(high_x, "gx", 1)
    east = ring(low_x, "gx", -1)
    south = ring(jnp.concatenate([west[:, 768:], high_y, east[:, 768:]], 0), "gy", 1)
    north = ring(jnp.concatenate([west[:, :256], low_y, east[:, :256]], 0), "gy", -1)
    features, down_two = leaf_levels(
        cells,
        (west, east, south, north),
        lift_block,
        taps,
        down_leaf.reshape(512, 128),
        coarse_one,
        downs[0],
        leaf_mask,
        mid_mask,
    )
    middle = jnp.stack([ring(down_two, "gx", 1), down_two, ring(down_two, "gx", -1)])
    top = coarse_levels(
        ring(middle, "gy", 1),
        middle,
        ring(middle, "gy", -1),
        coarse_two,
        downs[1],
        coarse_three,
        mid_mask,
        top_mask,
    )
    return (features, top)


def solution(mesh):
    in_specs = (
        P(("gx", "gy"), None, None, None),
        P(("gx", "gy"), None, None),
        P("gx", "gy", None),
        P(),
        P(),
        P(),
        P(),
        P(),
    )
    out_specs = (P("gx", "gy", None, None), P("gx", "gy", None, None))
    return jax.shard_map(
        per_device, mesh=mesh, in_specs=in_specs, out_specs=out_specs, check_vma=False
    )
```

time: 194 us -> 169 us (0.87)
  blocking collectives: 0 us -> 56.5 us
  waiting for transfers between devices: 50 us -> 7.28 us
  matrix products: 41.7 us -> 0.32 us
  Pallas kernels: 22.1 us -> 52.1 us
  starting transfers between devices: 53.7 us -> 25.9 us
  local copies, waits for them, and re-layouts: 11.2 us -> 19.8 us
  other arithmetic: 12.8 us -> 5.91 us
    all_gather x0 -> x1, blocking collectives: none -> 56.5 us  [masks_of(): whole = lax.all_gather(brick_mask, ('gx', 'gy'), axis=0, tiled=False)]
    dot_general x102 -> x0, matrix products: 41.4 us -> none  [the longest x18 27.5 us: leaf_sweep(): jnp.einsum('xyzk,kc->xyzc', window, tap_table[step_x, step_y], preferred_...]
    pallas_call x0 -> x3, Pallas kernels: none -> 29.3 us  [the longest x1 23.5 us: leaf_levels(): pl.pallas_call(leaf_kernel, out_shape=[jax.ShapeDtypeStruct((16, 16, 16,...]
    ppermute x20 -> x8, starting transfers between devices: 42.6 us -> 14.8 us  [ring(): lax.ppermute(values, axis, [(i, (i + step) % count) for i in range(count)])]
    all_to_all x1, waiting for transfers between devices: 27.7 us -> 0.01 us  [per_device(): lax.all_to_all(messages, ('gx', 'gy'), split_axis=0, concat_axis=0, tiled...]
    ppermute x20 -> x8, waiting for transfers between devices: 22.3 us -> 7.28 us  [ring(): lax.ppermute(values, axis, [(i, (i + step) % count) for i in range(count)])]
    unnamed x26 -> x46, local copies, waits for them, and re-layouts: 4.28 us -> 11 us
    concatenate x8 -> x2, other arithmetic: 6.03 us -> 1.44 us  [the longest x1 0.73 us: per_device(): jnp.concatenate([west[:, :256], low_y, east[:, :256]], 0)]
  transfers between devices with their start and end apart: 21 -> 9, of which waited for: 19 -> 5; matrix products, arithmetic and copies ran while one was open for 5% -> 5% of each run, Pallas kernels for 0% -> 2%
where the time goes in v1:
time: 169 us
  blocking collectives  56.5 us (33%)
  Pallas kernels  52.1 us (31%)
  starting transfers between devices  25.9 us (15%)
  local copies, waits for them, and re-layouts  19.8 us (12%)
  waiting for transfers between devices  7.28 us (4%)
  other arithmetic  5.91 us (3%)
    all_gather x1, blocking collectives, masks_of(): whole = lax.all_gather(brick_mask, ('gx', 'gy'), axis=0, tiled=False)  56.5 us
    pallas_call x1, Pallas kernels, leaf_levels(): pl.pallas_call(leaf_kernel, out_shape=[jax.ShapeDtypeStruct((16, 16, 16,...  23.5 us
    pallas_call x1, Pallas kernels, scatter_and_lift(): pl.pallas_call(scatter_kernel, grid=(sources // BUCKETS,), in_specs=[pl.B...  22.8 us
    ppermute x8, starting transfers between devices, ring(): lax.ppermute(values, axis, [(i, (i + step) % count) for i in range(count)])  14.8 us
    all_to_all x1, starting transfers between devices, per_device(): lax.all_to_all(messages, ('gx', 'gy'), split_axis=0, concat_axis=0, tiled...  11.1 us
    unnamed x46, local copies, waits for them, and re-layouts  11 us
    ppermute x8, waiting for transfers between devices, ring(): lax.ppermute(values, axis, [(i, (i + step) % count) for i in range(count)])  7.28 us
    pallas_call x1, Pallas kernels, leaf_taps(): pl.pallas_call(leaf_taps_kernel, out_shape=jax.ShapeDtypeStruct((2, 3, 10...  3.46 us
  transfers between devices with their start and end apart: 9, of which 5 were waited for; matrix products, arithmetic and copies ran while one was open for 5% of the time, Pallas kernels for 2%

profile of v1, /device:TPU:0, one launch (start us, length us, event | category | flops | bytes accessed | tf_op | source)
XLA Modules:
  0.0 168.7 jit_solution(337615677547209241)
XLA Ops:
  0.8 1.0 add_convert_fusion.1
  2.4 3.3 %pad_maximum_fusion = bf16[128,72,128]{2,1,0:T(8,128)(2,1)} fusion(bf16[128,8,128]{2,1,0:T(8,128)(2,1)S(1)} %copy.43, bf16[128,64,128]{2,1,0:T(8,128)(2,1)} %bitcast.49), kind=kLoop, calls=%fused_computation | loop fusion | flops 4718592 | bytes 4718592 | tf_op jit(solution)/shard_map/concatenate | solution.py:28
  5.7 11.1 %all-to-all-start = ((bf16[128,72,128]{2,1,0:T(8,128)(2,1)}), bf16[128,72,128]{2,1,0:T(8,128)(2,1)S(1)}, u32[]{:S(2)}, u32[]{:S(2)}) async-start(bf16[128,72,128]{2,1,0:T(8,128)(2,1)} %pad_maximum_fusion), calls=%async_computation | async-start | bytes 4718592 | tf_op jit(solution)/shard_map/all_to_all | solution.py:396
  17.3 56.5 %all-gather = s32[256,2,4]{2,1,0:T(2,128)S(1)} all-gather(s32[2,2,4]{2,1,0:T(2,128)S(1)} %copy-done.21), channel_id=2, replica_groups=mesh['gx'=16,'gy'=8] {'gx','gy'}, dimensions={0}, use_global_device_ids=true | all-gather | bytes 8256 | tf_op jit(solution)/shard_map/all_gather | solution.py:375
  74.4 3.2 %fusion.11 = (bf16[1,3,3,3,128,128]{5,4,3,2,1,0:T(8,128)(2,1)S(1)}, bf16[3,3,3,128,128]{4,3,1,2,0:T(8,128)(2,1)}, bf16[1,3,3,3,128,128]{5,4,3,2,1,0:T(8,128)(2,1)}) fusion(bf16[3,3,3,3,128,128]{5,4,3,2,1,0:T(8,128)(2,1)} %param.15), kind=kLoop, calls=%fused_computation.28 | loop fusion | bytes 5308416 | tf_op jit(solution)/shard_map/slice | solution.py:402
  77.6 22.8 %scatter.1 = (bf16[256,2048]{1,0:T(8,128)(2,1)S(1)}, bf16[64,1024]{1,0:T(8,128)(2,1)S(1)}, bf16[64,1024]{1,0:T(8,128)(2,1)}, bf16[256,256]{1,0:T(8,128)(2,1)S(1)}, bf16[256,256]{1,0:T(8,128)(2,1)S(1)}) custom-call(bf16[128,72,128]{2,1,0:T(8,128)(2,1)S(1)} %all-to-all-done.msg_ref, bf16[256,512]{1,0:T(8,128)(2,1)S(1)} %mul.60.lift_ref), custom_call_target="tpu_custom_call" | custom-call | tf_op jit(solution)/shard_map/scatter/pallas_call | solution.py:87
  100.4 1.0 copy-done.2
  103.8 1.2 copy.35
  105.0 5.4 %collective-permute-start.1 = (bf16[64,1024]{1,0:T(8,128)(2,1)S(1)}, bf16[64,1024]{1,0:T(8,128)(2,1)S(1)}, u32[]{:S(2)}, u32[]{:S(2)}) collective-permute-start(bf16[64,1024]{1,0:T(8,128)(2,1)S(1)} %copy-done.18), channel_id=1, source_target_pairs={{0,120},{8,0},{16,8},{24,16},{32,24},{40,32},{48,40},{56,48},{64,5... | collective-permute-start | bytes 393224 | tf_op jit(solution)/shard_map/ppermute | solution.py:369
  110.4 2.2 %collective-permute-done.west_ref = bf16[64,1024]{1,0:T(8,128)(2,1)S(1)} collective-permute-done((bf16[64,1024]{1,0:T(8,128)(2,1)}, bf16[64,1024]{1,0:T(8,128)(2,1)S(1)}, u32[]{:S(2)}, u32[]{:S(2)}) %collective-permute-start) | collective-permute-done | bytes 131104 | tf_op jit(solution)/shard_map/ppermute | solution.py:369
  116.5 3.5 %leaf_taps.1.taps_ref = bf16[2,3,1024,256]{3,2,1,0:T(8,128)(2,1)} custom-call(bf16[2,3,3,3,64,64]{5,4,3,2,1,0:T(8,128)(2,1)} %convs_ref.1), custom_call_target="tpu_custom_call" | custom-call | tf_op jit(solution)/shard_map/leaf_taps/pallas_call | solution.py:126
  119.9 1.5 collective-permute-done.2.south_ref
  122.1 1.9 %copy-done = bf16[2,3,1024,256]{3,2,1,0:T(8,128)(2,1)S(1)} copy-done((bf16[2,3,1024,256]{3,2,1,0:T(8,128)(2,1)S(1)}, bf16[2,3,1024,256]{3,2,1,0:T(8,128)(2,1)}, u32[]{:S(2)}) %copy-start) | copy-done | bytes 3145752
  124.0 1.2 copy-done.3
  125.2 0.9 copy-done.5
  127.0 0.9 copy-done.9
  128.0 0.9 copy-done.11
  129.8 23.5 %leaf_levels.1 = (bf16[16,16,16,128]{3,2,1,0:T(8,128)(2,1)}, bf16[128,128]{1,0:T(8,128)(2,1)S(1)}) custom-call(bf16[256,2048]{1,0:T(8,128)(2,1)S(1)} %copy-done.3, bf16[64,1024]{1,0:T(8,128)(2,1)S(1)} %copy-done.5, bf16[64,1024]{1,0:T(8,128)(2,1)S(1)} %copy-done.7, bf16[384,256]{1,0:T(8,128)(2,1)S(1)} %copy-done.11, bf16[384,256]{1,0:T(8,128)(2,1)S(1)} %copy-done.9, ...), custom_call_target="tpu_custom_call" | custom-call | tf_op jit(solution)/shard_map/leaf_levels/pallas_call | solution.py:270
  153.3 5.8 %collective-permute-start.5 = (bf16[128,128]{1,0:T(8,128)(2,1)S(1)}, bf16[128,128]{1,0:T(8,128)(2,1)S(1)}, u32[]{:S(2)}, u32[]{:S(2)}) collective-permute-start(bf16[128,128]{1,0:T(8,128)(2,1)S(1)} %get-tuple-element.15), channel_id=1, source_target_pairs={{0,120},{8,0},{16,8},{24,16},{32,24},{40,32},{48,40},{56,48},{64,5... | collective-permute-start | bytes 98312 | tf_op jit(solution)/shard_map/ppermute | solution.py:369
  159.1 1.9 %collective-permute-done.4 = bf16[128,128]{1,0:T(8,128)(2,1)S(1)} collective-permute-done((bf16[128,128]{1,0:T(8,128)(2,1)S(1)}, bf16[128,128]{1,0:T(8,128)(2,1)S(1)}, u32[]{:S(2)}, u32[]{:S(2)}) %collective-permute-start.4) | collective-permute-done | bytes 32800 | tf_op jit(solution)/shard_map/ppermute | solution.py:369
  161.0 2.9 %collective-permute-start.7 = (bf16[3,128,128]{2,1,0:T(8,128)(2,1)S(1)}, bf16[3,128,128]{2,1,0:T(8,128)(2,1)S(1)}, u32[]{:S(2)}, u32[]{:S(2)}) collective-permute-start(bf16[3,128,128]{2,1,0:T(8,128)(2,1)S(1)} %pad_maximum_fusion.3.middle_ref), channel_id=1, source_target_pairs={{0,7},{1,0},{2,1},{3,2},{4,3},{5,4},{6,5},{7,6},{8,15},{9,8},{10,9... | collective-permute-start | bytes 294920 | tf_op jit(solution)/shard_map/ppermute | solution.py:369
  164.1 1.2 copy.42
  165.3 0.9 collective-permute-done.6.south_ref
  166.3 2.4 %coarse_levels.1 = bf16[2,2,4,128]{3,2,1,0:T(4,128)(2,1)} custom-call(bf16[3,128,128]{2,1,0:T(8,128)(2,1)S(1)} %collective-permute-done.6.south_ref, bf16[3,128,128]{2,1,0:T(8,128)(2,1)S(1)} %pad_maximum_fusion.3.middle_ref, bf16[3,128,128]{2,1,0:T(8,128)(2,1)S(1)} %collective-permute-done.7.north_ref, bf16[3456,128]{1,0:T(8,128)(2,1)S(1)} %bitcast.44, ...), custom_call_target="tpu_custom_call" | custom-call | tf_op jit(solution)/shard_map/coarse_levels/pallas_call | solution.py:358
  (86 shorter events, 10.7 us)
Async XLA Ops:
  5.7 11.2 %copy-start.20 = (bf16[32,64]{1,0:T(8,128)(2,1)S(1)}, bf16[32,64]{1,0:T(8,128)(2,1)}, u32[]{:S(2)}) copy-start(bf16[32,64]{1,0:T(8,128)(2,1)} %param.11) | copy-start | bytes 12292
  5.7 11.6 %copy-start.21 = (s32[2,2,4]{2,1,0:T(2,128)S(1)}, s32[2,2,4]{2,1,0:T(2,128)}, u32[]{:S(2)}) copy-start(s32[2,2,4]{2,1,0:T(2,128)} %param.10) | copy-start | bytes 196
  5.7 71.9 %all-to-all-start = ((bf16[128,72,128]{2,1,0:T(8,128)(2,1)}), bf16[128,72,128]{2,1,0:T(8,128)(2,1)S(1)}, u32[]{:S(2)}, u32[]{:S(2)}) async-start(bf16[128,72,128]{2,1,0:T(8,128)(2,1)} %pad_maximum_fusion), calls=%async_computation | async-start | bytes 4718592 | tf_op jit(solution)/shard_map/all_to_all | solution.py:396
  100.4 1.0 copy-start.2
  103.3 12.1 %copy-start.19 = (bf16[2,2,2,2,128,128]{5,4,3,2,1,0:T(8,128)(2,1)S(1)}, bf16[2,2,2,2,128,128]{5,4,3,2,1,0:T(8,128)(2,1)}, u32[]{:S(2)}) copy-start(bf16[2,2,2,2,128,128]{5,4,3,2,1,0:T(8,128)(2,1)} %param.14) | copy-start | bytes 1572868
  103.3 1.7 %copy-start.18 = (bf16[64,1024]{1,0:T(8,128)(2,1)S(1)}, bf16[64,1024]{1,0:T(8,128)(2,1)}, u32[]{:S(2)}) copy-start(bf16[64,1024]{1,0:T(8,128)(2,1)} %copy-done.17) | copy-start | bytes 393220
  103.3 10.1 %copy-start.16 = (bf16[256,256]{1,0:T(8,128)(2,1)S(1)}, bf16[256,256]{1,0:T(8,128)(2,1)}, u32[]{:S(2)}) copy-start(bf16[256,256]{1,0:T(8,128)(2,1)} %copy-done.15) | copy-start | bytes 393220
  103.3 10.9 %copy-start.14 = (bf16[256,256]{1,0:T(8,128)(2,1)S(1)}, bf16[256,256]{1,0:T(8,128)(2,1)}, u32[]{:S(2)}) copy-start(bf16[256,256]{1,0:T(8,128)(2,1)} %copy-done.13) | copy-start | bytes 393220
  103.3 9.4 %collective-permute-start = (bf16[64,1024]{1,0:T(8,128)(2,1)}, bf16[64,1024]{1,0:T(8,128)(2,1)S(1)}, u32[]{:S(2)}, u32[]{:S(2)}) collective-permute-start(bf16[64,1024]{1,0:T(8,128)(2,1)} %get-tuple-element.10), channel_id=1, source_target_pairs={{0,8},{8,16},{16,24},{24,32},{32,40},{40,48},{48,56},{56,64},{64,7... | collective-permute-start | bytes 393224 | tf_op jit(solution)/shard_map/ppermute | solution.py:369
  105.0 8.4 %collective-permute-start.1 = (bf16[64,1024]{1,0:T(8,128)(2,1)S(1)}, bf16[64,1024]{1,0:T(8,128)(2,1)S(1)}, u32[]{:S(2)}, u32[]{:S(2)}) collective-permute-start(bf16[64,1024]{1,0:T(8,128)(2,1)S(1)} %copy-done.18), channel_id=1, source_target_pairs={{0,120},{8,0},{16,8},{24,16},{32,24},{40,32},{48,40},{56,48},{64,5... | collective-permute-start | bytes 393224 | tf_op jit(solution)/shard_map/ppermute | solution.py:369
  112.7 7.3 %copy-start.4 = (bf16[64,1024]{1,0:T(8,128)(2,1)}, bf16[64,1024]{1,0:T(8,128)(2,1)S(1)}, u32[]{:S(2)}) copy-start(bf16[64,1024]{1,0:T(8,128)(2,1)S(1)} %collective-permute-done.west_ref) | copy-start | bytes 393220
  113.4 6.5 %copy-start.6 = (bf16[64,1024]{1,0:T(8,128)(2,1)}, bf16[64,1024]{1,0:T(8,128)(2,1)S(1)}, u32[]{:S(2)}) copy-start(bf16[64,1024]{1,0:T(8,128)(2,1)S(1)} %collective-permute-done.1.east_ref) | copy-start | bytes 393220
  114.2 5.8 %collective-permute-start.3 = (bf16[384,256]{1,0:T(8,128)(2,1)}, bf16[384,256]{1,0:T(8,128)(2,1)S(1)}, u32[]{:S(2)}, u32[]{:S(2)}) collective-permute-start(bf16[384,256]{1,0:T(8,128)(2,1)} %pad_maximum_fusion.2), channel_id=1, source_target_pairs={{0,7},{1,0},{2,1},{3,2},{4,3},{5,4},{6,5},{7,6},{8,15},{9,8},{10,9... | collective-permute-start | bytes 589832 | tf_op jit(solution)/shard_map/ppermute | solution.py:369
  114.9 6.5 %collective-permute-start.2 = (bf16[384,256]{1,0:T(8,128)(2,1)}, bf16[384,256]{1,0:T(8,128)(2,1)S(1)}, u32[]{:S(2)}, u32[]{:S(2)}) collective-permute-start(bf16[384,256]{1,0:T(8,128)(2,1)} %pad_maximum_fusion.1), channel_id=1, source_target_pairs={{0,1},{1,2},{2,3},{3,4},{4,5},{5,6},{6,7},{7,0},{8,9},{9,10},{10,1... | collective-permute-start | bytes 589832 | tf_op jit(solution)/shard_map/ppermute | solution.py:369
  119.9 1.9 %copy-start.8 = (bf16[384,256]{1,0:T(8,128)(2,1)}, bf16[384,256]{1,0:T(8,128)(2,1)S(1)}, u32[]{:S(2)}) copy-start(bf16[384,256]{1,0:T(8,128)(2,1)S(1)} %collective-permute-done.3.north_ref) | copy-start | bytes 589828
  122.1 1.9 %copy-start = (bf16[2,3,1024,256]{3,2,1,0:T(8,128)(2,1)S(1)}, bf16[2,3,1024,256]{3,2,1,0:T(8,128)(2,1)}, u32[]{:S(2)}) copy-start(bf16[2,3,1024,256]{3,2,1,0:T(8,128)(2,1)} %leaf_taps.1.taps_ref) | copy-start | bytes 9437188
  124.0 1.2 copy-start.3
  127.0 0.9 copy-start.9
  128.0 0.9 copy-start.11
  129.8 36.5 %copy-start.1 = (bf16[1,3,3,3,128,128]{5,4,3,2,1,0:T(8,128)(2,1)S(1)}, bf16[1,3,3,3,128,128]{5,4,3,2,1,0:T(8,128)(2,1)}, u32[]{:S(2)}) copy-start(bf16[1,3,3,3,128,128]{5,4,3,2,1,0:T(8,128)(2,1)} %get-tuple-element.18) | copy-start | bytes 2654212
  153.3 7.7 %collective-permute-start.4 = (bf16[128,128]{1,0:T(8,128)(2,1)S(1)}, bf16[128,128]{1,0:T(8,128)(2,1)S(1)}, u32[]{:S(2)}, u32[]{:S(2)}) collective-permute-start(bf16[128,128]{1,0:T(8,128)(2,1)S(1)} %get-tuple-element.15), channel_id=1, source_target_pairs={{0,8},{8,16},{16,24},{24,32},{32,40},{40,48},{48,56},{56,64},{64,7... | collective-permute-start | bytes 98312 | tf_op jit(solution)/shard_map/ppermute | solution.py:369
  153.3 7.7 %collective-permute-start.5 = (bf16[128,128]{1,0:T(8,128)(2,1)S(1)}, bf16[128,128]{1,0:T(8,128)(2,1)S(1)}, u32[]{:S(2)}, u32[]{:S(2)}) collective-permute-start(bf16[128,128]{1,0:T(8,128)(2,1)S(1)} %get-tuple-element.15), channel_id=1, source_target_pairs={{0,120},{8,0},{16,8},{24,16},{32,24},{40,32},{48,40},{56,48},{64,5... | collective-permute-start | bytes 98312 | tf_op jit(solution)/shard_map/ppermute | solution.py:369
  161.0 5.3 %collective-permute-start.6 = (bf16[3,128,128]{2,1,0:T(8,128)(2,1)S(1)}, bf16[3,128,128]{2,1,0:T(8,128)(2,1)S(1)}, u32[]{:S(2)}, u32[]{:S(2)}) collective-permute-start(bf16[3,128,128]{2,1,0:T(8,128)(2,1)S(1)} %pad_maximum_fusion.3.middle_ref), channel_id=1, source_target_pairs={{0,1},{1,2},{2,3},{3,4},{4,5},{5,6},{6,7},{7,0},{8,9},{9,10},{10,1... | collective-permute-start | bytes 294920 | tf_op jit(solution)/shard_map/ppermute | solution.py:369
  161.0 5.2 %collective-permute-start.7 = (bf16[3,128,128]{2,1,0:T(8,128)(2,1)S(1)}, bf16[3,128,128]{2,1,0:T(8,128)(2,1)S(1)}, u32[]{:S(2)}, u32[]{:S(2)}) collective-permute-start(bf16[3,128,128]{2,1,0:T(8,128)(2,1)S(1)} %pad_maximum_fusion.3.middle_ref), channel_id=1, source_target_pairs={{0,7},{1,0},{2,1},{3,2},{4,3},{5,4},{6,5},{7,6},{8,15},{9,8},{10,9... | collective-permute-start | bytes 294920 | tf_op jit(solution)/shard_map/ppermute | solution.py:369
  (7 other events, 5.3 us)

commit v2 on v1

--- a/solution.py
+++ b/solution.py
@@ -11,21 +11,76 @@
 BUCKETS = 8
 
 
-def pack_messages(records, slot_voxels):
-    fours = slot_voxels.shape[-1] // 4
-    high = (slot_voxels >> 9) * 16 + ((slot_voxels & 31) >> 1)
-    low = ((slot_voxels >> 5) & 15) * 2 + (slot_voxels & 1)
-    parity = lax.axis_index("gy") % 2
-    source = lax.broadcasted_iota(jnp.int32, (4 * fours, 4, 2, fours), 0)
-    quarter = lax.broadcasted_iota(jnp.int32, (4 * fours, 4, 2, fours), 1)
-    side = lax.broadcasted_iota(jnp.int32, (4 * fours, 4, 2, fours), 2)
-    row = lax.broadcasted_iota(jnp.int32, (4 * fours, 4, 2, fours), 3)
-    picks = ((source == 4 * row + quarter) & (side == parity)).astype(jnp.bfloat16)
-    picks = picks.reshape(4 * fours, 4 * 2 * fours)
-    both = jnp.stack([high, low]).astype(jnp.bfloat16)
-    ids = jnp.einsum("tds,sk->dtk", both, picks, preferred_element_type=jnp.float32)
-    ids = ids.astype(jnp.bfloat16).reshape(slot_voxels.shape[0], 8, 2 * fours)
-    return jnp.concatenate([records, ids], 1)
+def pack_kernel(records_ref, slots_ref, bricks_ref, messages_ref, ids_ref, records_sem, ids_sem):
+    buckets = slots_ref.shape[0]
+    chunk = buckets // 8
+    copies = []
+    for part in range(8):
+        copies.append(
+            pltpu.make_async_copy(
+                records_ref.at[part * chunk : part * chunk + chunk],
+                messages_ref.at[part * chunk : part * chunk + chunk, 0:64],
+                records_sem.at[part],
+            )
+        )
+    for copy in copies:
+        copy.start()
+    side = lax.rem(lax.axis_index("gy"), 2)
+    slot = lax.broadcasted_iota(jnp.int32, (256, 128), 0)
+    lane = lax.broadcasted_iota(jnp.int32, (256, 128), 1)
+    picks = jnp.where((slot >> 2) + side * 64 == lane, 1.0, 0.0).astype(jnp.bfloat16)
+    level = lax.broadcasted_iota(jnp.int32, (8, 128), 0) // 2
+    place = lax.broadcasted_iota(jnp.int32, (8, 128), 1) - (1 - side) * 64
+    bricks = jnp.zeros((8, 128), jnp.int32)
+    for column in range(4):
+        for z in range(4):
+            here = (level == z) & (place >= column * 16) & (place < column * 16 + 16)
+            bricks = jnp.where(here, bricks_ref[column // 2, column % 2, z], bricks)
+    bricks = jnp.broadcast_to(bricks.astype(jnp.float32)[None], (chunk, 8, 128))
+    shape = (chunk, 8, 256)
+    row = lax.broadcasted_iota(jnp.int32, shape, 1)
+    mine = (lax.broadcasted_iota(jnp.int32, shape, 2) & 3) == (row & 3)
+
+    @pl.loop(0, 8)
+    def _(part):
+        here = pl.ds(pl.multiple_of(part * chunk, chunk), chunk)
+        slots = slots_ref[here]
+        high = (slots >> 9) * 16 + ((slots & 31) >> 1)
+        low = ((slots >> 5) & 15) * 2 + (slots & 1)
+        both = jnp.where(
+            row < 4,
+            jnp.broadcast_to(high.reshape(chunk, 1, 256), shape),
+            jnp.broadcast_to(low.reshape(chunk, 1, 256), shape),
+        )
+        both = jnp.where(mine, both, 0).astype(jnp.float32)
+        both = both.reshape(chunk * 8, 256).astype(jnp.bfloat16)
+        ids = jnp.dot(both, picks, preferred_element_type=jnp.float32)
+        ids_ref[here] = (ids.reshape(chunk, 8, 128) + bricks).astype(jnp.bfloat16)
+
+    copies.append(pltpu.make_async_copy(ids_ref, messages_ref.at[:, 64:72], ids_sem))
+    copies[-1].start()
+    for copy in copies:
+        copy.wait()
+
+
+def pack_messages(records, slot_voxels, brick_mask):
+    buckets, rows, width = records.shape
+    return pl.pallas_call(
+        pack_kernel,
+        in_specs=[
+            pl.BlockSpec(memory_space=pltpu.HBM),
+            pl.BlockSpec(memory_space=pltpu.VMEM),
+            pl.BlockSpec(memory_space=pltpu.SMEM),
+        ],
+        out_specs=pl.BlockSpec(memory_space=pltpu.HBM),
+        out_shape=jax.ShapeDtypeStruct((buckets, rows + 8, width), jnp.bfloat16),
+        scratch_shapes=[
+            pltpu.VMEM((buckets, 8, width), jnp.bfloat16),
+            pltpu.SemaphoreType.DMA((8,)),
+            pltpu.SemaphoreType.DMA,
+        ],
+        name="pack",
+    )(records, slot_voxels, brick_mask)
 
 
 def scatter_kernel(
@@ -40,6 +95,7 @@
     wide = 256
     lanes = lax.broadcasted_iota(jnp.int32, (wide, wide), 0).astype(jnp.bfloat16)
     zero = jnp.zeros((32, wide), jnp.bfloat16)
+    left = lax.broadcasted_iota(jnp.int32, (8, 128), 1) < 64
     for quad in range(BUCKETS // 4):
         turned, ids = [], []
         for pair in range(2):
@@ -47,8 +103,11 @@
             rows = jnp.concatenate([msg_ref[first, 0:64], msg_ref[first + 1, 0:64]], 0)
             turned.append(jnp.transpose(rows))
             ids.append(
-                msg_ref[first, 64:72].astype(jnp.float32)
-                + msg_ref[first + 1, 64:72].astype(jnp.float32)
+                jnp.where(
+                    left,
+                    msg_ref[first, 64:72].astype(jnp.float32),
+                    msg_ref[first + 1, 64:72].astype(jnp.float32),
+                )
             )
         turned = jnp.concatenate(turned, 1)
         ids = jnp.concatenate(ids, 1)
@@ -94,7 +153,7 @@
         out_specs=[pl.BlockSpec(shape, lambda i: (0, 0)) for shape in shapes],
         out_shape=[jax.ShapeDtypeStruct(shape, jnp.bfloat16) for shape in shapes],
         scratch_shapes=[pltpu.VMEM((1024, 256), jnp.float32)],
-        compiler_params=pltpu.CompilerParams(vmem_limit_bytes=24 << 20),
+        compiler_params=pltpu.CompilerParams(vmem_limit_bytes=12 << 20),
         name="scatter",
     )(messages, lift_block)
 
@@ -144,6 +203,29 @@
     return jnp.where(lane < 64, after, before).astype(jnp.bfloat16)
 
 
+def spread_bricks(near, flags):
+    side = lax.rem(lax.axis_index("gy"), 2)
+    columns = []
+    for y in range(4):
+        for x in range(4):
+            source_x, source_y = (0, 1, 1, 2)[x], (0, 1, 1, 2)[y]
+            lane = ((1, 0, 1, 0)[x] * 2 + (1, 0, 1, 0)[y]) * 16
+            tile = near[source_x * 3 + source_y].astype(jnp.float32)
+            upper = side == 0 if source_y == 1 else side == 1
+            value = jnp.where(upper, tile[:, 64 + lane : 65 + lane], tile[:, lane : lane + 1])
+            flag = flags[0][source_x] * flags[1][source_y]
+            columns.append(jnp.broadcast_to(value, (8, 128)) * flag)
+    return columns
+
+
+def doubled(column):
+    level = lax.broadcasted_iota(jnp.int32, (16, 128), 0) // 4
+    tile = jnp.broadcast_to(column[0:1], (16, 128))
+    for z in range(1, 4):
+        tile = jnp.where(level == z, jnp.broadcast_to(column[2 * z : 2 * z + 1], (16, 128)), tile)
+    return tile
+
+
 def leaf_kernel(
     cells_ref,
     west_ref,
@@ -155,23 +237,66 @@
     down_leaf_ref,
     coarse_ref,
     down_ref,
-    leaf_mask_ref,
-    mid_mask_ref,
+    arrived_ref,
     features_ref,
     down_two_ref,
+    bricks_ref,
     cell_ref,
     cell_z_ref,
     one_ref,
     one_z_ref,
     down_one_ref,
     parts_ref,
+    down_leaf_vmem,
+    coarse_vmem,
+    down_vmem,
+    leaf_mask_ref,
+    near_vmem,
+    near_sem,
+    leaf_sem,
+    coarse_sem,
+    down_sem,
 ):
     here_x = lax.axis_index("gx")
     here_y = lax.axis_index("gy")
+    last_x, last_y = lax.axis_size("gx") - 1, lax.axis_size("gy") - 1
+    near_copies = []
+    for x in range(3):
+        for y in range(3):
+            source = jnp.clip(here_x + x - 1, 0, last_x) * (last_y + 1)
+            source = source + jnp.clip(here_y + y - 1, 0, last_y)
+            near_copies.append(
+                pltpu.make_async_copy(
+                    arrived_ref.at[source, 64:72], near_vmem.at[x * 3 + y], near_sem.at[x, y]
+                )
+            )
+    for copy in near_copies:
+        copy.start()
+    copies = [pltpu.make_async_copy(down_leaf_ref, down_leaf_vmem, leaf_sem)]
+    for dx in range(3):
+        for dz in range(3):
+            copies.append(
+                pltpu.make_async_copy(
+                    coarse_ref.at[0, dx, :, dz], coarse_vmem.at[dx, dz], coarse_sem.at[dx, dz]
+                )
+            )
+    for a in range(2):
+        for b in range(2):
+            for c in range(2):
+                copies.append(
+                    pltpu.make_async_copy(
+                        down_ref.at[0, a, b, c],
+                        down_vmem.at[a, b, :, c * 128 : c * 128 + 128],
+                        down_sem.at[a, b, c],
+                    )
+                )
+    for copy in copies:
+        copy.start()
+
     from_west = jnp.where(here_x > 0, 1.0, 0.0)
-    from_east = jnp.where(here_x < lax.axis_size("gx") - 1, 1.0, 0.0)
+    from_east = jnp.where(here_x < last_x, 1.0, 0.0)
     from_south = jnp.where(here_y > 0, 1.0, 0.0)
-    from_north = jnp.where(here_y < lax.axis_size("gy") - 1, 1.0, 0.0)
+    from_north = jnp.where(here_y < last_y, 1.0, 0.0)
     lift = lift_ref[...]
 
     def place(row, lane, values):
@@ -189,6 +314,17 @@
             lifted = jnp.dot(ref[row : row + rows], lift, preferred_element_type=jnp.float32)
             place(row, lane, lifted * (flag * other))
 
+    for copy in near_copies:
+        copy.wait()
+    flags = ((from_west, 1.0, from_east), (from_south, 1.0, from_north))
+    columns = spread_bricks([near_vmem[i] for i in range(9)], flags)
+    for y in range(4):
+        for x in range(4):
+            bricks_ref[y * 4 + x] = columns[y * 4 + x]
+            tile = doubled(columns[y * 4 + x])
+            for place_x in range(*((0, 4), (4, 12), (12, 20), (20, 24))[x]):
+                leaf_mask_ref[y, place_x * 16 : place_x * 16 + 16] = tile
+
     @pl.loop(0, 12)
     def _(step):
         lanes = pl.ds(pl.multiple_of(step * 256, 256), 256)
@@ -213,6 +349,8 @@
         one_ref[:, lanes] = values
         one_z_ref[:, lanes] = z_neighbours(values.astype(jnp.float32))
 
+    copies[0].wait()
+
     @pl.loop(0, 10)
     def _(step):
         total = sweep(1, one_ref, one_z_ref, 320, step)
@@ -229,7 +367,7 @@
         merged = jnp.concatenate(
             [pairs[:, 0].reshape(160, 256), pairs[:, 1].reshape(160, 256)], 1
         )
-        total = jnp.dot(merged, down_leaf_ref[...], preferred_element_type=jnp.float32)
+        total = jnp.dot(merged, down_leaf_vmem[...].reshape(512, 128), preferred_element_type=jnp.float32)
         mask = mask.reshape(10, 2, 16, 128)[:, 0].reshape(160, 128)
         down = (jnp.maximum(total, 0.0) * mask).astype(jnp.bfloat16)
         before, after = row_shifts(down.astype(jnp.float32), 16)
@@ -238,6 +376,8 @@
         down_one_ref[1, :, lanes] = down
         down_one_ref[2, :, lanes] = after.astype(jnp.bfloat16)
 
+    for copy in copies[1:]:
+        copy.wait()
     windows = []
     for y in range(8):
         windows.append(
@@ -250,7 +390,8 @@
                 1,
             )
         )
-    total = jnp.dot(jnp.concatenate(windows, 0), coarse_ref[...], preferred_element_type=jnp.float32)
+    taps = coarse_vmem[...].reshape(3456, 128)
+    total = jnp.dot(jnp.concatenate(windows, 0), taps, preferred_element_type=jnp.float32)
     total = jnp.maximum(total, 0.0).reshape(8, 128, 128)
     masks = [leaf_mask_ref[1 + y // 4, 64:320].reshape(8, 2, 16, 128)[:, 0] for y in range(8)]
     level = total * jnp.concatenate(masks, 0).reshape(8, 128, 128)
@@ -258,21 +399,26 @@
     merged = jnp.concatenate(
         [level[:, b, :, a].reshape(256, 128) for a in range(2) for b in range(2)], 1
     )
-    parts = jnp.dot(merged, down_ref[...], preferred_element_type=jnp.float32)
+    taps = down_vmem[...].reshape(512, 256)
+    parts = jnp.dot(merged, taps, preferred_element_type=jnp.float32)
     parts_ref[0] = parts[:, :128]
     parts_ref[1] = parts[:, 128:]
     total = parts_ref[0, pl.ds(0, 128, stride=2)] + parts_ref[1, pl.ds(1, 128, stride=2)]
-    mask = mid_mask_ref[2:6, 2:6].reshape(128, 128)
+    tiles = [bricks_ref[(1 + y // 2) * 4 + 1 + x // 2] for y in range(4) for x in range(4)]
+    mask = jnp.concatenate(tiles, 0)
     down_two_ref[...] = (jnp.maximum(total, 0.0) * mask).astype(jnp.bfloat16)
 
 
-def leaf_levels(cells, halos, lift_block, taps, down_leaf, coarse, down, leaf_mask, mid_mask):
+def leaf_levels(cells, halos, lift_block, taps, down_leaf, coarse, down, arrived):
     return pl.pallas_call(
         leaf_kernel,
         out_shape=[
             jax.ShapeDtypeStruct((16, 16, 16, 128), jnp.bfloat16),
             jax.ShapeDtypeStruct((128, 128), jnp.bfloat16),
+            jax.ShapeDtypeStruct((16, 8, 128), jnp.float32),
         ],
+        in_specs=[pl.BlockSpec(memory_space=pltpu.VMEM)] * 7
+        + [pl.BlockSpec(memory_space=pltpu.HBM)] * 4,
         scratch_shapes=[
             pltpu.VMEM((384, 3072), jnp.bfloat16),
             pltpu.VMEM((384, 3072), jnp.bfloat16),
@@ -280,10 +426,19 @@
             pltpu.VMEM((352, 2816), jnp.bfloat16),
             pltpu.VMEM((3, 160, 1280), jnp.bfloat16),
             pltpu.VMEM((2, 256, 128), jnp.float32),
+            pltpu.VMEM((2, 2, 2, 64, 128), jnp.bfloat16),
+            pltpu.VMEM((3, 3, 3, 128, 128), jnp.bfloat16),
+            pltpu.VMEM((2, 2, 128, 256), jnp.bfloat16),
+            pltpu.VMEM((4, 384, 128), jnp.float32),
+            pltpu.VMEM((9, 8, 128), jnp.bfloat16),
+            pltpu.SemaphoreType.DMA((3, 3)),
+            pltpu.SemaphoreType.DMA,
+            pltpu.SemaphoreType.DMA((3, 3)),
+            pltpu.SemaphoreType.DMA((2, 2, 2)),
         ],
-        compiler_params=pltpu.CompilerParams(vmem_limit_bytes=40 << 20),
+        compiler_params=pltpu.CompilerParams(vmem_limit_bytes=24 << 20),
         name="leaf_levels",
-    )(cells, *halos, lift_block, taps, down_leaf, coarse, down, leaf_mask, mid_mask)
+    )(cells, *halos, lift_block, taps, down_leaf, coarse, down, arrived)
 
 
 def coarse_kernel(
@@ -292,12 +447,32 @@
     north_ref,
     coarse_ref,
     down_ref,
-    last_ref,
-    mid_mask_ref,
-    top_mask_ref,
+    bricks_ref,
     top_ref,
     parts_ref,
+    coarse_vmem,
+    last_vmem,
+    down_vmem,
+    coarse_sem,
+    last_sem,
+    down_sem,
 ):
+    copies = [
+        pltpu.make_async_copy(coarse_ref.at[1], coarse_vmem, coarse_sem),
+        pltpu.make_async_copy(coarse_ref.at[2], last_vmem, last_sem),
+    ]
+    for a in range(2):
+        for b in range(2):
+            for c in range(2):
+                copies.append(
+                    pltpu.make_async_copy(
+                        down_ref.at[1, a, b, c],
+                        down_vmem.at[a, b, :, c * 128 : c * 128 + 128],
+                        down_sem.at[a, b, c],
+                    )
+                )
+    for copy in copies:
+        copy.start()
     here_x = lax.axis_index("gx")
     here_y = lax.axis_index("gy")
     from_west = jnp.where(here_x > 0, 1.0, 0.0)
@@ -325,17 +500,28 @@
         for dy in range(3)
         for dz in range(3)
     ]
-    total = jnp.dot(jnp.concatenate(pieces, 1), coarse_ref[...], preferred_element_type=jnp.float32)
-    level = jnp.maximum(total, 0.0) * mid_mask_ref[...].reshape(512, 128)
+    for copy in copies:
+        copy.wait()
+    taps = coarse_vmem[...].reshape(3456, 128)
+    total = jnp.dot(jnp.concatenate(pieces, 1), taps, preferred_element_type=jnp.float32)
+    tiles = [bricks_ref[y // 2 * 4 + x // 2] for y in range(8) for x in range(8)]
+    mask = jnp.concatenate(tiles, 0)
+    level = jnp.maximum(total, 0.0) * mask
     level = level.reshape(4, 2, 4, 2, 8, 128)
     merged = jnp.concatenate(
         [level[:, b, :, a].reshape(128, 128) for a in range(2) for b in range(2)], 1
     ).astype(jnp.bfloat16)
-    parts = jnp.dot(merged, down_ref[...], preferred_element_type=jnp.float32)
+    taps = down_vmem[...].reshape(512, 256)
+    parts = jnp.dot(merged, taps, preferred_element_type=jnp.float32)
     parts_ref[0] = parts[:, :128]
     parts_ref[1] = parts[:, 128:]
     total = parts_ref[0, pl.ds(0, 64, stride=2)] + parts_ref[1, pl.ds(1, 64, stride=2)]
-    down = jnp.maximum(total, 0.0) * top_mask_ref[...]
+    picks = lax.broadcasted_iota(jnp.int32, (64, 128), 0) * 2
+    picks = picks == lax.broadcasted_iota(jnp.int32, (64, 128), 1)
+    picks = jnp.where(picks, 1.0, 0.0).astype(jnp.bfloat16)
+    bricks = bricks_ref[...].reshape(128, 128).astype(jnp.bfloat16)
+    mask = jnp.dot(picks, bricks, preferred_element_type=jnp.float32)
+    down = jnp.maximum(total, 0.0) * mask
     down = down.astype(jnp.bfloat16).astype(jnp.float32)
     before, after = row_shifts(down, 4)
     shifted = [before, down, after]
@@ -346,22 +532,34 @@
                 turn = (64 - (dy - 1) * 16 - (dx - 1) * 4) % 64
                 moved = pltpu.roll(shifted[dz], turn, 0) if turn else shifted[dz]
                 pieces.append(moved.astype(jnp.bfloat16))
-    total = jnp.dot(jnp.concatenate(pieces, 1), last_ref[...], preferred_element_type=jnp.float32)
-    top = (jnp.maximum(total, 0.0) * top_mask_ref[...]).astype(jnp.bfloat16)
+    taps = last_vmem[...].reshape(3456, 128)
+    total = jnp.dot(jnp.concatenate(pieces, 1), taps, preferred_element_type=jnp.float32)
+    top = (jnp.maximum(total, 0.0) * mask).astype(jnp.bfloat16)
     for x in range(2):
         for y in range(2):
             row = (y + 1) * 16 + (x + 1) * 4
             top_ref[x, y] = top[row : row + 4]
 
 
-def coarse_levels(south, middle, north, coarse, down, last, mid_mask, top_mask):
+def coarse_levels(south, middle, north, coarse, down, bricks):
     return pl.pallas_call(
         coarse_kernel,
         out_shape=jax.ShapeDtypeStruct((2, 2, 4, 128), jnp.bfloat16),
-        scratch_shapes=[pltpu.VMEM((2, 128, 128), jnp.float32)],
-        compiler_params=pltpu.CompilerParams(vmem_limit_bytes=24 << 20),
+        in_specs=[pl.BlockSpec(memory_space=pltpu.VMEM)] * 3
+        + [pl.BlockSpec(memory_space=pltpu.HBM)] * 2
+        + [pl.BlockSpec(memory_space=pltpu.VMEM)],
+        scratch_shapes=[
+            pltpu.VMEM((2, 128, 128), jnp.float32),
+            pltpu.VMEM((3, 3, 3, 128, 128), jnp.bfloat16),
+            pltpu.VMEM((3, 3, 3, 128, 128), jnp.bfloat16),
+            pltpu.VMEM((2, 2, 128, 256), jnp.bfloat16),
+            pltpu.SemaphoreType.DMA,
+            pltpu.SemaphoreType.DMA,
+            pltpu.SemaphoreType.DMA((2, 2, 2)),
+        ],
+        compiler_params=pltpu.CompilerParams(vmem_limit_bytes=16 << 20),
         name="coarse_levels",
-    )(south, middle, north, coarse, down, last, mid_mask, top_mask)
+    )(south, middle, north, coarse, down, bricks)
 
 
 def ring(values, axis, step):
@@ -369,66 +567,30 @@
     return lax.ppermute(values, axis, [(i, (i + step) % count) for i in range(count)])
 
 
-def masks_of(brick_mask):
-    size_x, size_y, size_z = brick_mask.shape
-    count_x, count_y = lax.axis_size("gx"), lax.axis_size("gy")
-    whole = lax.all_gather(brick_mask, ("gx", "gy"), axis=0, tiled=False)
-    whole = whole.reshape(count_x, count_y, size_x, size_y, size_z).transpose(0, 2, 1, 3, 4)
-    whole = whole.reshape(count_x * size_x, count_y * size_y, size_z).astype(jnp.float32)
-    whole = jnp.pad(whole, ((1, 1), (1, 1), (0, 0)))
-    start = (lax.axis_index("gx") * size_x, lax.axis_index("gy") * size_y, 0)
-    near = lax.dynamic_slice(whole, start, (size_x + 2, size_y + 2, size_z))
-    near = near.transpose(1, 0, 2)
-    leaf = jnp.repeat(jnp.repeat(near, 8, 1)[:, 4:28], 4, 2).reshape(4, 384, 1)
-    middle = jnp.repeat(jnp.repeat(jnp.repeat(near, 2, 0), 2, 1), 2, 2)[..., None]
-    top = near.reshape(64, 1)
-    return (
-        jnp.broadcast_to(leaf, (4, 384, 128)),
-        jnp.broadcast_to(middle, (8, 8, 8, 128)),
-        jnp.broadcast_to(top, (64, 128)),
-    )
-
-
 def per_device(
     records, slot_voxels, brick_mask, lift_weight, leaf_convs, down_leaf, down_coarse, coarse_convs
 ):
-    messages = pack_messages(records[0], slot_voxels[0])
+    messages = pack_messages(records[0], slot_voxels[0], brick_mask)
     arrived = lax.all_to_all(messages, ("gx", "gy"), split_axis=0, concat_axis=0, tiled=True)
-    leaf_mask, mid_mask, top_mask = masks_of(brick_mask)
     lift_block = jnp.kron(jnp.eye(8, dtype=jnp.bfloat16), lift_weight)
     taps = leaf_taps(leaf_convs)
-    coarse_one = coarse_convs[0].transpose(0, 2, 1, 3, 4).reshape(3456, 128)
-    coarse_two = coarse_convs[1].reshape(3456, 128)
-    coarse_three = coarse_convs[2].reshape(3456, 128)
-    downs = down_coarse.transpose(0, 1, 2, 4, 3, 5).reshape(2, 512, 256)
+    arrived, lift_block, taps = lax.optimization_barrier((arrived, lift_block, taps))
+    coarse_convs = pltpu.with_memory_space_constraint(coarse_convs, pltpu.HBM)
+    down_coarse = pltpu.with_memory_space_constraint(down_coarse, pltpu.HBM)
+    arrived = pltpu.with_memory_space_constraint(arrived, pltpu.HBM)
 
     cells, low_x, high_x, low_y, high_y = scatter_and_lift(arrived, lift_block)
     west = ring(high_x, "gx", 1)
     east = ring(low_x, "gx", -1)
     south = ring(jnp.concatenate([west[:, 768:], high_y, east[:, 768:]], 0), "gy", 1)
     north = ring(jnp.concatenate([west[:, :256], low_y, east[:, :256]], 0), "gy", -1)
-    features, down_two = leaf_levels(
-        cells,
-        (west, east, south, north),
-        lift_block,
-        taps,
-        down_leaf.reshape(512, 128),
-        coarse_one,
-        downs[0],
-        leaf_mask,
-        mid_mask,
+    halos = (west, east, south, north)
+    features, down_two, bricks = leaf_levels(
+        cells, halos, lift_block, taps, down_leaf, coarse_convs, down_coarse, arrived
     )
     middle = jnp.stack([ring(down_two, "gx", 1), down_two, ring(down_two, "gx", -1)])
-    top = coarse_levels(
-        ring(middle, "gy", 1),
-        middle,
-        ring(middle, "gy", -1),
-        coarse_two,
-        downs[1],
-        coarse_three,
-        mid_mask,
-        top_mask,
-    )
+    south, north = ring(middle, "gy", 1), ring(middle, "gy", -1)
+    top = coarse_levels(south, middle, north, coarse_convs, down_coarse, bricks)
     return (features, top)
 
 

time: 169 us -> 196 us (1.16)
  Pallas kernels: 52.1 us -> 120 us
  blocking collectives: 56.5 us -> 0 us
  waiting for transfers between devices: 7.28 us -> 47.7 us
  local copies, waits for them, and re-layouts: 19.8 us -> 0.35 us
  other arithmetic: 5.91 us -> 0.16 us
    pallas_call x0 -> x1, Pallas kernels: none -> 65.6 us  [pack_messages(): pl.pallas_call(pack_kernel, in_specs=[pl.BlockSpec(memory_space=pltpu.HBM...]
    all_gather x1 -> x0, blocking collectives: 56.5 us -> none  [masks_of(): whole = lax.all_gather(brick_mask, ('gx', 'gy'), axis=0, tiled=False)]
    all_to_all x1, waiting for transfers between devices: 0.01 us -> 28.9 us  [per_device(): lax.all_to_all(messages, ('gx', 'gy'), split_axis=0, concat_axis=0, tiled...]
    ppermute x8, waiting for transfers between devices: 7.28 us -> 18.7 us  [ring(): lax.ppermute(values, axis, [(i, (i + step) % count) for i in range(count)])]
    unnamed x46 -> x6, local copies, waits for them, and re-layouts: 11 us -> 0.01 us
    slice x5 -> x0, local copies, waits for them, and re-layouts: 5.48 us -> none  [the longest x1 3.23 us: per_device(): coarse_three = coarse_convs[2].reshape(3456, 128)]
    concatenate x1 -> x0, other arithmetic: 3.28 us -> none  [pack_messages(): return jnp.concatenate([records, ids], 1)]
  transfers between devices with their start and end apart: 9 -> 9, of which waited for: 5 -> 7; matrix products, arithmetic and copies ran while one was open for 5% -> 0% of each run, Pallas kernels for 2% -> 2%
where the time goes in v2:
time: 196 us
  Pallas kernels  120 us (61%)
  waiting for transfers between devices  47.7 us (24%)
  starting transfers between devices  26.9 us (14%)
    pallas_call x1, Pallas kernels, pack_messages(): pl.pallas_call(pack_kernel, in_specs=[pl.BlockSpec(memory_space=pltpu.HBM...  65.6 us
    all_to_all x1, waiting for transfers between devices, per_device(): lax.all_to_all(messages, ('gx', 'gy'), split_axis=0, concat_axis=0, tiled...  28.9 us
    pallas_call x1, Pallas kernels, leaf_levels(): pl.pallas_call(leaf_kernel, out_shape=[jax.ShapeDtypeStruct((16, 16, 16,...  23.5 us
    pallas_call x1, Pallas kernels, scatter_and_lift(): pl.pallas_call(scatter_kernel, grid=(sources // BUCKETS,), in_specs=[pl.B...  23 us
    ppermute x8, waiting for transfers between devices, ring(): lax.ppermute(values, axis, [(i, (i + step) % count) for i in range(count)])  18.7 us
    ppermute x8, starting transfers between devices, ring(): lax.ppermute(values, axis, [(i, (i + step) % count) for i in range(count)])  15.3 us
    all_to_all x1, starting transfers between devices, per_device(): lax.all_to_all(messages, ('gx', 'gy'), split_axis=0, concat_axis=0, tiled...  11.6 us
    pallas_call x1, Pallas kernels, coarse_levels(): pl.pallas_call(coarse_kernel, out_shape=jax.ShapeDtypeStruct((2, 2, 4, 12...  4.05 us
  transfers between devices with their start and end apart: 9, of which 7 were waited for; matrix products, arithmetic and copies ran while one was open for 0% of the time, Pallas kernels for 2%

profile of v2, /device:TPU:0, one launch (start us, length us, event | category | flops | bytes accessed | tf_op | source)
XLA Modules:
  0.0 195.5 jit_solution(16128556674006386831)
XLA Ops:
  0.6 65.6 %pack.1 = bf16[128,72,128]{2,1,0:T(8,128)(2,1)} custom-call(bf16[128,64,128]{2,1,0:T(8,128)(2,1)} %bitcast.8, s32[128,256]{1,0:T(8,128)} %bitcast.9, s32[2,2,4]{2,1,0:T(2,128)} %bricks_ref.1), custom_call_target="tpu_custom_call" | custom-call | tf_op jit(solution)/shard_map/pack/pallas_call | solution.py:68
  66.3 0.0 copy-start.2
  66.3 11.6 %all-to-all-start = ((bf16[128,72,128]{2,1,0:T(8,128)(2,1)}), bf16[128,72,128]{2,1,0:T(8,128)(2,1)}, u32[]{:S(2)}, u32[]{:S(2)}) async-start(bf16[128,72,128]{2,1,0:T(8,128)(2,1)} %pack.1), calls=%async_computation | async-start | bytes 4718592 | tf_op jit(solution)/shard_map/all_to_all | solution.py:574
  77.9 0.1 broadcast_multiply_fusion
  78.0 0.3 mul.27.lift_ref
  78.4 3.5 %leaf_taps.1.taps_ref = bf16[2,3,1024,256]{3,2,1,0:T(8,128)(2,1)} custom-call(bf16[2,3,3,3,64,64]{5,4,3,2,1,0:T(8,128)(2,1)} %convs_ref.1), custom_call_target="tpu_custom_call" | custom-call | tf_op jit(solution)/shard_map/leaf_taps/pallas_call | solution.py:185
  81.8 28.9 %all-to-all-done.msg_ref.arrived_ref = bf16[128,72,128]{2,1,0:T(8,128)(2,1)} async-done(((bf16[128,72,128]{2,1,0:T(8,128)(2,1)}), bf16[128,72,128]{2,1,0:T(8,128)(2,1)}, u32[]{:S(2)}, u32[]{:S(2)}) %all-to-all-start) | async-done | bytes 2359328 | tf_op jit(solution)/shard_map/all_to_all | solution.py:574
  110.8 23.0 %scatter.1 = (bf16[256,2048]{1,0:T(8,128)(2,1)S(1)}, bf16[64,1024]{1,0:T(8,128)(2,1)S(1)}, bf16[64,1024]{1,0:T(8,128)(2,1)S(1)}, bf16[256,256]{1,0:T(8,128)(2,1)S(1)}, bf16[256,256]{1,0:T(8,128)(2,1)S(1)}) custom-call(bf16[128,72,128]{2,1,0:T(8,128)(2,1)} %all-to-all-done.msg_ref.arrived_ref, bf16[256,512]{1,0:T(8,128)(2,1)S(1)} %mul.27.lift_ref), custom_call_target="tpu_custom_call" | custom-call | tf_op jit(solution)/shard_map/scatter/pallas_call | solution.py:146
  133.8 0.8 collective-permute-start
  134.6 4.6 %collective-permute-start.1 = (bf16[64,1024]{1,0:T(8,128)(2,1)S(1)}, bf16[64,1024]{1,0:T(8,128)(2,1)S(1)}, u32[]{:S(2)}, u32[]{:S(2)}) collective-permute-start(bf16[64,1024]{1,0:T(8,128)(2,1)S(1)} %get-tuple-element.17), channel_id=1, source_target_pairs={{0,120},{8,0},{16,8},{24,16},{32,24},{40,32},{48,40},{56,48},{64,5... | collective-permute-start | bytes 393224 | tf_op jit(solution)/shard_map/ppermute | solution.py:567
  139.2 2.9 %collective-permute-done.west_ref = bf16[64,1024]{1,0:T(8,128)(2,1)S(1)} collective-permute-done((bf16[64,1024]{1,0:T(8,128)(2,1)S(1)}, bf16[64,1024]{1,0:T(8,128)(2,1)S(1)}, u32[]{:S(2)}, u32[]{:S(2)}) %collective-permute-start) | collective-permute-done | bytes 131104 | tf_op jit(solution)/shard_map/ppermute | solution.py:567
  142.2 0.0 collective-permute-done.1.east_ref
  142.2 0.0 collective-permute-start.2
  142.2 2.9 %collective-permute-start.3 = (bf16[384,256]{1,0:T(8,128)(2,1)S(1)}, bf16[384,256]{1,0:T(8,128)(2,1)S(1)}, u32[]{:S(2)}, u32[]{:S(2)}) collective-permute-start(bf16[384,256]{1,0:T(8,128)(2,1)S(1)} %pad_maximum_fusion.1), channel_id=1, source_target_pairs={{0,7},{1,0},{2,1},{3,2},{4,3},{5,4},{6,5},{7,6},{8,15},{9,8},{10,9... | collective-permute-start | bytes 589832 | tf_op jit(solution)/shard_map/ppermute | solution.py:567
  145.2 3.3 %collective-permute-done.2.south_ref = bf16[384,256]{1,0:T(8,128)(2,1)S(1)} collective-permute-done((bf16[384,256]{1,0:T(8,128)(2,1)S(1)}, bf16[384,256]{1,0:T(8,128)(2,1)S(1)}, u32[]{:S(2)}, u32[]{:S(2)}) %collective-permute-start.2) | collective-permute-done | bytes 196640 | tf_op jit(solution)/shard_map/ppermute | solution.py:567
  148.5 23.5 %leaf_levels.1 = (bf16[16,16,16,128]{3,2,1,0:T(8,128)(2,1)}, bf16[128,128]{1,0:T(8,128)(2,1)S(1)}, f32[16,8,128]{2,1,0:T(8,128)S(1)}) custom-call(bf16[256,2048]{1,0:T(8,128)(2,1)S(1)} %get-tuple-element.15.cells_ref, bf16[64,1024]{1,0:T(8,128)(2,1)S(1)} %collective-permute-done.west_ref, bf16[64,1024]{1,0:T(8,128)(2,1)S(1)} %collective-permute-done.1.east_ref, ...), custom_call_target="tpu_custom_call" | custom-call | tf_op jit(solution)/shard_map/leaf_levels/pallas_call | solution.py:413
  172.0 5.4 %collective-permute-start.5 = (bf16[128,128]{1,0:T(8,128)(2,1)S(1)}, bf16[128,128]{1,0:T(8,128)(2,1)S(1)}, u32[]{:S(2)}, u32[]{:S(2)}) collective-permute-start(bf16[128,128]{1,0:T(8,128)(2,1)S(1)} %get-tuple-element.22), channel_id=1, source_target_pairs={{0,120},{8,0},{16,8},{24,16},{32,24},{40,32},{48,40},{56,48},{64,5... | collective-permute-start | bytes 98312 | tf_op jit(solution)/shard_map/ppermute | solution.py:567
  177.4 0.0 collective-permute-start.4
  177.4 1.6 collective-permute-done.5
  179.0 5.6 %collective-permute-done.4 = bf16[128,128]{1,0:T(8,128)(2,1)S(1)} collective-permute-done((bf16[128,128]{1,0:T(8,128)(2,1)S(1)}, bf16[128,128]{1,0:T(8,128)(2,1)S(1)}, u32[]{:S(2)}, u32[]{:S(2)}) %collective-permute-start.4) | collective-permute-done | bytes 32800 | tf_op jit(solution)/shard_map/ppermute | solution.py:567
  184.7 1.5 collective-permute-start.7
  186.2 2.2 %collective-permute-done.7.north_ref = bf16[3,128,128]{2,1,0:T(8,128)(2,1)S(1)} collective-permute-done((bf16[3,128,128]{2,1,0:T(8,128)(2,1)S(1)}, bf16[3,128,128]{2,1,0:T(8,128)(2,1)S(1)}, u32[]{:S(2)}, u32[]{:S(2)}) %collective-permute-start.7) | collective-permute-done | bytes 98336 | tf_op jit(solution)/shard_map/ppermute | solution.py:567
  188.4 3.0 %collective-permute-done.6.south_ref = bf16[3,128,128]{2,1,0:T(8,128)(2,1)S(1)} collective-permute-done((bf16[3,128,128]{2,1,0:T(8,128)(2,1)S(1)}, bf16[3,128,128]{2,1,0:T(8,128)(2,1)S(1)}, u32[]{:S(2)}, u32[]{:S(2)}) %collective-permute-start.6) | collective-permute-done | bytes 98336 | tf_op jit(solution)/shard_map/ppermute | solution.py:567
  191.5 4.1 %coarse_levels.1 = bf16[2,2,4,128]{3,2,1,0:T(4,128)(2,1)} custom-call(bf16[3,128,128]{2,1,0:T(8,128)(2,1)S(1)} %collective-permute-done.6.south_ref, bf16[3,128,128]{2,1,0:T(8,128)(2,1)S(1)} %pad_maximum_fusion.2.middle_ref, bf16[3,128,128]{2,1,0:T(8,128)(2,1)S(1)} %collective-permute-done.7.north_ref, bf16[3,3,3,3,128,128]{5,4,3,2,1,0:T(8,128)(2,1)} %coarse_ref.3, ...), custom_call_target="tpu_custom_call" | custom-call | tf_op jit(solution)/shard_map/coarse_levels/pallas_call | solution.py:545
  (13 shorter events, 0.1 us)
Async XLA Ops:
  66.3 11.7 %copy-start.2 = (bf16[32,64]{1,0:T(8,128)(2,1)S(1)}, bf16[32,64]{1,0:T(8,128)(2,1)}, u32[]{:S(2)}) copy-start(bf16[32,64]{1,0:T(8,128)(2,1)} %param.11) | copy-start | bytes 12292
  66.3 44.5 %all-to-all-start = ((bf16[128,72,128]{2,1,0:T(8,128)(2,1)}), bf16[128,72,128]{2,1,0:T(8,128)(2,1)}, u32[]{:S(2)}, u32[]{:S(2)}) async-start(bf16[128,72,128]{2,1,0:T(8,128)(2,1)} %pack.1), calls=%async_computation | async-start | bytes 4718592 | tf_op jit(solution)/shard_map/all_to_all | solution.py:574
  81.8 66.7 %copy-start = (bf16[2,3,1024,256]{3,2,1,0:T(8,128)(2,1)S(1)}, bf16[2,3,1024,256]{3,2,1,0:T(8,128)(2,1)}, u32[]{:S(2)}) copy-start(bf16[2,3,1024,256]{3,2,1,0:T(8,128)(2,1)} %leaf_taps.1.taps_ref) | copy-start | bytes 9437188
  81.8 66.7 %copy-start.1 = (bf16[2,2,2,64,128]{4,3,2,1,0:T(8,128)(2,1)S(1)}, bf16[2,2,2,64,128]{4,3,2,1,0:T(8,128)(2,1)}, u32[]{:S(2)}) copy-start(bf16[2,2,2,64,128]{4,3,2,1,0:T(8,128)(2,1)} %down_leaf_ref.1) | copy-start | bytes 393220
  133.8 8.4 %collective-permute-start = (bf16[64,1024]{1,0:T(8,128)(2,1)S(1)}, bf16[64,1024]{1,0:T(8,128)(2,1)S(1)}, u32[]{:S(2)}, u32[]{:S(2)}) collective-permute-start(bf16[64,1024]{1,0:T(8,128)(2,1)S(1)} %get-tuple-element.16), channel_id=1, source_target_pairs={{0,8},{8,16},{16,24},{24,32},{32,40},{40,48},{48,56},{56,64},{64,7... | collective-permute-start | bytes 393224 | tf_op jit(solution)/shard_map/ppermute | solution.py:567
  134.6 7.5 %collective-permute-start.1 = (bf16[64,1024]{1,0:T(8,128)(2,1)S(1)}, bf16[64,1024]{1,0:T(8,128)(2,1)S(1)}, u32[]{:S(2)}, u32[]{:S(2)}) collective-permute-start(bf16[64,1024]{1,0:T(8,128)(2,1)S(1)} %get-tuple-element.17), channel_id=1, source_target_pairs={{0,120},{8,0},{16,8},{24,16},{32,24},{40,32},{48,40},{56,48},{64,5... | collective-permute-start | bytes 393224 | tf_op jit(solution)/shard_map/ppermute | solution.py:567
  142.2 6.3 %collective-permute-start.2 = (bf16[384,256]{1,0:T(8,128)(2,1)S(1)}, bf16[384,256]{1,0:T(8,128)(2,1)S(1)}, u32[]{:S(2)}, u32[]{:S(2)}) collective-permute-start(bf16[384,256]{1,0:T(8,128)(2,1)S(1)} %pad_maximum_fusion), channel_id=1, source_target_pairs={{0,1},{1,2},{2,3},{3,4},{4,5},{5,6},{6,7},{7,0},{8,9},{9,10},{10,1... | collective-permute-start | bytes 589832 | tf_op jit(solution)/shard_map/ppermute | solution.py:567
  142.2 6.3 %collective-permute-start.3 = (bf16[384,256]{1,0:T(8,128)(2,1)S(1)}, bf16[384,256]{1,0:T(8,128)(2,1)S(1)}, u32[]{:S(2)}, u32[]{:S(2)}) collective-permute-start(bf16[384,256]{1,0:T(8,128)(2,1)S(1)} %pad_maximum_fusion.1), channel_id=1, source_target_pairs={{0,7},{1,0},{2,1},{3,2},{4,3},{5,4},{6,5},{7,6},{8,15},{9,8},{10,9... | collective-permute-start | bytes 589832 | tf_op jit(solution)/shard_map/ppermute | solution.py:567
  172.0 7.0 %collective-permute-start.5 = (bf16[128,128]{1,0:T(8,128)(2,1)S(1)}, bf16[128,128]{1,0:T(8,128)(2,1)S(1)}, u32[]{:S(2)}, u32[]{:S(2)}) collective-permute-start(bf16[128,128]{1,0:T(8,128)(2,1)S(1)} %get-tuple-element.22), channel_id=1, source_target_pairs={{0,120},{8,0},{16,8},{24,16},{32,24},{40,32},{48,40},{56,48},{64,5... | collective-permute-start | bytes 98312 | tf_op jit(solution)/shard_map/ppermute | solution.py:567
  177.4 7.2 %collective-permute-start.4 = (bf16[128,128]{1,0:T(8,128)(2,1)S(1)}, bf16[128,128]{1,0:T(8,128)(2,1)S(1)}, u32[]{:S(2)}, u32[]{:S(2)}) collective-permute-start(bf16[128,128]{1,0:T(8,128)(2,1)S(1)} %get-tuple-element.22), channel_id=1, source_target_pairs={{0,8},{8,16},{16,24},{24,32},{32,40},{40,48},{48,56},{56,64},{64,7... | collective-permute-start | bytes 98312 | tf_op jit(solution)/shard_map/ppermute | solution.py:567
  184.7 3.7 %collective-permute-start.7 = (bf16[3,128,128]{2,1,0:T(8,128)(2,1)S(1)}, bf16[3,128,128]{2,1,0:T(8,128)(2,1)S(1)}, u32[]{:S(2)}, u32[]{:S(2)}) collective-permute-start(bf16[3,128,128]{2,1,0:T(8,128)(2,1)S(1)} %pad_maximum_fusion.2.middle_ref), channel_id=1, source_target_pairs={{0,7},{1,0},{2,1},{3,2},{4,3},{5,4},{6,5},{7,6},{8,15},{9,8},{10,9... | collective-permute-start | bytes 294920 | tf_op jit(solution)/shard_map/ppermute | solution.py:567
  186.2 5.3 %collective-permute-start.6 = (bf16[3,128,128]{2,1,0:T(8,128)(2,1)S(1)}, bf16[3,128,128]{2,1,0:T(8,128)(2,1)S(1)}, u32[]{:S(2)}, u32[]{:S(2)}) collective-permute-start(bf16[3,128,128]{2,1,0:T(8,128)(2,1)S(1)} %pad_maximum_fusion.2.middle_ref), channel_id=1, source_target_pairs={{0,1},{1,2},{2,3},{3,4},{4,5},{5,6},{6,7},{7,0},{8,9},{9,10},{10,1... | collective-permute-start | bytes 294920 | tf_op jit(solution)/shard_map/ppermute | solution.py:567

commit v3 on v2

--- a/solution.py
+++ b/solution.py
@@ -8,22 +8,22 @@
 from jax.sharding import PartitionSpec as P
 
 BRICK = 8
-BUCKETS = 8
-
-
-def pack_kernel(records_ref, slots_ref, bricks_ref, messages_ref, ids_ref, records_sem, ids_sem):
+BUCKETS = 32
+
+
+def pack_kernel(records_ref, slots_ref, bricks_ref, messages_ref, buffer_ref, in_sem, out_sem):
     buckets = slots_ref.shape[0]
     chunk = buckets // 8
-    copies = []
+    incoming, outgoing = [], []
     for part in range(8):
-        copies.append(
-            pltpu.make_async_copy(
-                records_ref.at[part * chunk : part * chunk + chunk],
-                messages_ref.at[part * chunk : part * chunk + chunk, 0:64],
-                records_sem.at[part],
-            )
+        here = slice(part * chunk, part * chunk + chunk)
+        incoming.append(
+            pltpu.make_async_copy(records_ref.at[here], buffer_ref.at[here, 0:64], in_sem.at[part])
         )
-    for copy in copies:
+        outgoing.append(
+            pltpu.make_async_copy(buffer_ref.at[here], messages_ref.at[here], out_sem.at[part])
+        )
+    for copy in incoming:
         copy.start()
     side = lax.rem(lax.axis_index("gy"), 2)
     slot = lax.broadcasted_iota(jnp.int32, (256, 128), 0)
@@ -41,9 +41,8 @@
     row = lax.broadcasted_iota(jnp.int32, shape, 1)
     mine = (lax.broadcasted_iota(jnp.int32, shape, 2) & 3) == (row & 3)
 
-    @pl.loop(0, 8)
-    def _(part):
-        here = pl.ds(pl.multiple_of(part * chunk, chunk), chunk)
+    for part in range(8):
+        here = slice(part * chunk, part * chunk + chunk)
         slots = slots_ref[here]
         high = (slots >> 9) * 16 + ((slots & 31) >> 1)
         low = ((slots >> 5) & 15) * 2 + (slots & 1)
@@ -55,11 +54,10 @@
         both = jnp.where(mine, both, 0).astype(jnp.float32)
         both = both.reshape(chunk * 8, 256).astype(jnp.bfloat16)
         ids = jnp.dot(both, picks, preferred_element_type=jnp.float32)
-        ids_ref[here] = (ids.reshape(chunk, 8, 128) + bricks).astype(jnp.bfloat16)
-
-    copies.append(pltpu.make_async_copy(ids_ref, messages_ref.at[:, 64:72], ids_sem))
-    copies[-1].start()
-    for copy in copies:
+        buffer_ref[here, 64:72] = (ids.reshape(chunk, 8, 128) + bricks).astype(jnp.bfloat16)
+        incoming[part].wait()
+        outgoing[part].start()
+    for copy in outgoing:
         copy.wait()
 
 
@@ -75,9 +73,9 @@
         out_specs=pl.BlockSpec(memory_space=pltpu.HBM),
         out_shape=jax.ShapeDtypeStruct((buckets, rows + 8, width), jnp.bfloat16),
         scratch_shapes=[
-            pltpu.VMEM((buckets, 8, width), jnp.bfloat16),
+            pltpu.VMEM((buckets, rows + 8, width), jnp.bfloat16),
             pltpu.SemaphoreType.DMA((8,)),
-            pltpu.SemaphoreType.DMA,
+            pltpu.SemaphoreType.DMA((8,)),
         ],
         name="pack",
     )(records, slot_voxels, brick_mask)
@@ -111,16 +109,24 @@
             )
         turned = jnp.concatenate(turned, 1)
         ids = jnp.concatenate(ids, 1)
-        for quarter in range(4):
-            features = turned[quarter * 32 : quarter * 32 + 32]
-            high = jnp.broadcast_to(ids[quarter : quarter + 1], (wide, wide)).astype(jnp.bfloat16)
-            low = jnp.broadcast_to(ids[quarter + 4 : quarter + 5], (32, wide)).astype(jnp.bfloat16)
-            hot = jnp.where(lanes == high, 1.0, 0.0).astype(jnp.bfloat16)
-            spread = jnp.concatenate(
-                [jnp.where(low == jnp.bfloat16(value), features, zero) for value in range(32)], 0
-            )
+        for base in (0, 2):
+            spreads, hots = [], []
+            for quarter in (base, base + 1):
+                features = turned[quarter * 32 : quarter * 32 + 32]
+                high = jnp.broadcast_to(ids[quarter : quarter + 1], (wide, wide))
+                low = jnp.broadcast_to(ids[quarter + 4 : quarter + 5], (32, wide))
+                high, low = high.astype(jnp.bfloat16), low.astype(jnp.bfloat16)
+                hots.append(jnp.where(lanes == high, 1.0, 0.0).astype(jnp.bfloat16))
+                spreads += [
+                    jnp.concatenate(
+                        [jnp.where(low == jnp.bfloat16(i), features, zero) for i in range(32)], 0
+                    )
+                ]
             total_ref[...] += lax.dot_general(
-                spread, hot, (((1,), (1,)), ((), ())), preferred_element_type=jnp.float32
+                jnp.concatenate(spreads, 1),
+                jnp.concatenate(hots, 1),
+                (((1,), (1,)), ((), ())),
+                preferred_element_type=jnp.float32,
             )
 
     @pl.when(step == pl.num_programs(0) - 1)
@@ -226,23 +232,140 @@
     return tile
 
 
-def leaf_kernel(
+def grid_flags():
+    here_x, here_y = lax.axis_index("gx"), lax.axis_index("gy")
+    last_x, last_y = lax.axis_size("gx") - 1, lax.axis_size("gy") - 1
+    return (
+        (jnp.where(here_x > 0, 1.0, 0.0), 1.0, jnp.where(here_x < last_x, 1.0, 0.0)),
+        (jnp.where(here_y > 0, 1.0, 0.0), 1.0, jnp.where(here_y < last_y, 1.0, 0.0)),
+    )
+
+
+def fill_leaf_mask(columns, leaf_mask_ref):
+    for y in range(4):
+        for x in range(4):
+            tile = doubled(columns[y * 4 + x])
+            for place_x in range(*((0, 4), (4, 12), (12, 20), (20, 24))[x]):
+                leaf_mask_ref[y, place_x * 16 : place_x * 16 + 16] = tile
+
+
+def leaf_sweep(sources, taps, rows):
+    windows = []
+    for source_ref, source_z_ref, lane in sources:
+        pieces = []
+        for dx in range(3):
+            pieces.append(source_ref[dx * 16 : dx * 16 + rows, pl.ds(lane, 512)])
+            pieces.append(source_z_ref[dx * 16 : dx * 16 + rows, pl.ds(lane, 512)])
+        windows.append(jnp.concatenate(pieces, 1))
+    total = jnp.dot(jnp.concatenate(windows, 0), taps, preferred_element_type=jnp.float32)
+    total = jnp.maximum(total, 0.0)
+    return [total[i * rows : i * rows + rows] for i in range(len(sources))]
+
+
+def middle_kernel(
     cells_ref,
     west_ref,
     east_ref,
+    lift_ref,
+    taps_ref,
+    arrived_ref,
+    one_ref,
+    one_z_ref,
+    low_ref,
+    high_ref,
+    bricks_ref,
+    cell_ref,
+    cell_z_ref,
+    leaf_mask_ref,
+    near_vmem,
+    near_sem,
+):
+    last_x, last_y = lax.axis_size("gx") - 1, lax.axis_size("gy") - 1
+    copies = []
+    for x in range(3):
+        for y in range(3):
+            source = jnp.clip(lax.axis_index("gx") + x - 1, 0, last_x) * (last_y + 1)
+            source = source + jnp.clip(lax.axis_index("gy") + y - 1, 0, last_y)
+            copies.append(
+                pltpu.make_async_copy(
+                    arrived_ref.at[source, 64:72], near_vmem.at[x * 3 + y], near_sem.at[x, y]
+                )
+            )
+    for copy in copies:
+        copy.start()
+    flags = grid_flags()
+    cell_ref[64:320] = cells_ref[...]
+    for part in range(4):
+        for row, ref, flag in ((0, west_ref, flags[0][0]), (320, east_ref, flags[0][2])):
+            sums = ref[:, part * 256 : part * 256 + 256]
+            lifted = jnp.dot(sums, lift_ref[...], preferred_element_type=jnp.float32) * flag
+            cell_ref[row : row + 64, part * 512 : part * 512 + 512] = lifted.astype(jnp.bfloat16)
+    low_ref[...] = cell_ref[:, :256]
+    high_ref[...] = cell_ref[:, 1792:]
+
+    @pl.loop(0, 8)
+    def _(step):
+        lanes = pl.ds(pl.multiple_of(step * 256, 256), 256)
+        cell_z_ref[:, lanes] = z_neighbours(cell_ref[:, lanes].astype(jnp.float32))
+
+    for copy in copies:
+        copy.wait()
+    columns = spread_bricks([near_vmem[i] for i in range(9)], flags)
+    for index, column in enumerate(columns):
+        bricks_ref[index] = column
+    fill_leaf_mask(columns, leaf_mask_ref)
+    taps = taps_ref[0].reshape(3072, 256)
+    for first, count in ((0, 4), (4, 3)):
+        sources = [(cell_ref, cell_z_ref, (first + i) * 256) for i in range(count)]
+        for window, total in enumerate(leaf_sweep(sources, taps, 352)):
+            step = first + window
+            masks = [leaf_mask_ref[(2 * step + half + 9) // 8, 16:368] for half in range(2)]
+            values = (total * jnp.concatenate(masks, 1)).astype(jnp.bfloat16)
+            one_ref[:, step * 256 : step * 256 + 256] = values
+            one_z_ref[:, step * 256 : step * 256 + 256] = z_neighbours(values.astype(jnp.float32))
+
+
+def middle_part(cells, west, east, lift_block, taps, arrived):
+    return pl.pallas_call(
+        middle_kernel,
+        out_shape=[
+            jax.ShapeDtypeStruct((352, 1792), jnp.bfloat16),
+            jax.ShapeDtypeStruct((352, 1792), jnp.bfloat16),
+            jax.ShapeDtypeStruct((384, 256), jnp.bfloat16),
+            jax.ShapeDtypeStruct((384, 256), jnp.bfloat16),
+            jax.ShapeDtypeStruct((16, 8, 128), jnp.float32),
+        ],
+        in_specs=[pl.BlockSpec(memory_space=pltpu.VMEM)] * 5
+        + [pl.BlockSpec(memory_space=pltpu.HBM)],
+        scratch_shapes=[
+            pltpu.VMEM((384, 2048), jnp.bfloat16),
+            pltpu.VMEM((384, 2048), jnp.bfloat16),
+            pltpu.VMEM((4, 384, 128), jnp.float32),
+            pltpu.VMEM((9, 8, 128), jnp.bfloat16),
+            pltpu.SemaphoreType.DMA((3, 3)),
+        ],
+        compiler_params=pltpu.CompilerParams(vmem_limit_bytes=24 << 20),
+        name="leaf_middle",
+    )(cells, west, east, lift_block, taps, arrived)
+
+
+def border_kernel(
+    low_ref,
+    high_ref,
     south_ref,
     north_ref,
     lift_ref,
     taps_ref,
+    bricks_ref,
+    one_middle_ref,
+    one_z_middle_ref,
     down_leaf_ref,
     coarse_ref,
     down_ref,
-    arrived_ref,
     features_ref,
     down_two_ref,
-    bricks_ref,
-    cell_ref,
-    cell_z_ref,
+    edge_ref,
+    edge_z_ref,
     one_ref,
     one_z_ref,
     down_one_ref,
@@ -251,28 +374,17 @@
     coarse_vmem,
     down_vmem,
     leaf_mask_ref,
-    near_vmem,
-    near_sem,
+    one_sem,
     leaf_sem,
     coarse_sem,
     down_sem,
 ):
-    here_x = lax.axis_index("gx")
-    here_y = lax.axis_index("gy")
-    last_x, last_y = lax.axis_size("gx") - 1, lax.axis_size("gy") - 1
-    near_copies = []
-    for x in range(3):
-        for y in range(3):
-            source = jnp.clip(here_x + x - 1, 0, last_x) * (last_y + 1)
-            source = source + jnp.clip(here_y + y - 1, 0, last_y)
-            near_copies.append(
-                pltpu.make_async_copy(
-                    arrived_ref.at[source, 64:72], near_vmem.at[x * 3 + y], near_sem.at[x, y]
-                )
-            )
-    for copy in near_copies:
-        copy.start()
-    copies = [pltpu.make_async_copy(down_leaf_ref, down_leaf_vmem, leaf_sem)]
+    early = [
+        pltpu.make_async_copy(one_middle_ref, one_ref.at[:, 512:2304], one_sem.at[0]),
+        pltpu.make_async_copy(one_z_middle_ref, one_z_ref.at[:, 512:2304], one_sem.at[1]),
+        pltpu.make_async_copy(down_leaf_ref, down_leaf_vmem, leaf_sem),
+    ]
+    copies = []
     for dx in range(3):
         for dz in range(3):
             copies.append(
@@ -290,93 +402,70 @@
                         down_sem.at[a, b, c],
                     )
                 )
-    for copy in copies:
+    for copy in early + copies:
         copy.start()
-
-    from_west = jnp.where(here_x > 0, 1.0, 0.0)
-    from_east = jnp.where(here_x < last_x, 1.0, 0.0)
-    from_south = jnp.where(here_y > 0, 1.0, 0.0)
-    from_north = jnp.where(here_y < last_y, 1.0, 0.0)
-    lift = lift_ref[...]
-
-    def place(row, lane, values):
-        rows, lanes = values.shape
-        cell_ref[row : row + rows, lane : lane + lanes] = values.astype(jnp.bfloat16)
-
-    cell_ref[64:320, 512:2560] = cells_ref[...]
-    for part in range(4):
-        for row, ref, flag in ((0, west_ref, from_west), (320, east_ref, from_east)):
-            sums = ref[:, part * 256 : part * 256 + 256]
-            lifted = jnp.dot(sums, lift, preferred_element_type=jnp.float32)
-            place(row, 512 + part * 512, lifted * flag)
-    for lane, ref, flag in ((0, south_ref, from_south), (2560, north_ref, from_north)):
-        for row, rows, other in ((0, 64, from_west), (64, 256, 1.0), (320, 64, from_east)):
-            lifted = jnp.dot(ref[row : row + rows], lift, preferred_element_type=jnp.float32)
-            place(row, lane, lifted * (flag * other))
-
-    for copy in near_copies:
-        copy.wait()
-    flags = ((from_west, 1.0, from_east), (from_south, 1.0, from_north))
-    columns = spread_bricks([near_vmem[i] for i in range(9)], flags)
-    for y in range(4):
-        for x in range(4):
-            bricks_ref[y * 4 + x] = columns[y * 4 + x]
-            tile = doubled(columns[y * 4 + x])
-            for place_x in range(*((0, 4), (4, 12), (12, 20), (20, 24))[x]):
-                leaf_mask_ref[y, place_x * 16 : place_x * 16 + 16] = tile
-
-    @pl.loop(0, 12)
-    def _(step):
-        lanes = pl.ds(pl.multiple_of(step * 256, 256), 256)
-        cell_z_ref[:, lanes] = z_neighbours(cell_ref[:, lanes].astype(jnp.float32))
-
-    def sweep(layer, source_ref, source_z_ref, rows, step):
-        lanes = pl.ds(pl.multiple_of(step * 256, 256), 512)
-        pieces = []
-        for dx in range(3):
-            pieces.append(source_ref[dx * 16 : dx * 16 + rows, lanes])
-            pieces.append(source_z_ref[dx * 16 : dx * 16 + rows, lanes])
-        taps = taps_ref[layer].reshape(3072, 256)
-        total = jnp.dot(jnp.concatenate(pieces, 1), taps, preferred_element_type=jnp.float32)
-        return jnp.maximum(total, 0.0)
-
-    @pl.loop(0, 11)
-    def _(step):
-        total = sweep(0, cell_ref, cell_z_ref, 352, step)
+    flags = grid_flags()
+    edge_ref[0, :, 512:768] = low_ref[...]
+    edge_ref[1, :, 0:256] = high_ref[...]
+    for edge, lane, ref, flag in ((0, 0, south_ref, flags[1][0]), (1, 256, north_ref, flags[1][2])):
+        for row, rows, other in ((0, 64, flags[0][0]), (64, 256, 1.0), (320, 64, flags[0][2])):
+            sums = ref[row : row + rows]
+            lifted = jnp.dot(sums, lift_ref[...], preferred_element_type=jnp.float32)
+            lifted = (lifted * (flag * other)).astype(jnp.bfloat16)
+            edge_ref[edge, row : row + rows, lane : lane + 512] = lifted
+    fill_leaf_mask([bricks_ref[i] for i in range(16)], leaf_mask_ref)
+    for edge in range(2):
+        for part in range(3):
+            lanes = slice(part * 256, part * 256 + 256)
+            edge_z_ref[edge, :, lanes] = z_neighbours(edge_ref[edge, :, lanes].astype(jnp.float32))
+    sources, steps = [], []
+    for edge in range(2):
+        for window in range(2):
+            sources.append((edge_ref.at[edge], edge_z_ref.at[edge], window * 256))
+            steps.append(edge * 9 + window)
+    taps = taps_ref[0].reshape(3072, 256)
+    for step, total in zip(steps, leaf_sweep(sources, taps, 352)):
         masks = [leaf_mask_ref[(2 * step + half + 5) // 8, 16:368] for half in range(2)]
         values = (total * jnp.concatenate(masks, 1)).astype(jnp.bfloat16)
-        lanes = pl.ds(pl.multiple_of(step * 256, 256), 256)
-        one_ref[:, lanes] = values
-        one_z_ref[:, lanes] = z_neighbours(values.astype(jnp.float32))
-
-    copies[0].wait()
-
-    @pl.loop(0, 10)
-    def _(step):
-        total = sweep(1, one_ref, one_z_ref, 320, step)
-        mask = leaf_mask_ref[(2 * step + 6) // 8, 32:352]
-        values = (total * jnp.concatenate([mask, mask], 1)).astype(jnp.bfloat16)
-
-        @pl.when((step >= 1) & (step < 9))
-        def _():
-            for half in range(2):
-                inner = values[32:288, half * 128 : half * 128 + 128]
-                features_ref[:, 2 * step - 2 + half] = inner.reshape(16, 16, 128)
-
-        pairs = values.reshape(10, 2, 16, 256)
-        merged = jnp.concatenate(
-            [pairs[:, 0].reshape(160, 256), pairs[:, 1].reshape(160, 256)], 1
-        )
-        total = jnp.dot(merged, down_leaf_vmem[...].reshape(512, 128), preferred_element_type=jnp.float32)
-        mask = mask.reshape(10, 2, 16, 128)[:, 0].reshape(160, 128)
-        down = (jnp.maximum(total, 0.0) * mask).astype(jnp.bfloat16)
-        before, after = row_shifts(down.astype(jnp.float32), 16)
-        lanes = pl.ds(pl.multiple_of(step * 128, 128), 128)
-        down_one_ref[0, :, lanes] = before.astype(jnp.bfloat16)
-        down_one_ref[1, :, lanes] = down
-        down_one_ref[2, :, lanes] = after.astype(jnp.bfloat16)
-
-    for copy in copies[1:]:
+        one_ref[:, step * 256 : step * 256 + 256] = values
+        one_z_ref[:, step * 256 : step * 256 + 256] = z_neighbours(values.astype(jnp.float32))
+    for copy in early:
+        copy.wait()
+
+    @pl.loop(0, 2)
+    def _(half_step):
+        first = half_step * 5
+        lanes = [pl.multiple_of((first + i) * 256, 256) for i in range(5)]
+        taps = taps_ref[1].reshape(3072, 256)
+        totals = leaf_sweep([(one_ref, one_z_ref, lane) for lane in lanes], taps, 320)
+        merges, masks = [], []
+        for window, total in enumerate(totals):
+            step = first + window
+            mask = leaf_mask_ref[(2 * step + 6) // 8, 32:352]
+            values = (total * jnp.concatenate([mask, mask], 1)).astype(jnp.bfloat16)
+
+            @pl.when((step >= 1) & (step < 9))
+            def _():
+                for half in range(2):
+                    inner = values[32:288, half * 128 : half * 128 + 128]
+                    features_ref[:, 2 * step - 2 + half] = inner.reshape(16, 16, 128)
+
+            pairs = values.reshape(10, 2, 16, 256)
+            halves = [pairs[:, a].reshape(160, 256) for a in range(2)]
+            merges.append(jnp.concatenate(halves, 1))
+            masks.append(mask.reshape(10, 2, 16, 128)[:, 0].reshape(160, 128))
+        taps = down_leaf_vmem[...].reshape(512, 128)
+        total = jnp.dot(jnp.concatenate(merges, 0), taps, preferred_element_type=jnp.float32)
+        total = jnp.maximum(total, 0.0) * jnp.concatenate(masks, 0)
+        for window in range(5):
+            down = total[window * 160 : window * 160 + 160].astype(jnp.bfloat16)
+            before, after = row_shifts(down.astype(jnp.float32), 16)
+            here = pl.ds(pl.multiple_of((first + window) * 128, 128), 128)
+            down_one_ref[0, :, here] = before.astype(jnp.bfloat16)
+            down_one_ref[1, :, here] = down
+            down_one_ref[2, :, here] = after.astype(jnp.bfloat16)
+
+    for copy in copies:
         copy.wait()
     windows = []
     for y in range(8):
@@ -409,19 +498,19 @@
     down_two_ref[...] = (jnp.maximum(total, 0.0) * mask).astype(jnp.bfloat16)
 
 
-def leaf_levels(cells, halos, lift_block, taps, down_leaf, coarse, down, arrived):
+def border_part(low, high, south, north, lift_block, taps, bricks, one, one_z, down_leaf, coarse, down):
     return pl.pallas_call(
-        leaf_kernel,
+        border_kernel,
         out_shape=[
             jax.ShapeDtypeStruct((16, 16, 16, 128), jnp.bfloat16),
             jax.ShapeDtypeStruct((128, 128), jnp.bfloat16),
-            jax.ShapeDtypeStruct((16, 8, 128), jnp.float32),
         ],
         in_specs=[pl.BlockSpec(memory_space=pltpu.VMEM)] * 7
-        + [pl.BlockSpec(memory_space=pltpu.HBM)] * 4,
+        + [pl.BlockSpec(memory_space=pl.ANY)] * 3
+        + [pl.BlockSpec(memory_space=pltpu.HBM)] * 2,
         scratch_shapes=[
-            pltpu.VMEM((384, 3072), jnp.bfloat16),
-            pltpu.VMEM((384, 3072), jnp.bfloat16),
+            pltpu.VMEM((2, 384, 768), jnp.bfloat16),
+            pltpu.VMEM((2, 384, 768), jnp.bfloat16),
             pltpu.VMEM((352, 2816), jnp.bfloat16),
             pltpu.VMEM((352, 2816), jnp.bfloat16),
             pltpu.VMEM((3, 160, 1280), jnp.bfloat16),
@@ -430,15 +519,14 @@
             pltpu.VMEM((3, 3, 3, 128, 128), jnp.bfloat16),
             pltpu.VMEM((2, 2, 128, 256), jnp.bfloat16),
             pltpu.VMEM((4, 384, 128), jnp.float32),
-            pltpu.VMEM((9, 8, 128), jnp.bfloat16),
-            pltpu.SemaphoreType.DMA((3, 3)),
+            pltpu.SemaphoreType.DMA((2,)),
             pltpu.SemaphoreType.DMA,
             pltpu.SemaphoreType.DMA((3, 3)),
             pltpu.SemaphoreType.DMA((2, 2, 2)),
         ],
-        compiler_params=pltpu.CompilerParams(vmem_limit_bytes=24 << 20),
-        name="leaf_levels",
-    )(cells, *halos, lift_block, taps, down_leaf, coarse, down, arrived)
+        compiler_params=pltpu.CompilerParams(vmem_limit_bytes=32 << 20),
+        name="leaf_border",
+    )(low, high, south, north, lift_block, taps, bricks, one, one_z, down_leaf, coarse, down)
 
 
 def coarse_kernel(
@@ -584,9 +672,20 @@
     east = ring(low_x, "gx", -1)
     south = ring(jnp.concatenate([west[:, 768:], high_y, east[:, 768:]], 0), "gy", 1)
     north = ring(jnp.concatenate([west[:, :256], low_y, east[:, :256]], 0), "gy", -1)
-    halos = (west, east, south, north)
-    features, down_two, bricks = leaf_levels(
-        cells, halos, lift_block, taps, down_leaf, coarse_convs, down_coarse, arrived
+    one, one_z, low, high, bricks = middle_part(cells, west, east, lift_block, taps, arrived)
+    features, down_two = border_part(
+        low,
+        high,
+        south,
+        north,
+        lift_block,
+        taps,
+        bricks,
+        one,
+        one_z,
+        down_leaf,
+        coarse_convs,
+        down_coarse,
     )
     middle = jnp.stack([ring(down_two, "gx", 1), down_two, ring(down_two, "gx", -1)])
     south, north = ring(middle, "gy", 1), ring(middle, "gy", -1)

time: 196 us -> 116 us (0.59)
  Pallas kernels: 120 us -> 51.8 us
  waiting for transfers between devices: 47.7 us -> 34 us
    pallas_call x1, Pallas kernels: 65.6 us -> 3.89 us  [pack_messages(): pl.pallas_call(pack_kernel, in_specs=[pl.BlockSpec(memory_space=pltpu.HBM...]
    ppermute x8, waiting for transfers between devices: 18.7 us -> 7.08 us  [ring(): lax.ppermute(values, axis, [(i, (i + step) % count) for i in range(count)])]
    pallas_call x1 -> x2, Pallas kernels: 23.5 us -> 20.2 us  [the longest x1 13.8 us: border_part(): pl.pallas_call(border_kernel, out_shape=[jax.ShapeDtypeStruct((16, 16, 16...]
    pallas_call x1, Pallas kernels: 23 us -> 20.2 us  [scatter_and_lift(): pl.pallas_call(scatter_kernel, grid=(sources // BUCKETS,), in_specs=[pl.B...]
    all_to_all x1, waiting for transfers between devices: 28.9 us -> 26.9 us  [per_device(): lax.all_to_all(messages, ('gx', 'gy'), split_axis=0, concat_axis=0, tiled...]
  transfers between devices with their start and end apart: 9 -> 9, of which waited for: 7 -> 4; matrix products, arithmetic and copies ran while one was open for 0% -> 2% of each run, Pallas kernels for 2% -> 9%
where the time goes in v3:
time: 116 us; the launch traced here: 115 us
  Pallas kernels  51.8 us (45%)
  waiting for transfers between devices  34 us (29%)
  starting transfers between devices  26 us (22%)
  local copies, waits for them, and re-layouts  1.55 us (1%)
    all_to_all x1, waiting for transfers between devices, per_device(): lax.all_to_all(messages, ('gx', 'gy'), split_axis=0, concat_axis=0, tiled...  26.9 us
    pallas_call x1, Pallas kernels, scatter_and_lift(): pl.pallas_call(scatter_kernel, grid=(sources // BUCKETS,), in_specs=[pl.B...  20.2 us
    ppermute x8, starting transfers between devices, ring(): lax.ppermute(values, axis, [(i, (i + step) % count) for i in range(count)])  14.4 us
    pallas_call x1, Pallas kernels, border_part(): pl.pallas_call(border_kernel, out_shape=[jax.ShapeDtypeStruct((16, 16, 16...  13.8 us
    all_to_all x1, starting transfers between devices, per_device(): lax.all_to_all(messages, ('gx', 'gy'), split_axis=0, concat_axis=0, tiled...  11.6 us
    ppermute x8, waiting for transfers between devices, ring(): lax.ppermute(values, axis, [(i, (i + step) % count) for i in range(count)])  7.08 us
    pallas_call x1, Pallas kernels, middle_part(): pl.pallas_call(middle_kernel, out_shape=[jax.ShapeDtypeStruct((352, 1792)...  6.45 us
    pallas_call x1, Pallas kernels, coarse_levels(): pl.pallas_call(coarse_kernel, out_shape=jax.ShapeDtypeStruct((2, 2, 4, 12...  4.06 us
  transfers between devices with their start and end apart: 9, of which 4 were waited for; matrix products, arithmetic and copies ran while one was open for 2% of the time, Pallas kernels for 9%

profile of v3, /device:TPU:0, one launch (start us, length us, event | category | flops | bytes accessed | tf_op | source)
XLA Modules:
  0.0 115.2 jit_solution(9350256016118254430)
XLA Ops:
  0.6 3.9 %pack.1 = bf16[128,72,128]{2,1,0:T(8,128)(2,1)} custom-call(bf16[128,64,128]{2,1,0:T(8,128)(2,1)} %bitcast.8, s32[128,256]{1,0:T(8,128)} %bitcast.9, s32[2,2,4]{2,1,0:T(2,128)} %bricks_ref.1), custom_call_target="tpu_custom_call" | custom-call | tf_op jit(solution)/shard_map/pack/pallas_call | solution.py:66
  4.5 11.6 %all-to-all-start = ((bf16[128,72,128]{2,1,0:T(8,128)(2,1)}), bf16[128,72,128]{2,1,0:T(8,128)(2,1)}, u32[]{:S(2)}, u32[]{:S(2)}) async-start(bf16[128,72,128]{2,1,0:T(8,128)(2,1)} %pack.1), calls=%async_computation | async-start | bytes 4718592 | tf_op jit(solution)/shard_map/all_to_all | solution.py:662
  16.2 0.0 copy-start.2
  16.2 3.5 %leaf_taps.1.taps_ref = bf16[2,3,1024,256]{3,2,1,0:T(8,128)(2,1)} custom-call(bf16[2,3,3,3,64,64]{5,4,3,2,1,0:T(8,128)(2,1)} %convs_ref.1), custom_call_target="tpu_custom_call" | custom-call | tf_op jit(solution)/shard_map/leaf_taps/pallas_call | solution.py:191
  19.7 0.9 broadcast_multiply_fusion
  20.6 1.5 %mul.27.lift_ref = bf16[256,512]{1,0:T(8,128)(2,1)S(1)} reshape(bf16[8,32,8,64]{3,2,1,0:T(8,128)(2,1)} %broadcast_multiply_fusion) | data formatting | bytes 524288 | tf_op jit(solution)/shard_map/jit(kron)/mul | solution.py:663
  22.1 26.9 %all-to-all-done.msg_ref.arrived_ref = bf16[128,72,128]{2,1,0:T(8,128)(2,1)} async-done(((bf16[128,72,128]{2,1,0:T(8,128)(2,1)}), bf16[128,72,128]{2,1,0:T(8,128)(2,1)}, u32[]{:S(2)}, u32[]{:S(2)}) %all-to-all-start) | async-done | bytes 2359328 | tf_op jit(solution)/shard_map/all_to_all | solution.py:662
  49.0 20.2 %scatter.1 = (bf16[256,2048]{1,0:T(8,128)(2,1)S(1)}, bf16[64,1024]{1,0:T(8,128)(2,1)S(1)}, bf16[64,1024]{1,0:T(8,128)(2,1)S(1)}, bf16[256,256]{1,0:T(8,128)(2,1)S(1)}, bf16[256,256]{1,0:T(8,128)(2,1)S(1)}) custom-call(bf16[128,72,128]{2,1,0:T(8,128)(2,1)} %all-to-all-done.msg_ref.arrived_ref, bf16[256,512]{1,0:T(8,128)(2,1)S(1)} %mul.27.lift_ref), custom_call_target="tpu_custom_call" | custom-call | tf_op jit(solution)/shard_map/scatter/pallas_call | solution.py:152
  69.2 0.8 collective-permute-start
  70.0 4.6 %collective-permute-start.1 = (bf16[64,1024]{1,0:T(8,128)(2,1)S(1)}, bf16[64,1024]{1,0:T(8,128)(2,1)S(1)}, u32[]{:S(2)}, u32[]{:S(2)}) collective-permute-start(bf16[64,1024]{1,0:T(8,128)(2,1)S(1)} %get-tuple-element.21), channel_id=1, source_target_pairs={{0,120},{8,0},{16,8},{24,16},{32,24},{40,32},{48,40},{56,48},{64,5... | collective-permute-start | bytes 393224 | tf_op jit(solution)/shard_map/ppermute | solution.py:655
  74.6 2.9 %collective-permute-done.west_ref = bf16[64,1024]{1,0:T(8,128)(2,1)S(1)} collective-permute-done((bf16[64,1024]{1,0:T(8,128)(2,1)S(1)}, bf16[64,1024]{1,0:T(8,128)(2,1)S(1)}, u32[]{:S(2)}, u32[]{:S(2)}) %collective-permute-start) | collective-permute-done | bytes 131104 | tf_op jit(solution)/shard_map/ppermute | solution.py:655
  77.6 0.0 collective-permute-start.3
  77.7 0.5 collective-permute-start.2
  78.2 6.5 %leaf_middle.1 = (bf16[352,1792]{1,0:T(8,128)(2,1)S(1)}, bf16[352,1792]{1,0:T(8,128)(2,1)S(1)}, bf16[384,256]{1,0:T(8,128)(2,1)S(1)}, bf16[384,256]{1,0:T(8,128)(2,1)S(1)}, f32[16,8,128]{2,1,0:T(8,128)S(1)}) custom-call(bf16[256,2048]{1,0:T(8,128)(2,1)S(1)} %get-tuple-element.19.cells_ref, bf16[64,1024]{1,0:T(8,128)(2,1)S(1)} %collective-permute-done.west_ref, ...), custom_call_target="tpu_custom_call" | custom-call | tf_op jit(solution)/shard_map/leaf_middle/pallas_call | solution.py:329
  84.6 0.0 collective-permute-done.3.north_ref
  84.7 13.8 %leaf_border.1 = (bf16[16,16,16,128]{3,2,1,0:T(8,128)(2,1)}, bf16[128,128]{1,0:T(8,128)(2,1)S(1)}) custom-call(bf16[384,256]{1,0:T(8,128)(2,1)S(1)} %get-tuple-element.23.low_ref, bf16[384,256]{1,0:T(8,128)(2,1)S(1)} %get-tuple-element.24.high_ref, bf16[384,256]{1,0:T(8,128)(2,1)S(1)} %collective-permute-done.2.south_ref, ...), custom_call_target="tpu_custom_call" | custom-call | tf_op jit(solution)/shard_map/leaf_border/pallas_call | solution.py:502
  98.4 0.1 collective-permute-start.4
  98.5 5.4 %collective-permute-start.5 = (bf16[128,128]{1,0:T(8,128)(2,1)S(1)}, bf16[128,128]{1,0:T(8,128)(2,1)S(1)}, u32[]{:S(2)}, u32[]{:S(2)}) collective-permute-start(bf16[128,128]{1,0:T(8,128)(2,1)S(1)} %get-tuple-element.31), channel_id=1, source_target_pairs={{0,120},{8,0},{16,8},{24,16},{32,24},{40,32},{48,40},{56,48},{64,5... | collective-permute-start | bytes 98312 | tf_op jit(solution)/shard_map/ppermute | solution.py:655
  103.9 1.8 %collective-permute-done.4 = bf16[128,128]{1,0:T(8,128)(2,1)S(1)} collective-permute-done((bf16[128,128]{1,0:T(8,128)(2,1)S(1)}, bf16[128,128]{1,0:T(8,128)(2,1)S(1)}, u32[]{:S(2)}, u32[]{:S(2)}) %collective-permute-start.4) | collective-permute-done | bytes 32800 | tf_op jit(solution)/shard_map/ppermute | solution.py:655
  105.7 0.0 collective-permute-start.6
  105.8 2.9 %collective-permute-start.7 = (bf16[3,128,128]{2,1,0:T(8,128)(2,1)S(1)}, bf16[3,128,128]{2,1,0:T(8,128)(2,1)S(1)}, u32[]{:S(2)}, u32[]{:S(2)}) collective-permute-start(bf16[3,128,128]{2,1,0:T(8,128)(2,1)S(1)} %pad_maximum_fusion.2.middle_ref), channel_id=1, source_target_pairs={{0,7},{1,0},{2,1},{3,2},{4,3},{5,4},{6,5},{7,6},{8,15},{9,8},{10,9... | collective-permute-start | bytes 294920 | tf_op jit(solution)/shard_map/ppermute | solution.py:655
  108.7 2.3 %collective-permute-done.6.south_ref = bf16[3,128,128]{2,1,0:T(8,128)(2,1)S(1)} collective-permute-done((bf16[3,128,128]{2,1,0:T(8,128)(2,1)S(1)}, bf16[3,128,128]{2,1,0:T(8,128)(2,1)S(1)}, u32[]{:S(2)}, u32[]{:S(2)}) %collective-permute-start.6) | collective-permute-done | bytes 98336 | tf_op jit(solution)/shard_map/ppermute | solution.py:655
  111.0 0.0 collective-permute-done.7.north_ref
  111.0 4.1 %coarse_levels.1 = bf16[2,2,4,128]{3,2,1,0:T(4,128)(2,1)} custom-call(bf16[3,128,128]{2,1,0:T(8,128)(2,1)S(1)} %collective-permute-done.6.south_ref, bf16[3,128,128]{2,1,0:T(8,128)(2,1)S(1)} %pad_maximum_fusion.2.middle_ref, bf16[3,128,128]{2,1,0:T(8,128)(2,1)S(1)} %collective-permute-done.7.north_ref, bf16[3,3,3,3,128,128]{5,4,3,2,1,0:T(8,128)(2,1)} %coarse_ref.3, ...), custom_call_target="tpu_custom_call" | custom-call | tf_op jit(solution)/shard_map/coarse_levels/pallas_call | solution.py:633
  (14 shorter events, 0.1 us)
Async XLA Ops:
  4.5 44.5 %all-to-all-start = ((bf16[128,72,128]{2,1,0:T(8,128)(2,1)}), bf16[128,72,128]{2,1,0:T(8,128)(2,1)}, u32[]{:S(2)}, u32[]{:S(2)}) async-start(bf16[128,72,128]{2,1,0:T(8,128)(2,1)} %pack.1), calls=%async_computation | async-start | bytes 4718592 | tf_op jit(solution)/shard_map/all_to_all | solution.py:662
  16.2 3.5 %copy-start.2 = (bf16[32,64]{1,0:T(8,128)(2,1)S(1)}, bf16[32,64]{1,0:T(8,128)(2,1)}, u32[]{:S(2)}) copy-start(bf16[32,64]{1,0:T(8,128)(2,1)} %param.11) | copy-start | bytes 12292
  20.6 57.6 %copy-start = (bf16[2,3,1024,256]{3,2,1,0:T(8,128)(2,1)S(1)}, bf16[2,3,1024,256]{3,2,1,0:T(8,128)(2,1)}, u32[]{:S(2)}) copy-start(bf16[2,3,1024,256]{3,2,1,0:T(8,128)(2,1)} %leaf_taps.1.taps_ref) | copy-start | bytes 9437188
  69.2 8.4 %collective-permute-start = (bf16[64,1024]{1,0:T(8,128)(2,1)S(1)}, bf16[64,1024]{1,0:T(8,128)(2,1)S(1)}, u32[]{:S(2)}, u32[]{:S(2)}) collective-permute-start(bf16[64,1024]{1,0:T(8,128)(2,1)S(1)} %get-tuple-element.20), channel_id=1, source_target_pairs={{0,8},{8,16},{16,24},{24,32},{32,40},{40,48},{48,56},{56,64},{64,7... | collective-permute-start | bytes 393224 | tf_op jit(solution)/shard_map/ppermute | solution.py:655
  70.0 7.5 %collective-permute-start.1 = (bf16[64,1024]{1,0:T(8,128)(2,1)S(1)}, bf16[64,1024]{1,0:T(8,128)(2,1)S(1)}, u32[]{:S(2)}, u32[]{:S(2)}) collective-permute-start(bf16[64,1024]{1,0:T(8,128)(2,1)S(1)} %get-tuple-element.21), channel_id=1, source_target_pairs={{0,120},{8,0},{16,8},{24,16},{32,24},{40,32},{48,40},{56,48},{64,5... | collective-permute-start | bytes 393224 | tf_op jit(solution)/shard_map/ppermute | solution.py:655
  77.6 7.0 %collective-permute-start.3 = (bf16[384,256]{1,0:T(8,128)(2,1)S(1)}, bf16[384,256]{1,0:T(8,128)(2,1)S(1)}, u32[]{:S(2)}, u32[]{:S(2)}) collective-permute-start(bf16[384,256]{1,0:T(8,128)(2,1)S(1)} %pad_maximum_fusion.1), channel_id=1, source_target_pairs={{0,7},{1,0},{2,1},{3,2},{4,3},{5,4},{6,5},{7,6},{8,15},{9,8},{10,9... | collective-permute-start | bytes 589832 | tf_op jit(solution)/shard_map/ppermute | solution.py:655
  77.7 7.0 %collective-permute-start.2 = (bf16[384,256]{1,0:T(8,128)(2,1)S(1)}, bf16[384,256]{1,0:T(8,128)(2,1)S(1)}, u32[]{:S(2)}, u32[]{:S(2)}) collective-permute-start(bf16[384,256]{1,0:T(8,128)(2,1)S(1)} %pad_maximum_fusion), channel_id=1, source_target_pairs={{0,1},{1,2},{2,3},{3,4},{4,5},{5,6},{6,7},{7,0},{8,9},{9,10},{10,1... | collective-permute-start | bytes 589832 | tf_op jit(solution)/shard_map/ppermute | solution.py:655
  78.2 6.5 %copy-start.1 = (bf16[2,2,2,64,128]{4,3,2,1,0:T(8,128)(2,1)S(1)}, bf16[2,2,2,64,128]{4,3,2,1,0:T(8,128)(2,1)}, u32[]{:S(2)}) copy-start(bf16[2,2,2,64,128]{4,3,2,1,0:T(8,128)(2,1)} %down_leaf_ref.1) | copy-start | bytes 393220
  98.4 7.3 %collective-permute-start.4 = (bf16[128,128]{1,0:T(8,128)(2,1)S(1)}, bf16[128,128]{1,0:T(8,128)(2,1)S(1)}, u32[]{:S(2)}, u32[]{:S(2)}) collective-permute-start(bf16[128,128]{1,0:T(8,128)(2,1)S(1)} %get-tuple-element.31), channel_id=1, source_target_pairs={{0,8},{8,16},{16,24},{24,32},{32,40},{40,48},{48,56},{56,64},{64,7... | collective-permute-start | bytes 98312 | tf_op jit(solution)/shard_map/ppermute | solution.py:655
  98.5 7.2 %collective-permute-start.5 = (bf16[128,128]{1,0:T(8,128)(2,1)S(1)}, bf16[128,128]{1,0:T(8,128)(2,1)S(1)}, u32[]{:S(2)}, u32[]{:S(2)}) collective-permute-start(bf16[128,128]{1,0:T(8,128)(2,1)S(1)} %get-tuple-element.31), channel_id=1, source_target_pairs={{0,120},{8,0},{16,8},{24,16},{32,24},{40,32},{48,40},{56,48},{64,5... | collective-permute-start | bytes 98312 | tf_op jit(solution)/shard_map/ppermute | solution.py:655
  105.7 5.3 %collective-permute-start.6 = (bf16[3,128,128]{2,1,0:T(8,128)(2,1)S(1)}, bf16[3,128,128]{2,1,0:T(8,128)(2,1)S(1)}, u32[]{:S(2)}, u32[]{:S(2)}) collective-permute-start(bf16[3,128,128]{2,1,0:T(8,128)(2,1)S(1)} %pad_maximum_fusion.2.middle_ref), channel_id=1, source_target_pairs={{0,1},{1,2},{2,3},{3,4},{4,5},{5,6},{6,7},{7,0},{8,9},{9,10},{10,1... | collective-permute-start | bytes 294920 | tf_op jit(solution)/shard_map/ppermute | solution.py:655
  105.8 5.2 %collective-permute-start.7 = (bf16[3,128,128]{2,1,0:T(8,128)(2,1)S(1)}, bf16[3,128,128]{2,1,0:T(8,128)(2,1)S(1)}, u32[]{:S(2)}, u32[]{:S(2)}) collective-permute-start(bf16[3,128,128]{2,1,0:T(8,128)(2,1)S(1)} %pad_maximum_fusion.2.middle_ref), channel_id=1, source_target_pairs={{0,7},{1,0},{2,1},{3,2},{4,3},{5,4},{6,5},{7,6},{8,15},{9,8},{10,9... | collective-permute-start | bytes 294920 | tf_op jit(solution)/shard_map/ppermute | solution.py:655

commit v4 on v3

--- a/solution.py
+++ b/solution.py
@@ -8,7 +8,7 @@
 from jax.sharding import PartitionSpec as P
 
 BRICK = 8
-BUCKETS = 32
+BUCKETS = 64
 
 
 def pack_kernel(records_ref, slots_ref, bricks_ref, messages_ref, buffer_ref, in_sem, out_sem):
@@ -156,10 +156,10 @@
             pl.BlockSpec((BUCKETS, rows, width), lambda i: (i, 0, 0)),
             pl.BlockSpec((256, 512), lambda i: (0, 0)),
         ],
-        out_specs=[pl.BlockSpec(shape, lambda i: (0, 0)) for shape in shapes],
+        out_specs=[pl.BlockSpec(memory_space=pltpu.VMEM)] * 5,
         out_shape=[jax.ShapeDtypeStruct(shape, jnp.bfloat16) for shape in shapes],
         scratch_shapes=[pltpu.VMEM((1024, 256), jnp.float32)],
-        compiler_params=pltpu.CompilerParams(vmem_limit_bytes=12 << 20),
+        compiler_params=pltpu.CompilerParams(vmem_limit_bytes=14 << 20),
         name="scatter",
     )(messages, lift_block)
 
@@ -262,24 +262,7 @@
     return [total[i * rows : i * rows + rows] for i in range(len(sources))]
 
 
-def middle_kernel(
-    cells_ref,
-    west_ref,
-    east_ref,
-    lift_ref,
-    taps_ref,
-    arrived_ref,
-    one_ref,
-    one_z_ref,
-    low_ref,
-    high_ref,
-    bricks_ref,
-    cell_ref,
-    cell_z_ref,
-    leaf_mask_ref,
-    near_vmem,
-    near_sem,
-):
+def own_kernel(cells_ref, arrived_ref, cell_z_ref, bricks_ref, near_vmem, near_sem):
     last_x, last_y = lax.axis_size("gx") - 1, lax.axis_size("gy") - 1
     copies = []
     for x in range(3):
@@ -293,6 +276,52 @@
             )
     for copy in copies:
         copy.start()
+
+    @pl.loop(0, 8)
+    def _(step):
+        lanes = pl.ds(pl.multiple_of(step * 256, 256), 256)
+        cell_z_ref[:, lanes] = z_neighbours(cells_ref[:, lanes].astype(jnp.float32))
+
+    for copy in copies:
+        copy.wait()
+    for index, column in enumerate(spread_bricks([near_vmem[i] for i in range(9)], grid_flags())):
+        bricks_ref[index] = column
+
+
+def own_part(cells, arrived):
+    return pl.pallas_call(
+        own_kernel,
+        out_shape=[
+            jax.ShapeDtypeStruct((256, 2048), jnp.bfloat16),
+            jax.ShapeDtypeStruct((16, 8, 128), jnp.float32),
+        ],
+        in_specs=[pl.BlockSpec(memory_space=pltpu.VMEM), pl.BlockSpec(memory_space=pl.ANY)],
+        out_specs=[pl.BlockSpec(memory_space=pltpu.VMEM)] * 2,
+        scratch_shapes=[
+            pltpu.VMEM((9, 8, 128), jnp.bfloat16),
+            pltpu.SemaphoreType.DMA((3, 3)),
+        ],
+        compiler_params=pltpu.CompilerParams(vmem_limit_bytes=8 << 20),
+        name="leaf_own",
+    )(cells, arrived)
+
+
+def middle_kernel(
+    cells_ref,
+    west_ref,
+    east_ref,
+    lift_ref,
+    taps_ref,
+    own_z_ref,
+    bricks_ref,
+    one_ref,
+    one_z_ref,
+    low_ref,
+    high_ref,
+    cell_ref,
+    cell_z_ref,
+    leaf_mask_ref,
+):
     flags = grid_flags()
     cell_ref[64:320] = cells_ref[...]
     for part in range(4):
@@ -303,17 +332,13 @@
     low_ref[...] = cell_ref[:, :256]
     high_ref[...] = cell_ref[:, 1792:]
 
-    @pl.loop(0, 8)
-    def _(step):
-        lanes = pl.ds(pl.multiple_of(step * 256, 256), 256)
-        cell_z_ref[:, lanes] = z_neighbours(cell_ref[:, lanes].astype(jnp.float32))
-
-    for copy in copies:
-        copy.wait()
-    columns = spread_bricks([near_vmem[i] for i in range(9)], flags)
-    for index, column in enumerate(columns):
-        bricks_ref[index] = column
-    fill_leaf_mask(columns, leaf_mask_ref)
+    cell_z_ref[64:320] = own_z_ref[...]
+    for row in (0, 320):
+        for part in range(4):
+            lanes = slice(part * 512, part * 512 + 512)
+            halo = cell_ref[row : row + 64, lanes].astype(jnp.float32)
+            cell_z_ref[row : row + 64, lanes] = z_neighbours(halo)
+    fill_leaf_mask([bricks_ref[i] for i in range(16)], leaf_mask_ref)
     taps = taps_ref[0].reshape(3072, 256)
     for first, count in ((0, 4), (4, 3)):
         sources = [(cell_ref, cell_z_ref, (first + i) * 256) for i in range(count)]
@@ -325,7 +350,7 @@
             one_z_ref[:, step * 256 : step * 256 + 256] = z_neighbours(values.astype(jnp.float32))
 
 
-def middle_part(cells, west, east, lift_block, taps, arrived):
+def middle_part(cells, west, east, lift_block, taps, own_z, bricks):
     return pl.pallas_call(
         middle_kernel,
         out_shape=[
@@ -333,20 +358,17 @@
             jax.ShapeDtypeStruct((352, 1792), jnp.bfloat16),
             jax.ShapeDtypeStruct((384, 256), jnp.bfloat16),
             jax.ShapeDtypeStruct((384, 256), jnp.bfloat16),
-            jax.ShapeDtypeStruct((16, 8, 128), jnp.float32),
-        ],
-        in_specs=[pl.BlockSpec(memory_space=pltpu.VMEM)] * 5
-        + [pl.BlockSpec(memory_space=pltpu.HBM)],
+        ],
+        in_specs=[pl.BlockSpec(memory_space=pltpu.VMEM)] * 7,
+        out_specs=[pl.BlockSpec(memory_space=pltpu.VMEM)] * 4,
         scratch_shapes=[
             pltpu.VMEM((384, 2048), jnp.bfloat16),
             pltpu.VMEM((384, 2048), jnp.bfloat16),
             pltpu.VMEM((4, 384, 128), jnp.float32),
-            pltpu.VMEM((9, 8, 128), jnp.bfloat16),
-            pltpu.SemaphoreType.DMA((3, 3)),
         ],
         compiler_params=pltpu.CompilerParams(vmem_limit_bytes=24 << 20),
         name="leaf_middle",
-    )(cells, west, east, lift_block, taps, arrived)
+    )(cells, west, east, lift_block, taps, own_z, bricks)
 
 
 def border_kernel(
@@ -538,29 +560,7 @@
     bricks_ref,
     top_ref,
     parts_ref,
-    coarse_vmem,
-    last_vmem,
-    down_vmem,
-    coarse_sem,
-    last_sem,
-    down_sem,
 ):
-    copies = [
-        pltpu.make_async_copy(coarse_ref.at[1], coarse_vmem, coarse_sem),
-        pltpu.make_async_copy(coarse_ref.at[2], last_vmem, last_sem),
-    ]
-    for a in range(2):
-        for b in range(2):
-            for c in range(2):
-                copies.append(
-                    pltpu.make_async_copy(
-                        down_ref.at[1, a, b, c],
-                        down_vmem.at[a, b, :, c * 128 : c * 128 + 128],
-                        down_sem.at[a, b, c],
-                    )
-                )
-    for copy in copies:
-        copy.start()
     here_x = lax.axis_index("gx")
     here_y = lax.axis_index("gy")
     from_west = jnp.where(here_x > 0, 1.0, 0.0)
@@ -571,7 +571,7 @@
     strips = []
     for ref, first, flag in ((south_ref, 1, from_south), (middle_ref, 0, 1.0), (north_ref, 0, from_north)):
         count = 4 if ref is middle_ref else 3
-        tiles = [ref[i].astype(jnp.float32).reshape(4, 4, 8, 128) for i in range(3)]
+        tiles = [ref[i].astype(jnp.float32).reshape(4, 4, 8, 128) for i in (2, 1, 0)]
         tiles = [tile[first : first + count] for tile in tiles]
         tiles = [
             tiles[0][:, 1:] * (flag * from_west),
@@ -588,9 +588,7 @@
         for dy in range(3)
         for dz in range(3)
     ]
-    for copy in copies:
-        copy.wait()
-    taps = coarse_vmem[...].reshape(3456, 128)
+    taps = coarse_ref[1].reshape(3456, 128)
     total = jnp.dot(jnp.concatenate(pieces, 1), taps, preferred_element_type=jnp.float32)
     tiles = [bricks_ref[y // 2 * 4 + x // 2] for y in range(8) for x in range(8)]
     mask = jnp.concatenate(tiles, 0)
@@ -599,7 +597,12 @@
     merged = jnp.concatenate(
         [level[:, b, :, a].reshape(128, 128) for a in range(2) for b in range(2)], 1
     ).astype(jnp.bfloat16)
-    taps = down_vmem[...].reshape(512, 256)
+    taps = [
+        jnp.concatenate([down_ref[1, a, b, c] for c in range(2)], 1)
+        for a in range(2)
+        for b in range(2)
+    ]
+    taps = jnp.concatenate(taps, 0)
     parts = jnp.dot(merged, taps, preferred_element_type=jnp.float32)
     parts_ref[0] = parts[:, :128]
     parts_ref[1] = parts[:, 128:]
@@ -620,7 +623,7 @@
                 turn = (64 - (dy - 1) * 16 - (dx - 1) * 4) % 64
                 moved = pltpu.roll(shifted[dz], turn, 0) if turn else shifted[dz]
                 pieces.append(moved.astype(jnp.bfloat16))
-    taps = last_vmem[...].reshape(3456, 128)
+    taps = coarse_ref[2].reshape(3456, 128)
     total = jnp.dot(jnp.concatenate(pieces, 1), taps, preferred_element_type=jnp.float32)
     top = (jnp.maximum(total, 0.0) * mask).astype(jnp.bfloat16)
     for x in range(2):
@@ -633,18 +636,8 @@
     return pl.pallas_call(
         coarse_kernel,
         out_shape=jax.ShapeDtypeStruct((2, 2, 4, 128), jnp.bfloat16),
-        in_specs=[pl.BlockSpec(memory_space=pltpu.VMEM)] * 3
-        + [pl.BlockSpec(memory_space=pltpu.HBM)] * 2
-        + [pl.BlockSpec(memory_space=pltpu.VMEM)],
-        scratch_shapes=[
-            pltpu.VMEM((2, 128, 128), jnp.float32),
-            pltpu.VMEM((3, 3, 3, 128, 128), jnp.bfloat16),
-            pltpu.VMEM((3, 3, 3, 128, 128), jnp.bfloat16),
-            pltpu.VMEM((2, 2, 128, 256), jnp.bfloat16),
-            pltpu.SemaphoreType.DMA,
-            pltpu.SemaphoreType.DMA,
-            pltpu.SemaphoreType.DMA((2, 2, 2)),
-        ],
+        in_specs=[pl.BlockSpec(memory_space=pltpu.VMEM)] * 6,
+        scratch_shapes=[pltpu.VMEM((2, 128, 128), jnp.float32)],
         compiler_params=pltpu.CompilerParams(vmem_limit_bytes=16 << 20),
         name="coarse_levels",
     )(south, middle, north, coarse, down, bricks)
@@ -663,16 +656,17 @@
     lift_block = jnp.kron(jnp.eye(8, dtype=jnp.bfloat16), lift_weight)
     taps = leaf_taps(leaf_convs)
     arrived, lift_block, taps = lax.optimization_barrier((arrived, lift_block, taps))
-    coarse_convs = pltpu.with_memory_space_constraint(coarse_convs, pltpu.HBM)
-    down_coarse = pltpu.with_memory_space_constraint(down_coarse, pltpu.HBM)
-    arrived = pltpu.with_memory_space_constraint(arrived, pltpu.HBM)
+    coarse_hbm = pltpu.with_memory_space_constraint(coarse_convs, pltpu.HBM)
+    down_hbm = pltpu.with_memory_space_constraint(down_coarse, pltpu.HBM)
 
     cells, low_x, high_x, low_y, high_y = scatter_and_lift(arrived, lift_block)
     west = ring(high_x, "gx", 1)
     east = ring(low_x, "gx", -1)
+    own_z, bricks = own_part(cells, arrived)
+    west, east, own_z = lax.optimization_barrier((west, east, own_z))
     south = ring(jnp.concatenate([west[:, 768:], high_y, east[:, 768:]], 0), "gy", 1)
     north = ring(jnp.concatenate([west[:, :256], low_y, east[:, :256]], 0), "gy", -1)
-    one, one_z, low, high, bricks = middle_part(cells, west, east, lift_block, taps, arrived)
+    one, one_z, low, high = middle_part(cells, west, east, lift_block, taps, own_z, bricks)
     features, down_two = border_part(
         low,
         high,
@@ -684,11 +678,14 @@
         one,
         one_z,
         down_leaf,
-        coarse_convs,
-        down_coarse,
+        coarse_hbm,
+        down_hbm,
     )
-    middle = jnp.stack([ring(down_two, "gx", 1), down_two, ring(down_two, "gx", -1)])
-    south, north = ring(middle, "gy", 1), ring(middle, "gy", -1)
+    west = ring(down_two, "gx", 1)
+    east = ring(down_two, "gx", -1)
+    middle = jnp.stack([east, down_two, west])
+    south = ring(middle, "gy", 1)
+    north = ring(middle, "gy", -1)
     top = coarse_levels(south, middle, north, coarse_convs, down_coarse, bricks)
     return (features, top)
 

time: 116 us -> 114 us (0.983)
  Pallas kernels: 51.8 us -> 48.4 us
  starting transfers between devices: 26 us -> 28 us
  waiting for transfers between devices: 34 us -> 35.4 us
  local copies, waits for them, and re-layouts: 1.55 us -> 0.36 us
    ppermute x8, starting transfers between devices: 14.4 us -> 16.8 us  [ring(): lax.ppermute(values, axis, [(i, (i + step) % count) for i in range(count)])]
    all_to_all x1, waiting for transfers between devices: 26.9 us -> 29.3 us  [per_device(): lax.all_to_all(messages, ('gx', 'gy'), split_axis=0, concat_axis=0, tiled...]
    pallas_call x1, Pallas kernels: 4.06 us -> 2.4 us  [coarse_levels(): pl.pallas_call(coarse_kernel, out_shape=jax.ShapeDtypeStruct((2, 2, 4, 12...]
    pallas_call x1, Pallas kernels: 20.2 us -> 18.6 us  [scatter_and_lift(): pl.pallas_call(scatter_kernel, grid=(sources // BUCKETS,), in_specs=[pl.B...]
    pallas_call x1, Pallas kernels: 6.45 us -> 5.11 us  [middle_part(): pl.pallas_call(middle_kernel, out_shape=[jax.ShapeDtypeStruct((352, 1792)...]
    mul x1, local copies, waits for them, and re-layouts: 1.53 us -> 0.32 us  [per_device(): lift_block = jnp.kron(jnp.eye(8, dtype=jnp.bfloat16), lift_weight)]
  transfers between devices with their start and end apart: 9 -> 9, of which waited for: 4 -> 4; matrix products, arithmetic and copies ran while one was open for 2% -> 0% of each run, Pallas kernels for 9% -> 8%
where the time goes in v4:
time: 114 us; the launch traced here: 113 us
  Pallas kernels  48.4 us (42%)
  waiting for transfers between devices  35.4 us (31%)
  starting transfers between devices  28 us (25%)
    all_to_all x1, waiting for transfers between devices, per_device(): lax.all_to_all(messages, ('gx', 'gy'), split_axis=0, concat_axis=0, tiled...  29.3 us
    pallas_call x1, Pallas kernels, scatter_and_lift(): pl.pallas_call(scatter_kernel, grid=(sources // BUCKETS,), in_specs=[pl.B...  18.6 us
    ppermute x8, starting transfers between devices, ring(): lax.ppermute(values, axis, [(i, (i + step) % count) for i in range(count)])  16.8 us
    pallas_call x1, Pallas kernels, border_part(): pl.pallas_call(border_kernel, out_shape=[jax.ShapeDtypeStruct((16, 16, 16...  14 us
    all_to_all x1, starting transfers between devices, per_device(): lax.all_to_all(messages, ('gx', 'gy'), split_axis=0, concat_axis=0, tiled...  11.1 us
    ppermute x8, waiting for transfers between devices, ring(): lax.ppermute(values, axis, [(i, (i + step) % count) for i in range(count)])  6.14 us
    pallas_call x1, Pallas kernels, middle_part(): pl.pallas_call(middle_kernel, out_shape=[jax.ShapeDtypeStruct((352, 1792)...  5.11 us
    pallas_call x1, Pallas kernels, pack_messages(): pl.pallas_call(pack_kernel, in_specs=[pl.BlockSpec(memory_space=pltpu.HBM...  3.93 us
  transfers between devices with their start and end apart: 9, of which 4 were waited for; matrix products, arithmetic and copies ran while one was open for 0% of the time, Pallas kernels for 8%

profile of v4, /device:TPU:0, one launch (start us, length us, event | category | flops | bytes accessed | tf_op | source)
XLA Modules:
  0.0 113.1 jit_solution(16605018302416605609)
XLA Ops:
  0.6 3.9 %pack.1 = bf16[128,72,128]{2,1,0:T(8,128)(2,1)} custom-call(bf16[128,64,128]{2,1,0:T(8,128)(2,1)} %bitcast.8, s32[128,256]{1,0:T(8,128)} %bitcast.9, s32[2,2,4]{2,1,0:T(2,128)} %bricks_ref.1), custom_call_target="tpu_custom_call" | custom-call | tf_op jit(solution)/shard_map/pack/pallas_call | solution.py:66
  4.6 0.0 copy-start.4
  4.6 11.1 %all-to-all-start = ((bf16[128,72,128]{2,1,0:T(8,128)(2,1)}), bf16[128,72,128]{2,1,0:T(8,128)(2,1)S(1)}, u32[]{:S(2)}, u32[]{:S(2)}) async-start(bf16[128,72,128]{2,1,0:T(8,128)(2,1)} %pack.1), calls=%async_computation | async-start | bytes 4718592 | tf_op jit(solution)/shard_map/all_to_all | solution.py:655
  15.8 0.1 broadcast_multiply_fusion
  15.9 0.3 mul.27.lift_ref
  16.2 3.5 %leaf_taps.1.taps_ref = bf16[2,3,1024,256]{3,2,1,0:T(8,128)(2,1)} custom-call(bf16[2,3,3,3,64,64]{5,4,3,2,1,0:T(8,128)(2,1)} %convs_ref.1), custom_call_target="tpu_custom_call" | custom-call | tf_op jit(solution)/shard_map/leaf_taps/pallas_call | solution.py:191
  19.7 29.3 %all-to-all-done.msg_ref.arrived_ref = bf16[128,72,128]{2,1,0:T(8,128)(2,1)S(1)} async-done(((bf16[128,72,128]{2,1,0:T(8,128)(2,1)}), bf16[128,72,128]{2,1,0:T(8,128)(2,1)S(1)}, u32[]{:S(2)}, u32[]{:S(2)}) %all-to-all-start) | async-done | bytes 2359328 | tf_op jit(solution)/shard_map/all_to_all | solution.py:655
  49.0 18.6 %scatter.1 = (bf16[256,2048]{1,0:T(8,128)(2,1)S(1)}, bf16[64,1024]{1,0:T(8,128)(2,1)S(1)}, bf16[64,1024]{1,0:T(8,128)(2,1)S(1)}, bf16[256,256]{1,0:T(8,128)(2,1)S(1)}, bf16[256,256]{1,0:T(8,128)(2,1)S(1)}) custom-call(bf16[128,72,128]{2,1,0:T(8,128)(2,1)S(1)} %all-to-all-done.msg_ref.arrived_ref, bf16[256,512]{1,0:T(8,128)(2,1)S(1)} %mul.27.lift_ref), custom_call_target="tpu_custom_call" | custom-call | tf_op jit(solution)/shard_map/scatter/pallas_call | solution.py:152
  67.6 0.8 collective-permute-start
  68.4 4.6 %collective-permute-start.1 = (bf16[64,1024]{1,0:T(8,128)(2,1)S(1)}, bf16[64,1024]{1,0:T(8,128)(2,1)S(1)}, u32[]{:S(2)}, u32[]{:S(2)}) collective-permute-start(bf16[64,1024]{1,0:T(8,128)(2,1)S(1)} %get-tuple-element.25), channel_id=1, source_target_pairs={{0,120},{8,0},{16,8},{24,16},{32,24},{40,32},{48,40},{56,48},{64,5... | collective-permute-start | bytes 393224 | tf_op jit(solution)/shard_map/ppermute | solution.py:648
  73.0 0.9 leaf_own.1
  73.9 2.0 %collective-permute-done.west_ref = bf16[64,1024]{1,0:T(8,128)(2,1)S(1)} collective-permute-done((bf16[64,1024]{1,0:T(8,128)(2,1)S(1)}, bf16[64,1024]{1,0:T(8,128)(2,1)S(1)}, u32[]{:S(2)}, u32[]{:S(2)}) %collective-permute-start) | collective-permute-done | bytes 131104 | tf_op jit(solution)/shard_map/ppermute | solution.py:648
  76.0 0.0 collective-permute-start.2
  76.0 2.9 %collective-permute-start.3 = (bf16[384,256]{1,0:T(8,128)(2,1)S(1)}, bf16[384,256]{1,0:T(8,128)(2,1)S(1)}, u32[]{:S(2)}, u32[]{:S(2)}) collective-permute-start(bf16[384,256]{1,0:T(8,128)(2,1)S(1)} %pad_maximum_fusion.1), channel_id=1, source_target_pairs={{0,7},{1,0},{2,1},{3,2},{4,3},{5,4},{6,5},{7,6},{8,15},{9,8},{10,9... | collective-permute-start | bytes 589832 | tf_op jit(solution)/shard_map/ppermute | solution.py:648
  79.0 5.1 %leaf_middle.1 = (bf16[352,1792]{1,0:T(8,128)(2,1)S(1)}, bf16[352,1792]{1,0:T(8,128)(2,1)S(1)}, bf16[384,256]{1,0:T(8,128)(2,1)S(1)}, bf16[384,256]{1,0:T(8,128)(2,1)S(1)}) custom-call(bf16[256,2048]{1,0:T(8,128)(2,1)S(1)} %get-tuple-element.23.cells_ref, bf16[64,1024]{1,0:T(8,128)(2,1)S(1)} %collective-permute-done.west_ref, ...), custom_call_target="tpu_custom_call" | custom-call | tf_op jit(solution)/shard_map/leaf_middle/pallas_call | solution.py:354
  84.1 0.0 copy-start.1
  84.1 14.0 %leaf_border.1 = (bf16[16,16,16,128]{3,2,1,0:T(8,128)(2,1)}, bf16[128,128]{1,0:T(8,128)(2,1)S(1)}) custom-call(bf16[384,256]{1,0:T(8,128)(2,1)S(1)} %get-tuple-element.32.low_ref, bf16[384,256]{1,0:T(8,128)(2,1)S(1)} %get-tuple-element.33.high_ref, bf16[384,256]{1,0:T(8,128)(2,1)S(1)} %collective-permute-done.2.south_ref, ...), custom_call_target="tpu_custom_call" | custom-call | tf_op jit(solution)/shard_map/leaf_border/pallas_call | solution.py:524
  98.1 0.1 collective-permute-start.5
  98.2 5.4 %collective-permute-start.4 = (bf16[128,128]{1,0:T(8,128)(2,1)S(1)}, bf16[128,128]{1,0:T(8,128)(2,1)S(1)}, u32[]{:S(2)}, u32[]{:S(2)}) collective-permute-start(bf16[128,128]{1,0:T(8,128)(2,1)S(1)} %get-tuple-element.39), channel_id=1, source_target_pairs={{0,120},{8,0},{16,8},{24,16},{32,24},{40,32},{48,40},{56,48},{64,5... | collective-permute-start | bytes 98312 | tf_op jit(solution)/shard_map/ppermute | solution.py:648
  103.6 1.8 %collective-permute-done.5 = bf16[128,128]{1,0:T(8,128)(2,1)S(1)} collective-permute-done((bf16[128,128]{1,0:T(8,128)(2,1)S(1)}, bf16[128,128]{1,0:T(8,128)(2,1)S(1)}, u32[]{:S(2)}, u32[]{:S(2)}) %collective-permute-start.5) | collective-permute-done | bytes 32800 | tf_op jit(solution)/shard_map/ppermute | solution.py:648
  105.4 0.0 collective-permute-start.6
  105.5 2.9 %collective-permute-start.7 = (bf16[3,128,128]{2,1,0:T(8,128)(2,1)S(1)}, bf16[3,128,128]{2,1,0:T(8,128)(2,1)S(1)}, u32[]{:S(2)}, u32[]{:S(2)}) collective-permute-start(bf16[3,128,128]{2,1,0:T(8,128)(2,1)S(1)} %pad_maximum_fusion.2.middle_ref), channel_id=1, source_target_pairs={{0,7},{1,0},{2,1},{3,2},{4,3},{5,4},{6,5},{7,6},{8,15},{9,8},{10,9... | collective-permute-start | bytes 294920 | tf_op jit(solution)/shard_map/ppermute | solution.py:648
  108.4 2.3 %collective-permute-done.6.south_ref = bf16[3,128,128]{2,1,0:T(8,128)(2,1)S(1)} collective-permute-done((bf16[3,128,128]{2,1,0:T(8,128)(2,1)S(1)}, bf16[3,128,128]{2,1,0:T(8,128)(2,1)S(1)}, u32[]{:S(2)}, u32[]{:S(2)}) %collective-permute-start.6) | collective-permute-done | bytes 98336 | tf_op jit(solution)/shard_map/ppermute | solution.py:648
  110.7 2.4 %coarse_levels.1 = bf16[2,2,4,128]{3,2,1,0:T(4,128)(2,1)} custom-call(bf16[3,128,128]{2,1,0:T(8,128)(2,1)S(1)} %collective-permute-done.6.south_ref, bf16[3,128,128]{2,1,0:T(8,128)(2,1)S(1)} %pad_maximum_fusion.2.middle_ref, bf16[3,128,128]{2,1,0:T(8,128)(2,1)S(1)} %collective-permute-done.7.north_ref, bf16[3,3,3,3,128,128]{5,4,3,2,1,0:T(8,128)(2,1)S(1)} %copy-done.1, ...), custom_call_target="tpu_custom_call" | custom-call | tf_op jit(solution)/shard_map/coarse_levels/pallas_call | solution.py:636
  (18 shorter events, 0.1 us)
Async XLA Ops:
  4.6 11.2 %copy-start.4 = (bf16[32,64]{1,0:T(8,128)(2,1)S(1)}, bf16[32,64]{1,0:T(8,128)(2,1)}, u32[]{:S(2)}) copy-start(bf16[32,64]{1,0:T(8,128)(2,1)} %param.11) | copy-start | bytes 12292
  4.6 44.4 %all-to-all-start = ((bf16[128,72,128]{2,1,0:T(8,128)(2,1)}), bf16[128,72,128]{2,1,0:T(8,128)(2,1)S(1)}, u32[]{:S(2)}, u32[]{:S(2)}) async-start(bf16[128,72,128]{2,1,0:T(8,128)(2,1)} %pack.1), calls=%async_computation | async-start | bytes 4718592 | tf_op jit(solution)/shard_map/all_to_all | solution.py:655
  67.5 11.4 %copy-start = (bf16[2,3,1024,256]{3,2,1,0:T(8,128)(2,1)S(1)}, bf16[2,3,1024,256]{3,2,1,0:T(8,128)(2,1)}, u32[]{:S(2)}) copy-start(bf16[2,3,1024,256]{3,2,1,0:T(8,128)(2,1)} %leaf_taps.1.taps_ref) | copy-start | bytes 9437188
  67.6 8.4 %collective-permute-start = (bf16[64,1024]{1,0:T(8,128)(2,1)S(1)}, bf16[64,1024]{1,0:T(8,128)(2,1)S(1)}, u32[]{:S(2)}, u32[]{:S(2)}) collective-permute-start(bf16[64,1024]{1,0:T(8,128)(2,1)S(1)} %get-tuple-element.24), channel_id=1, source_target_pairs={{0,8},{8,16},{16,24},{24,32},{32,40},{40,48},{48,56},{56,64},{64,7... | collective-permute-start | bytes 393224 | tf_op jit(solution)/shard_map/ppermute | solution.py:648
  68.4 7.5 %collective-permute-start.1 = (bf16[64,1024]{1,0:T(8,128)(2,1)S(1)}, bf16[64,1024]{1,0:T(8,128)(2,1)S(1)}, u32[]{:S(2)}, u32[]{:S(2)}) collective-permute-start(bf16[64,1024]{1,0:T(8,128)(2,1)S(1)} %get-tuple-element.25), channel_id=1, source_target_pairs={{0,120},{8,0},{16,8},{24,16},{32,24},{40,32},{48,40},{56,48},{64,5... | collective-permute-start | bytes 393224 | tf_op jit(solution)/shard_map/ppermute | solution.py:648
  76.0 8.1 %collective-permute-start.2 = (bf16[384,256]{1,0:T(8,128)(2,1)S(1)}, bf16[384,256]{1,0:T(8,128)(2,1)S(1)}, u32[]{:S(2)}, u32[]{:S(2)}) collective-permute-start(bf16[384,256]{1,0:T(8,128)(2,1)S(1)} %pad_maximum_fusion), channel_id=1, source_target_pairs={{0,1},{1,2},{2,3},{3,4},{4,5},{5,6},{6,7},{7,0},{8,9},{9,10},{10,1... | collective-permute-start | bytes 589832 | tf_op jit(solution)/shard_map/ppermute | solution.py:648
  76.0 8.1 %collective-permute-start.3 = (bf16[384,256]{1,0:T(8,128)(2,1)S(1)}, bf16[384,256]{1,0:T(8,128)(2,1)S(1)}, u32[]{:S(2)}, u32[]{:S(2)}) collective-permute-start(bf16[384,256]{1,0:T(8,128)(2,1)S(1)} %pad_maximum_fusion.1), channel_id=1, source_target_pairs={{0,7},{1,0},{2,1},{3,2},{4,3},{5,4},{6,5},{7,6},{8,15},{9,8},{10,9... | collective-permute-start | bytes 589832 | tf_op jit(solution)/shard_map/ppermute | solution.py:648
  79.0 5.1 %copy-start.3 = (bf16[2,2,2,64,128]{4,3,2,1,0:T(8,128)(2,1)S(1)}, bf16[2,2,2,64,128]{4,3,2,1,0:T(8,128)(2,1)}, u32[]{:S(2)}) copy-start(bf16[2,2,2,64,128]{4,3,2,1,0:T(8,128)(2,1)} %down_leaf_ref.1) | copy-start | bytes 393220
  84.1 26.6 %copy-start.1 = (bf16[3,3,3,3,128,128]{5,4,3,2,1,0:T(8,128)(2,1)S(1)}, bf16[3,3,3,3,128,128]{5,4,3,2,1,0:T(8,128)(2,1)}, u32[]{:S(2)}) copy-start(bf16[3,3,3,3,128,128]{5,4,3,2,1,0:T(8,128)(2,1)} %coarse_ref.3) | copy-start | bytes 7962628
  84.1 26.6 %copy-start.2 = (bf16[2,2,2,2,128,128]{5,4,3,2,1,0:T(8,128)(2,1)S(1)}, bf16[2,2,2,2,128,128]{5,4,3,2,1,0:T(8,128)(2,1)}, u32[]{:S(2)}) copy-start(bf16[2,2,2,2,128,128]{5,4,3,2,1,0:T(8,128)(2,1)} %down_ref.3) | copy-start | bytes 1572868
  98.1 7.3 %collective-permute-start.5 = (bf16[128,128]{1,0:T(8,128)(2,1)S(1)}, bf16[128,128]{1,0:T(8,128)(2,1)S(1)}, u32[]{:S(2)}, u32[]{:S(2)}) collective-permute-start(bf16[128,128]{1,0:T(8,128)(2,1)S(1)} %get-tuple-element.39), channel_id=1, source_target_pairs={{0,8},{8,16},{16,24},{24,32},{32,40},{40,48},{48,56},{56,64},{64,7... | collective-permute-start | bytes 98312 | tf_op jit(solution)/shard_map/ppermute | solution.py:648
  98.2 7.2 %collective-permute-start.4 = (bf16[128,128]{1,0:T(8,128)(2,1)S(1)}, bf16[128,128]{1,0:T(8,128)(2,1)S(1)}, u32[]{:S(2)}, u32[]{:S(2)}) collective-permute-start(bf16[128,128]{1,0:T(8,128)(2,1)S(1)} %get-tuple-element.39), channel_id=1, source_target_pairs={{0,120},{8,0},{16,8},{24,16},{32,24},{40,32},{48,40},{56,48},{64,5... | collective-permute-start | bytes 98312 | tf_op jit(solution)/shard_map/ppermute | solution.py:648
  105.4 5.3 %collective-permute-start.6 = (bf16[3,128,128]{2,1,0:T(8,128)(2,1)S(1)}, bf16[3,128,128]{2,1,0:T(8,128)(2,1)S(1)}, u32[]{:S(2)}, u32[]{:S(2)}) collective-permute-start(bf16[3,128,128]{2,1,0:T(8,128)(2,1)S(1)} %pad_maximum_fusion.2.middle_ref), channel_id=1, source_target_pairs={{0,1},{1,2},{2,3},{3,4},{4,5},{5,6},{6,7},{7,0},{8,9},{9,10},{10,1... | collective-permute-start | bytes 294920 | tf_op jit(solution)/shard_map/ppermute | solution.py:648
  105.5 5.2 %collective-permute-start.7 = (bf16[3,128,128]{2,1,0:T(8,128)(2,1)S(1)}, bf16[3,128,128]{2,1,0:T(8,128)(2,1)S(1)}, u32[]{:S(2)}, u32[]{:S(2)}) collective-permute-start(bf16[3,128,128]{2,1,0:T(8,128)(2,1)S(1)} %pad_maximum_fusion.2.middle_ref), channel_id=1, source_target_pairs={{0,7},{1,0},{2,1},{3,2},{4,3},{5,4},{6,5},{7,6},{8,15},{9,8},{10,9... | collective-permute-start | bytes 294920 | tf_op jit(solution)/shard_map/ppermute | solution.py:648

commit v5 on v4

--- a/solution.py
+++ b/solution.py
@@ -13,9 +13,9 @@
 
 def pack_kernel(records_ref, slots_ref, bricks_ref, messages_ref, buffer_ref, in_sem, out_sem):
     buckets = slots_ref.shape[0]
-    chunk = buckets // 8
+    chunk = buckets // 4
     incoming, outgoing = [], []
-    for part in range(8):
+    for part in range(4):
         here = slice(part * chunk, part * chunk + chunk)
         incoming.append(
             pltpu.make_async_copy(records_ref.at[here], buffer_ref.at[here, 0:64], in_sem.at[part])
@@ -41,7 +41,7 @@
     row = lax.broadcasted_iota(jnp.int32, shape, 1)
     mine = (lax.broadcasted_iota(jnp.int32, shape, 2) & 3) == (row & 3)
 
-    for part in range(8):
+    for part in range(4):
         here = slice(part * chunk, part * chunk + chunk)
         slots = slots_ref[here]
         high = (slots >> 9) * 16 + ((slots & 31) >> 1)
@@ -74,8 +74,8 @@
         out_shape=jax.ShapeDtypeStruct((buckets, rows + 8, width), jnp.bfloat16),
         scratch_shapes=[
             pltpu.VMEM((buckets, rows + 8, width), jnp.bfloat16),
-            pltpu.SemaphoreType.DMA((8,)),
-            pltpu.SemaphoreType.DMA((8,)),
+            pltpu.SemaphoreType.DMA((4,)),
+            pltpu.SemaphoreType.DMA((4,)),
         ],
         name="pack",
     )(records, slot_voxels, brick_mask)
@@ -374,8 +374,8 @@
 def border_kernel(
     low_ref,
     high_ref,
+    north_ref,
     south_ref,
-    north_ref,
     lift_ref,
     taps_ref,
     bricks_ref,
@@ -520,7 +520,7 @@
     down_two_ref[...] = (jnp.maximum(total, 0.0) * mask).astype(jnp.bfloat16)
 
 
-def border_part(low, high, south, north, lift_block, taps, bricks, one, one_z, down_leaf, coarse, down):
+def border_part(low, high, north, south, lift_block, taps, bricks, one, one_z, down_leaf, coarse, down):
     return pl.pallas_call(
         border_kernel,
         out_shape=[
@@ -548,7 +548,7 @@
         ],
         compiler_params=pltpu.CompilerParams(vmem_limit_bytes=32 << 20),
         name="leaf_border",
-    )(low, high, south, north, lift_block, taps, bricks, one, one_z, down_leaf, coarse, down)
+    )(low, high, north, south, lift_block, taps, bricks, one, one_z, down_leaf, coarse, down)
 
 
 def coarse_kernel(
@@ -664,14 +664,14 @@
     east = ring(low_x, "gx", -1)
     own_z, bricks = own_part(cells, arrived)
     west, east, own_z = lax.optimization_barrier((west, east, own_z))
+    north = ring(jnp.concatenate([west[:, :256], low_y, east[:, :256]], 0), "gy", -1)
     south = ring(jnp.concatenate([west[:, 768:], high_y, east[:, 768:]], 0), "gy", 1)
-    north = ring(jnp.concatenate([west[:, :256], low_y, east[:, :256]], 0), "gy", -1)
     one, one_z, low, high = middle_part(cells, west, east, lift_block, taps, own_z, bricks)
     features, down_two = border_part(
         low,
         high,
+        north,
         south,
-        north,
         lift_block,
         taps,
         bricks,

time: 114 us -> 111 us (0.974)
  starting transfers between devices: 28 us -> 25.5 us
    ppermute x8, starting transfers between devices: 16.8 us -> 14.4 us  [ring(): lax.ppermute(values, axis, [(i, (i + step) % count) for i in range(count)])]
  transfers between devices with their start and end apart: 9 -> 9, of which waited for: 4 -> 5; matrix products, arithmetic and copies ran while one was open for 0% -> 0% of each run, Pallas kernels for 8% -> 9%
where the time goes in v5:
time: 111 us
  Pallas kernels  47.9 us (43%)
  waiting for transfers between devices  36.1 us (33%)
  starting transfers between devices  25.5 us (23%)
    all_to_all x1, waiting for transfers between devices, per_device(): lax.all_to_all(messages, ('gx', 'gy'), split_axis=0, concat_axis=0, tiled...  29.3 us
    pallas_call x1, Pallas kernels, scatter_and_lift(): pl.pallas_call(scatter_kernel, grid=(sources // BUCKETS,), in_specs=[pl.B...  18.6 us
    ppermute x8, starting transfers between devices, ring(): lax.ppermute(values, axis, [(i, (i + step) % count) for i in range(count)])  14.4 us
    pallas_call x1, Pallas kernels, border_part(): pl.pallas_call(border_kernel, out_shape=[jax.ShapeDtypeStruct((16, 16, 16...  14 us
    all_to_all x1, starting transfers between devices, per_device(): lax.all_to_all(messages, ('gx', 'gy'), split_axis=0, concat_axis=0, tiled...  11.1 us
    ppermute x8, waiting for transfers between devices, ring(): lax.ppermute(values, axis, [(i, (i + step) % count) for i in range(count)])  6.81 us
    pallas_call x1, Pallas kernels, middle_part(): pl.pallas_call(middle_kernel, out_shape=[jax.ShapeDtypeStruct((352, 1792)...  5.11 us
    pallas_call x1, Pallas kernels, pack_messages(): pl.pallas_call(pack_kernel, in_specs=[pl.BlockSpec(memory_space=pltpu.HBM...  3.51 us
  transfers between devices with their start and end apart: 9, of which 5 were waited for; matrix products, arithmetic and copies ran while one was open for 0% of the time, Pallas kernels for 9%

profile of v5, /device:TPU:0, one launch (start us, length us, event | category | flops | bytes accessed | tf_op | source)
XLA Modules:
  0.0 110.9 jit_solution(12895409524172756976)
XLA Ops:
  0.6 3.5 %pack.1 = bf16[128,72,128]{2,1,0:T(8,128)(2,1)} custom-call(bf16[128,64,128]{2,1,0:T(8,128)(2,1)} %bitcast.8, s32[128,256]{1,0:T(8,128)} %bitcast.9, s32[2,2,4]{2,1,0:T(2,128)} %bricks_ref.1), custom_call_target="tpu_custom_call" | custom-call | tf_op jit(solution)/shard_map/pack/pallas_call | solution.py:66
  4.1 0.0 copy-start.4
  4.2 11.1 %all-to-all-start = ((bf16[128,72,128]{2,1,0:T(8,128)(2,1)}), bf16[128,72,128]{2,1,0:T(8,128)(2,1)S(1)}, u32[]{:S(2)}, u32[]{:S(2)}) async-start(bf16[128,72,128]{2,1,0:T(8,128)(2,1)} %pack.1), calls=%async_computation | async-start | bytes 4718592 | tf_op jit(solution)/shard_map/all_to_all | solution.py:655
  15.3 0.1 broadcast_multiply_fusion
  15.4 0.3 mul.27.lift_ref
  15.8 3.5 %leaf_taps.1.taps_ref = bf16[2,3,1024,256]{3,2,1,0:T(8,128)(2,1)} custom-call(bf16[2,3,3,3,64,64]{5,4,3,2,1,0:T(8,128)(2,1)} %convs_ref.1), custom_call_target="tpu_custom_call" | custom-call | tf_op jit(solution)/shard_map/leaf_taps/pallas_call | solution.py:191
  19.2 29.3 %all-to-all-done.msg_ref.arrived_ref = bf16[128,72,128]{2,1,0:T(8,128)(2,1)S(1)} async-done(((bf16[128,72,128]{2,1,0:T(8,128)(2,1)}), bf16[128,72,128]{2,1,0:T(8,128)(2,1)S(1)}, u32[]{:S(2)}, u32[]{:S(2)}) %all-to-all-start) | async-done | bytes 2359328 | tf_op jit(solution)/shard_map/all_to_all | solution.py:655
  48.5 18.6 %scatter.1 = (bf16[256,2048]{1,0:T(8,128)(2,1)S(1)}, bf16[64,1024]{1,0:T(8,128)(2,1)S(1)}, bf16[64,1024]{1,0:T(8,128)(2,1)S(1)}, bf16[256,256]{1,0:T(8,128)(2,1)S(1)}, bf16[256,256]{1,0:T(8,128)(2,1)S(1)}) custom-call(bf16[128,72,128]{2,1,0:T(8,128)(2,1)S(1)} %all-to-all-done.msg_ref.arrived_ref, bf16[256,512]{1,0:T(8,128)(2,1)S(1)} %mul.27.lift_ref), custom_call_target="tpu_custom_call" | custom-call | tf_op jit(solution)/shard_map/scatter/pallas_call | solution.py:152
  67.1 0.8 collective-permute-start
  68.0 4.6 %collective-permute-start.1 = (bf16[64,1024]{1,0:T(8,128)(2,1)S(1)}, bf16[64,1024]{1,0:T(8,128)(2,1)S(1)}, u32[]{:S(2)}, u32[]{:S(2)}) collective-permute-start(bf16[64,1024]{1,0:T(8,128)(2,1)S(1)} %get-tuple-element.25), channel_id=1, source_target_pairs={{0,120},{8,0},{16,8},{24,16},{32,24},{40,32},{48,40},{56,48},{64,5... | collective-permute-start | bytes 393224 | tf_op jit(solution)/shard_map/ppermute | solution.py:648
  72.5 0.9 leaf_own.1
  73.5 2.0 %collective-permute-done.west_ref = bf16[64,1024]{1,0:T(8,128)(2,1)S(1)} collective-permute-done((bf16[64,1024]{1,0:T(8,128)(2,1)S(1)}, bf16[64,1024]{1,0:T(8,128)(2,1)S(1)}, u32[]{:S(2)}, u32[]{:S(2)}) %collective-permute-start) | collective-permute-done | bytes 131104 | tf_op jit(solution)/shard_map/ppermute | solution.py:648
  75.5 0.0 collective-permute-start.2
  75.6 0.5 collective-permute-start.3
  76.1 5.1 %leaf_middle.1 = (bf16[352,1792]{1,0:T(8,128)(2,1)S(1)}, bf16[352,1792]{1,0:T(8,128)(2,1)S(1)}, bf16[384,256]{1,0:T(8,128)(2,1)S(1)}, bf16[384,256]{1,0:T(8,128)(2,1)S(1)}) custom-call(bf16[256,2048]{1,0:T(8,128)(2,1)S(1)} %get-tuple-element.23.cells_ref, bf16[64,1024]{1,0:T(8,128)(2,1)S(1)} %collective-permute-done.west_ref, ...), custom_call_target="tpu_custom_call" | custom-call | tf_op jit(solution)/shard_map/leaf_middle/pallas_call | solution.py:354
  81.2 0.7 collective-permute-done.3.south_ref
  81.9 14.0 %leaf_border.1 = (bf16[16,16,16,128]{3,2,1,0:T(8,128)(2,1)}, bf16[128,128]{1,0:T(8,128)(2,1)S(1)}) custom-call(bf16[384,256]{1,0:T(8,128)(2,1)S(1)} %get-tuple-element.32.low_ref, bf16[384,256]{1,0:T(8,128)(2,1)S(1)} %get-tuple-element.33.high_ref, bf16[384,256]{1,0:T(8,128)(2,1)S(1)} %collective-permute-done.2.north_ref, ...), custom_call_target="tpu_custom_call" | custom-call | tf_op jit(solution)/shard_map/leaf_border/pallas_call | solution.py:524
  95.9 0.1 collective-permute-start.5
  96.0 5.4 %collective-permute-start.4 = (bf16[128,128]{1,0:T(8,128)(2,1)S(1)}, bf16[128,128]{1,0:T(8,128)(2,1)S(1)}, u32[]{:S(2)}, u32[]{:S(2)}) collective-permute-start(bf16[128,128]{1,0:T(8,128)(2,1)S(1)} %get-tuple-element.39), channel_id=1, source_target_pairs={{0,120},{8,0},{16,8},{24,16},{32,24},{40,32},{48,40},{56,48},{64,5... | collective-permute-start | bytes 98312 | tf_op jit(solution)/shard_map/ppermute | solution.py:648
  101.4 1.8 %collective-permute-done.5 = bf16[128,128]{1,0:T(8,128)(2,1)S(1)} collective-permute-done((bf16[128,128]{1,0:T(8,128)(2,1)S(1)}, bf16[128,128]{1,0:T(8,128)(2,1)S(1)}, u32[]{:S(2)}, u32[]{:S(2)}) %collective-permute-start.5) | collective-permute-done | bytes 32800 | tf_op jit(solution)/shard_map/ppermute | solution.py:648
  103.2 0.0 collective-permute-start.6
  103.2 2.9 %collective-permute-start.7 = (bf16[3,128,128]{2,1,0:T(8,128)(2,1)S(1)}, bf16[3,128,128]{2,1,0:T(8,128)(2,1)S(1)}, u32[]{:S(2)}, u32[]{:S(2)}) collective-permute-start(bf16[3,128,128]{2,1,0:T(8,128)(2,1)S(1)} %pad_maximum_fusion.2.middle_ref), channel_id=1, source_target_pairs={{0,7},{1,0},{2,1},{3,2},{4,3},{5,4},{6,5},{7,6},{8,15},{9,8},{10,9... | collective-permute-start | bytes 294920 | tf_op jit(solution)/shard_map/ppermute | solution.py:648
  106.2 2.3 %collective-permute-done.6.south_ref = bf16[3,128,128]{2,1,0:T(8,128)(2,1)S(1)} collective-permute-done((bf16[3,128,128]{2,1,0:T(8,128)(2,1)S(1)}, bf16[3,128,128]{2,1,0:T(8,128)(2,1)S(1)}, u32[]{:S(2)}, u32[]{:S(2)}) %collective-permute-start.6) | collective-permute-done | bytes 98336 | tf_op jit(solution)/shard_map/ppermute | solution.py:648
  108.5 2.4 %coarse_levels.1 = bf16[2,2,4,128]{3,2,1,0:T(4,128)(2,1)} custom-call(bf16[3,128,128]{2,1,0:T(8,128)(2,1)S(1)} %collective-permute-done.6.south_ref, bf16[3,128,128]{2,1,0:T(8,128)(2,1)S(1)} %pad_maximum_fusion.2.middle_ref, bf16[3,128,128]{2,1,0:T(8,128)(2,1)S(1)} %collective-permute-done.7.north_ref, bf16[3,3,3,3,128,128]{5,4,3,2,1,0:T(8,128)(2,1)S(1)} %copy-done.1, ...), custom_call_target="tpu_custom_call" | custom-call | tf_op jit(solution)/shard_map/coarse_levels/pallas_call | solution.py:636
  (18 shorter events, 0.1 us)
Async XLA Ops:
  4.1 11.2 %copy-start.4 = (bf16[32,64]{1,0:T(8,128)(2,1)S(1)}, bf16[32,64]{1,0:T(8,128)(2,1)}, u32[]{:S(2)}) copy-start(bf16[32,64]{1,0:T(8,128)(2,1)} %param.11) | copy-start | bytes 12292
  4.2 44.4 %all-to-all-start = ((bf16[128,72,128]{2,1,0:T(8,128)(2,1)}), bf16[128,72,128]{2,1,0:T(8,128)(2,1)S(1)}, u32[]{:S(2)}, u32[]{:S(2)}) async-start(bf16[128,72,128]{2,1,0:T(8,128)(2,1)} %pack.1), calls=%async_computation | async-start | bytes 4718592 | tf_op jit(solution)/shard_map/all_to_all | solution.py:655
  67.1 9.0 %copy-start = (bf16[2,3,1024,256]{3,2,1,0:T(8,128)(2,1)S(1)}, bf16[2,3,1024,256]{3,2,1,0:T(8,128)(2,1)}, u32[]{:S(2)}) copy-start(bf16[2,3,1024,256]{3,2,1,0:T(8,128)(2,1)} %leaf_taps.1.taps_ref) | copy-start | bytes 9437188
  67.1 8.4 %collective-permute-start = (bf16[64,1024]{1,0:T(8,128)(2,1)S(1)}, bf16[64,1024]{1,0:T(8,128)(2,1)S(1)}, u32[]{:S(2)}, u32[]{:S(2)}) collective-permute-start(bf16[64,1024]{1,0:T(8,128)(2,1)S(1)} %get-tuple-element.24), channel_id=1, source_target_pairs={{0,8},{8,16},{16,24},{24,32},{32,40},{40,48},{48,56},{56,64},{64,7... | collective-permute-start | bytes 393224 | tf_op jit(solution)/shard_map/ppermute | solution.py:648
  68.0 7.5 %collective-permute-start.1 = (bf16[64,1024]{1,0:T(8,128)(2,1)S(1)}, bf16[64,1024]{1,0:T(8,128)(2,1)S(1)}, u32[]{:S(2)}, u32[]{:S(2)}) collective-permute-start(bf16[64,1024]{1,0:T(8,128)(2,1)S(1)} %get-tuple-element.25), channel_id=1, source_target_pairs={{0,120},{8,0},{16,8},{24,16},{32,24},{40,32},{48,40},{56,48},{64,5... | collective-permute-start | bytes 393224 | tf_op jit(solution)/shard_map/ppermute | solution.py:648
  75.5 5.7 %collective-permute-start.2 = (bf16[384,256]{1,0:T(8,128)(2,1)S(1)}, bf16[384,256]{1,0:T(8,128)(2,1)S(1)}, u32[]{:S(2)}, u32[]{:S(2)}) collective-permute-start(bf16[384,256]{1,0:T(8,128)(2,1)S(1)} %pad_maximum_fusion), channel_id=1, source_target_pairs={{0,7},{1,0},{2,1},{3,2},{4,3},{5,4},{6,5},{7,6},{8,15},{9,8},{10,9... | collective-permute-start | bytes 589832 | tf_op jit(solution)/shard_map/ppermute | solution.py:648
  75.6 6.3 %collective-permute-start.3 = (bf16[384,256]{1,0:T(8,128)(2,1)S(1)}, bf16[384,256]{1,0:T(8,128)(2,1)S(1)}, u32[]{:S(2)}, u32[]{:S(2)}) collective-permute-start(bf16[384,256]{1,0:T(8,128)(2,1)S(1)} %pad_maximum_fusion.1), channel_id=1, source_target_pairs={{0,1},{1,2},{2,3},{3,4},{4,5},{5,6},{6,7},{7,0},{8,9},{9,10},{10,1... | collective-permute-start | bytes 589832 | tf_op jit(solution)/shard_map/ppermute | solution.py:648
  76.1 5.8 %copy-start.3 = (bf16[2,2,2,64,128]{4,3,2,1,0:T(8,128)(2,1)S(1)}, bf16[2,2,2,64,128]{4,3,2,1,0:T(8,128)(2,1)}, u32[]{:S(2)}) copy-start(bf16[2,2,2,64,128]{4,3,2,1,0:T(8,128)(2,1)} %down_leaf_ref.1) | copy-start | bytes 393220
  81.9 26.6 %copy-start.1 = (bf16[3,3,3,3,128,128]{5,4,3,2,1,0:T(8,128)(2,1)S(1)}, bf16[3,3,3,3,128,128]{5,4,3,2,1,0:T(8,128)(2,1)}, u32[]{:S(2)}) copy-start(bf16[3,3,3,3,128,128]{5,4,3,2,1,0:T(8,128)(2,1)} %coarse_ref.3) | copy-start | bytes 7962628
  81.9 26.6 %copy-start.2 = (bf16[2,2,2,2,128,128]{5,4,3,2,1,0:T(8,128)(2,1)S(1)}, bf16[2,2,2,2,128,128]{5,4,3,2,1,0:T(8,128)(2,1)}, u32[]{:S(2)}) copy-start(bf16[2,2,2,2,128,128]{5,4,3,2,1,0:T(8,128)(2,1)} %down_ref.3) | copy-start | bytes 1572868
  95.9 7.3 %collective-permute-start.5 = (bf16[128,128]{1,0:T(8,128)(2,1)S(1)}, bf16[128,128]{1,0:T(8,128)(2,1)S(1)}, u32[]{:S(2)}, u32[]{:S(2)}) collective-permute-start(bf16[128,128]{1,0:T(8,128)(2,1)S(1)} %get-tuple-element.39), channel_id=1, source_target_pairs={{0,8},{8,16},{16,24},{24,32},{32,40},{40,48},{48,56},{56,64},{64,7... | collective-permute-start | bytes 98312 | tf_op jit(solution)/shard_map/ppermute | solution.py:648
  96.0 7.2 %collective-permute-start.4 = (bf16[128,128]{1,0:T(8,128)(2,1)S(1)}, bf16[128,128]{1,0:T(8,128)(2,1)S(1)}, u32[]{:S(2)}, u32[]{:S(2)}) collective-permute-start(bf16[128,128]{1,0:T(8,128)(2,1)S(1)} %get-tuple-element.39), channel_id=1, source_target_pairs={{0,120},{8,0},{16,8},{24,16},{32,24},{40,32},{48,40},{56,48},{64,5... | collective-permute-start | bytes 98312 | tf_op jit(solution)/shard_map/ppermute | solution.py:648
  103.2 5.3 %collective-permute-start.6 = (bf16[3,128,128]{2,1,0:T(8,128)(2,1)S(1)}, bf16[3,128,128]{2,1,0:T(8,128)(2,1)S(1)}, u32[]{:S(2)}, u32[]{:S(2)}) collective-permute-start(bf16[3,128,128]{2,1,0:T(8,128)(2,1)S(1)} %pad_maximum_fusion.2.middle_ref), channel_id=1, source_target_pairs={{0,1},{1,2},{2,3},{3,4},{4,5},{5,6},{6,7},{7,0},{8,9},{9,10},{10,1... | collective-permute-start | bytes 294920 | tf_op jit(solution)/shard_map/ppermute | solution.py:648
  103.2 5.2 %collective-permute-start.7 = (bf16[3,128,128]{2,1,0:T(8,128)(2,1)S(1)}, bf16[3,128,128]{2,1,0:T(8,128)(2,1)S(1)}, u32[]{:S(2)}, u32[]{:S(2)}) collective-permute-start(bf16[3,128,128]{2,1,0:T(8,128)(2,1)S(1)} %pad_maximum_fusion.2.middle_ref), channel_id=1, source_target_pairs={{0,7},{1,0},{2,1},{3,2},{4,3},{5,4},{6,5},{7,6},{8,15},{9,8},{10,9... | collective-permute-start | bytes 294920 | tf_op jit(solution)/shard_map/ppermute | solution.py:648

commit v6 on v5

--- a/solution.py
+++ b/solution.py
@@ -82,7 +82,7 @@
 
 
 def scatter_kernel(
-    msg_ref, lift_ref, cells_ref, west_ref, east_ref, south_ref, north_ref, total_ref
+    msg_ref, coarse_ref, fine_ref, west_ref, east_ref, south_ref, north_ref, total_ref
 ):
     step = pl.program_id(0)
 
@@ -134,34 +134,32 @@
         for part in range(4):
             summed = jnp.transpose(total_ref[part * wide : part * wide + wide])
             coarse = summed.astype(jnp.bfloat16)
-            west_ref[:, part * wide : part * wide + wide] = coarse[:64]
-            east_ref[:, part * wide : part * wide + wide] = coarse[192:]
+            lanes = slice(part * wide, part * wide + wide)
+            coarse_ref[:, lanes] = coarse
+            fine_ref[:, lanes] = (summed - coarse.astype(jnp.float32)).astype(jnp.bfloat16)
+            west_ref[:, lanes] = coarse[:64]
+            east_ref[:, lanes] = coarse[192:]
             if part == 0:
                 south_ref[...] = coarse
             if part == 3:
                 north_ref[...] = coarse
-            fine = (summed - coarse.astype(jnp.float32)).astype(jnp.bfloat16)
-            lifted = jnp.dot(coarse, lift_ref[...], preferred_element_type=jnp.float32)
-            lifted += jnp.dot(fine, lift_ref[...], preferred_element_type=jnp.float32)
-            cells_ref[:, part * 512 : part * 512 + 512] = lifted.astype(jnp.bfloat16)
-
-
-def scatter_and_lift(messages, lift_block):
+
+
+def scatter(messages):
     sources, rows, width = messages.shape
-    shapes = [(256, 2048), (64, 1024), (64, 1024), (256, 256), (256, 256)]
+    shapes = [(256, 1024)] * 2 + [(64, 1024)] * 2 + [(256, 256)] * 2
     return pl.pallas_call(
         scatter_kernel,
         grid=(sources // BUCKETS,),
         in_specs=[
             pl.BlockSpec((BUCKETS, rows, width), lambda i: (i, 0, 0)),
-            pl.BlockSpec((256, 512), lambda i: (0, 0)),
-        ],
-        out_specs=[pl.BlockSpec(memory_space=pltpu.VMEM)] * 5,
+        ],
+        out_specs=[pl.BlockSpec(memory_space=pltpu.VMEM)] * 6,
         out_shape=[jax.ShapeDtypeStruct(shape, jnp.bfloat16) for shape in shapes],
         scratch_shapes=[pltpu.VMEM((1024, 256), jnp.float32)],
         compiler_params=pltpu.CompilerParams(vmem_limit_bytes=14 << 20),
         name="scatter",
-    )(messages, lift_block)
+    )(messages)
 
 
 def leaf_taps_kernel(convs_ref, taps_ref):
@@ -262,7 +260,17 @@
     return [total[i * rows : i * rows + rows] for i in range(len(sources))]
 
 
-def own_kernel(cells_ref, arrived_ref, cell_z_ref, bricks_ref, near_vmem, near_sem):
+def own_kernel(
+    coarse_ref,
+    fine_ref,
+    lift_ref,
+    arrived_ref,
+    cells_ref,
+    cell_z_ref,
+    bricks_ref,
+    near_vmem,
+    near_sem,
+):
     last_x, last_y = lax.axis_size("gx") - 1, lax.axis_size("gy") - 1
     copies = []
     for x in range(3):
@@ -277,10 +285,15 @@
     for copy in copies:
         copy.start()
 
-    @pl.loop(0, 8)
-    def _(step):
-        lanes = pl.ds(pl.multiple_of(step * 256, 256), 256)
-        cell_z_ref[:, lanes] = z_neighbours(cells_ref[:, lanes].astype(jnp.float32))
+    @pl.loop(0, 4)
+    def _(part):
+        sums = pl.ds(pl.multiple_of(part * 256, 256), 256)
+        lanes = pl.ds(pl.multiple_of(part * 512, 512), 512)
+        lifted = jnp.dot(coarse_ref[:, sums], lift_ref[...], preferred_element_type=jnp.float32)
+        lifted += jnp.dot(fine_ref[:, sums], lift_ref[...], preferred_element_type=jnp.float32)
+        cells = lifted.astype(jnp.bfloat16)
+        cells_ref[:, lanes] = cells
+        cell_z_ref[:, lanes] = z_neighbours(cells.astype(jnp.float32))
 
     for copy in copies:
         copy.wait()
@@ -288,22 +301,24 @@
         bricks_ref[index] = column
 
 
-def own_part(cells, arrived):
+def own_part(coarse, fine, lift_block, arrived):
     return pl.pallas_call(
         own_kernel,
         out_shape=[
             jax.ShapeDtypeStruct((256, 2048), jnp.bfloat16),
+            jax.ShapeDtypeStruct((256, 2048), jnp.bfloat16),
             jax.ShapeDtypeStruct((16, 8, 128), jnp.float32),
         ],
-        in_specs=[pl.BlockSpec(memory_space=pltpu.VMEM), pl.BlockSpec(memory_space=pl.ANY)],
-        out_specs=[pl.BlockSpec(memory_space=pltpu.VMEM)] * 2,
+        in_specs=[pl.BlockSpec(memory_space=pltpu.VMEM)] * 3
+        + [pl.BlockSpec(memory_space=pl.ANY)],
+        out_specs=[pl.BlockSpec(memory_space=pltpu.VMEM)] * 3,
         scratch_shapes=[
             pltpu.VMEM((9, 8, 128), jnp.bfloat16),
             pltpu.SemaphoreType.DMA((3, 3)),
         ],
         compiler_params=pltpu.CompilerParams(vmem_limit_bytes=8 << 20),
         name="leaf_own",
-    )(cells, arrived)
+    )(coarse, fine, lift_block, arrived)
 
 
 def middle_kernel(
@@ -552,9 +567,9 @@
 
 
 def coarse_kernel(
+    north_ref,
+    middle_ref,
     south_ref,
-    middle_ref,
-    north_ref,
     coarse_ref,
     down_ref,
     bricks_ref,
@@ -632,7 +647,7 @@
             top_ref[x, y] = top[row : row + 4]
 
 
-def coarse_levels(south, middle, north, coarse, down, bricks):
+def coarse_levels(north, middle, south, coarse, down, bricks):
     return pl.pallas_call(
         coarse_kernel,
         out_shape=jax.ShapeDtypeStruct((2, 2, 4, 128), jnp.bfloat16),
@@ -640,7 +655,7 @@
         scratch_shapes=[pltpu.VMEM((2, 128, 128), jnp.float32)],
         compiler_params=pltpu.CompilerParams(vmem_limit_bytes=16 << 20),
         name="coarse_levels",
-    )(south, middle, north, coarse, down, bricks)
+    )(north, middle, south, coarse, down, bricks)
 
 
 def ring(values, axis, step):
@@ -659,10 +674,10 @@
     coarse_hbm = pltpu.with_memory_space_constraint(coarse_convs, pltpu.HBM)
     down_hbm = pltpu.with_memory_space_constraint(down_coarse, pltpu.HBM)
 
-    cells, low_x, high_x, low_y, high_y = scatter_and_lift(arrived, lift_block)
+    coarse, fine, low_x, high_x, low_y, high_y = scatter(arrived)
     west = ring(high_x, "gx", 1)
     east = ring(low_x, "gx", -1)
-    own_z, bricks = own_part(cells, arrived)
+    cells, own_z, bricks = own_part(coarse, fine, lift_block, arrived)
     west, east, own_z = lax.optimization_barrier((west, east, own_z))
     north = ring(jnp.concatenate([west[:, :256], low_y, east[:, :256]], 0), "gy", -1)
     south = ring(jnp.concatenate([west[:, 768:], high_y, east[:, 768:]], 0), "gy", 1)
@@ -686,7 +701,7 @@
     middle = jnp.stack([east, down_two, west])
     south = ring(middle, "gy", 1)
     north = ring(middle, "gy", -1)
-    top = coarse_levels(south, middle, north, coarse_convs, down_coarse, bricks)
+    top = coarse_levels(north, middle, south, coarse_convs, down_coarse, bricks)
     return (features, top)
 
 

time: 111 us -> 111 us (level)
  no operation moved by 1% of the time
where the time goes in v6:
time: 111 us
  Pallas kernels  48.5 us (44%)
  waiting for transfers between devices  35.2 us (32%)
  starting transfers between devices  25.5 us (23%)
    all_to_all x1, waiting for transfers between devices, per_device(): lax.all_to_all(messages, ('gx', 'gy'), split_axis=0, concat_axis=0, tiled...  29.3 us
    pallas_call x1, Pallas kernels, scatter(): pl.pallas_call(scatter_kernel, grid=(sources // BUCKETS,), in_specs=[pl.B...  18.2 us
    ppermute x8, starting transfers between devices, ring(): lax.ppermute(values, axis, [(i, (i + step) % count) for i in range(count)])  14.4 us
    pallas_call x1, Pallas kernels, border_part(): pl.pallas_call(border_kernel, out_shape=[jax.ShapeDtypeStruct((16, 16, 16...  14 us
    all_to_all x1, starting transfers between devices, per_device(): lax.all_to_all(messages, ('gx', 'gy'), split_axis=0, concat_axis=0, tiled...  11.1 us
    ppermute x8, waiting for transfers between devices, ring(): lax.ppermute(values, axis, [(i, (i + step) % count) for i in range(count)])  5.88 us
    pallas_call x1, Pallas kernels, middle_part(): pl.pallas_call(middle_kernel, out_shape=[jax.ShapeDtypeStruct((352, 1792)...  5.11 us
    pallas_call x1, Pallas kernels, pack_messages(): pl.pallas_call(pack_kernel, in_specs=[pl.BlockSpec(memory_space=pltpu.HBM...  3.51 us
  transfers between devices with their start and end apart: 9, of which 5 were waited for; matrix products, arithmetic and copies ran while one was open for 0% of the time, Pallas kernels for 9%

profile of v6, /device:TPU:0, one launch (start us, length us, event | category | flops | bytes accessed | tf_op | source)
XLA Modules:
  0.0 110.5 jit_solution(6783459618009508589)
XLA Ops:
  0.6 3.5 %pack.1 = bf16[128,72,128]{2,1,0:T(8,128)(2,1)} custom-call(bf16[128,64,128]{2,1,0:T(8,128)(2,1)} %bitcast.8, s32[128,256]{1,0:T(8,128)} %bitcast.9, s32[2,2,4]{2,1,0:T(2,128)} %bricks_ref.1), custom_call_target="tpu_custom_call" | custom-call | tf_op jit(solution)/shard_map/pack/pallas_call | solution.py:66
  4.1 0.0 copy-start.4
  4.2 11.1 %all-to-all-start = ((bf16[128,72,128]{2,1,0:T(8,128)(2,1)}), bf16[128,72,128]{2,1,0:T(8,128)(2,1)S(1)}, u32[]{:S(2)}, u32[]{:S(2)}) async-start(bf16[128,72,128]{2,1,0:T(8,128)(2,1)} %pack.1), calls=%async_computation | async-start | bytes 4718592 | tf_op jit(solution)/shard_map/all_to_all | solution.py:670
  15.3 0.1 broadcast_multiply_fusion
  15.4 0.3 mul.27.lift_ref
  15.8 3.5 %leaf_taps.1.taps_ref = bf16[2,3,1024,256]{3,2,1,0:T(8,128)(2,1)} custom-call(bf16[2,3,3,3,64,64]{5,4,3,2,1,0:T(8,128)(2,1)} %convs_ref.1), custom_call_target="tpu_custom_call" | custom-call | tf_op jit(solution)/shard_map/leaf_taps/pallas_call | solution.py:189
  19.2 29.3 %all-to-all-done.msg_ref.arrived_ref = bf16[128,72,128]{2,1,0:T(8,128)(2,1)S(1)} async-done(((bf16[128,72,128]{2,1,0:T(8,128)(2,1)}), bf16[128,72,128]{2,1,0:T(8,128)(2,1)S(1)}, u32[]{:S(2)}, u32[]{:S(2)}) %all-to-all-start) | async-done | bytes 2359328 | tf_op jit(solution)/shard_map/all_to_all | solution.py:670
  48.5 18.2 %scatter.1 = (bf16[256,1024]{1,0:T(8,128)(2,1)S(1)}, bf16[256,1024]{1,0:T(8,128)(2,1)S(1)}, bf16[64,1024]{1,0:T(8,128)(2,1)S(1)}, bf16[64,1024]{1,0:T(8,128)(2,1...) custom-call(bf16[128,72,128]{2,1,0:T(8,128)(2,1)S(1)} %all-to-all-done.msg_ref.arrived_ref), custom_call_target="tpu_custom_call" | custom-call | tf_op jit(solution)/shard_map/scatter/pallas_call | solution.py:151
  66.8 0.8 collective-permute-start
  67.6 4.6 %collective-permute-start.1 = (bf16[64,1024]{1,0:T(8,128)(2,1)S(1)}, bf16[64,1024]{1,0:T(8,128)(2,1)S(1)}, u32[]{:S(2)}, u32[]{:S(2)}) collective-permute-start(bf16[64,1024]{1,0:T(8,128)(2,1)S(1)} %get-tuple-element.29), channel_id=1, source_target_pairs={{0,120},{8,0},{16,8},{24,16},{32,24},{40,32},{48,40},{56,48},{64,5... | collective-permute-start | bytes 393224 | tf_op jit(solution)/shard_map/ppermute | solution.py:663
  72.2 1.8 %leaf_own.1 = (bf16[256,2048]{1,0:T(8,128)(2,1)S(1)}, bf16[256,2048]{1,0:T(8,128)(2,1)S(1)}, f32[16,8,128]{2,1,0:T(8,128)S(1)}) custom-call(bf16[256,1024]{1,0:T(8,128)(2,1)S(1)} %get-tuple-element.24.coarse_ref, bf16[256,1024]{1,0:T(8,128)(2,1)S(1)} %get-tuple-element.25.fine_ref, bf16[256,512]{1,0:T(8,128)(2,1)S(1)} %mul.27.lift_ref, ...), custom_call_target="tpu_custom_call" | custom-call | tf_op jit(solution)/shard_map/leaf_own/pallas_call | solution.py:305
  74.0 1.1 collective-permute-done.west_ref
  75.2 0.0 collective-permute-start.2
  75.2 0.5 collective-permute-start.3
  75.7 5.1 %leaf_middle.1 = (bf16[352,1792]{1,0:T(8,128)(2,1)S(1)}, bf16[352,1792]{1,0:T(8,128)(2,1)S(1)}, bf16[384,256]{1,0:T(8,128)(2,1)S(1)}, bf16[384,256]{1,0:T(8,128)(2,1)S(1)}) custom-call(bf16[256,2048]{1,0:T(8,128)(2,1)S(1)} %get-tuple-element.27.cells_ref, bf16[64,1024]{1,0:T(8,128)(2,1)S(1)} %collective-permute-done.west_ref, ...), custom_call_target="tpu_custom_call" | custom-call | tf_op jit(solution)/shard_map/leaf_middle/pallas_call | solution.py:369
  80.8 0.7 collective-permute-done.3.south_ref
  81.5 14.0 %leaf_border.1 = (bf16[16,16,16,128]{3,2,1,0:T(8,128)(2,1)}, bf16[128,128]{1,0:T(8,128)(2,1)S(1)}) custom-call(bf16[384,256]{1,0:T(8,128)(2,1)S(1)} %get-tuple-element.36.low_ref, bf16[384,256]{1,0:T(8,128)(2,1)S(1)} %get-tuple-element.37.high_ref, bf16[384,256]{1,0:T(8,128)(2,1)S(1)} %collective-permute-done.2.north_ref, ...), custom_call_target="tpu_custom_call" | custom-call | tf_op jit(solution)/shard_map/leaf_border/pallas_call | solution.py:539
  95.5 0.1 collective-permute-start.5
  95.6 5.4 %collective-permute-start.4 = (bf16[128,128]{1,0:T(8,128)(2,1)S(1)}, bf16[128,128]{1,0:T(8,128)(2,1)S(1)}, u32[]{:S(2)}, u32[]{:S(2)}) collective-permute-start(bf16[128,128]{1,0:T(8,128)(2,1)S(1)} %get-tuple-element.43), channel_id=1, source_target_pairs={{0,120},{8,0},{16,8},{24,16},{32,24},{40,32},{48,40},{56,48},{64,5... | collective-permute-start | bytes 98312 | tf_op jit(solution)/shard_map/ppermute | solution.py:663
  101.0 1.8 %collective-permute-done.5 = bf16[128,128]{1,0:T(8,128)(2,1)S(1)} collective-permute-done((bf16[128,128]{1,0:T(8,128)(2,1)S(1)}, bf16[128,128]{1,0:T(8,128)(2,1)S(1)}, u32[]{:S(2)}, u32[]{:S(2)}) %collective-permute-start.5) | collective-permute-done | bytes 32800 | tf_op jit(solution)/shard_map/ppermute | solution.py:663
  102.8 0.0 collective-permute-start.7
  102.9 2.9 %collective-permute-start.6 = (bf16[3,128,128]{2,1,0:T(8,128)(2,1)S(1)}, bf16[3,128,128]{2,1,0:T(8,128)(2,1)S(1)}, u32[]{:S(2)}, u32[]{:S(2)}) collective-permute-start(bf16[3,128,128]{2,1,0:T(8,128)(2,1)S(1)} %pad_maximum_fusion.2.middle_ref), channel_id=1, source_target_pairs={{0,7},{1,0},{2,1},{3,2},{4,3},{5,4},{6,5},{7,6},{8,15},{9,8},{10,9... | collective-permute-start | bytes 294920 | tf_op jit(solution)/shard_map/ppermute | solution.py:663
  105.8 2.3 %collective-permute-done.7.south_ref = bf16[3,128,128]{2,1,0:T(8,128)(2,1)S(1)} collective-permute-done((bf16[3,128,128]{2,1,0:T(8,128)(2,1)S(1)}, bf16[3,128,128]{2,1,0:T(8,128)(2,1)S(1)}, u32[]{:S(2)}, u32[]{:S(2)}) %collective-permute-start.7) | collective-permute-done | bytes 98336 | tf_op jit(solution)/shard_map/ppermute | solution.py:663
  108.1 2.4 %coarse_levels.1 = bf16[2,2,4,128]{3,2,1,0:T(4,128)(2,1)} custom-call(bf16[3,128,128]{2,1,0:T(8,128)(2,1)S(1)} %collective-permute-done.6.north_ref, bf16[3,128,128]{2,1,0:T(8,128)(2,1)S(1)} %pad_maximum_fusion.2.middle_ref, bf16[3,128,128]{2,1,0:T(8,128)(2,1)S(1)} %collective-permute-done.7.south_ref, bf16[3,3,3,3,128,128]{5,4,3,2,1,0:T(8,128)(2,1)S(1)} %copy-done.1, ...), custom_call_target="tpu_custom_call" | custom-call | tf_op jit(solution)/shard_map/coarse_levels/pallas_call | solution.py:651
  (18 shorter events, 0.1 us)
Async XLA Ops:
  4.1 11.2 %copy-start.4 = (bf16[32,64]{1,0:T(8,128)(2,1)S(1)}, bf16[32,64]{1,0:T(8,128)(2,1)}, u32[]{:S(2)}) copy-start(bf16[32,64]{1,0:T(8,128)(2,1)} %param.11) | copy-start | bytes 12292
  4.2 44.4 %all-to-all-start = ((bf16[128,72,128]{2,1,0:T(8,128)(2,1)}), bf16[128,72,128]{2,1,0:T(8,128)(2,1)S(1)}, u32[]{:S(2)}, u32[]{:S(2)}) async-start(bf16[128,72,128]{2,1,0:T(8,128)(2,1)} %pack.1), calls=%async_computation | async-start | bytes 4718592 | tf_op jit(solution)/shard_map/all_to_all | solution.py:670
  66.8 8.4 %collective-permute-start = (bf16[64,1024]{1,0:T(8,128)(2,1)S(1)}, bf16[64,1024]{1,0:T(8,128)(2,1)S(1)}, u32[]{:S(2)}, u32[]{:S(2)}) collective-permute-start(bf16[64,1024]{1,0:T(8,128)(2,1)S(1)} %get-tuple-element.28), channel_id=1, source_target_pairs={{0,8},{8,16},{16,24},{24,32},{32,40},{40,48},{48,56},{56,64},{64,7... | collective-permute-start | bytes 393224 | tf_op jit(solution)/shard_map/ppermute | solution.py:663
  67.6 7.5 %collective-permute-start.1 = (bf16[64,1024]{1,0:T(8,128)(2,1)S(1)}, bf16[64,1024]{1,0:T(8,128)(2,1)S(1)}, u32[]{:S(2)}, u32[]{:S(2)}) collective-permute-start(bf16[64,1024]{1,0:T(8,128)(2,1)S(1)} %get-tuple-element.29), channel_id=1, source_target_pairs={{0,120},{8,0},{16,8},{24,16},{32,24},{40,32},{48,40},{56,48},{64,5... | collective-permute-start | bytes 393224 | tf_op jit(solution)/shard_map/ppermute | solution.py:663
  72.2 3.5 %copy-start = (bf16[2,3,1024,256]{3,2,1,0:T(8,128)(2,1)S(1)}, bf16[2,3,1024,256]{3,2,1,0:T(8,128)(2,1)}, u32[]{:S(2)}) copy-start(bf16[2,3,1024,256]{3,2,1,0:T(8,128)(2,1)} %leaf_taps.1.taps_ref) | copy-start | bytes 9437188
  75.2 5.7 %collective-permute-start.2 = (bf16[384,256]{1,0:T(8,128)(2,1)S(1)}, bf16[384,256]{1,0:T(8,128)(2,1)S(1)}, u32[]{:S(2)}, u32[]{:S(2)}) collective-permute-start(bf16[384,256]{1,0:T(8,128)(2,1)S(1)} %pad_maximum_fusion), channel_id=1, source_target_pairs={{0,7},{1,0},{2,1},{3,2},{4,3},{5,4},{6,5},{7,6},{8,15},{9,8},{10,9... | collective-permute-start | bytes 589832 | tf_op jit(solution)/shard_map/ppermute | solution.py:663
  75.2 6.3 %collective-permute-start.3 = (bf16[384,256]{1,0:T(8,128)(2,1)S(1)}, bf16[384,256]{1,0:T(8,128)(2,1)S(1)}, u32[]{:S(2)}, u32[]{:S(2)}) collective-permute-start(bf16[384,256]{1,0:T(8,128)(2,1)S(1)} %pad_maximum_fusion.1), channel_id=1, source_target_pairs={{0,1},{1,2},{2,3},{3,4},{4,5},{5,6},{6,7},{7,0},{8,9},{9,10},{10,1... | collective-permute-start | bytes 589832 | tf_op jit(solution)/shard_map/ppermute | solution.py:663
  75.7 5.8 %copy-start.3 = (bf16[2,2,2,64,128]{4,3,2,1,0:T(8,128)(2,1)S(1)}, bf16[2,2,2,64,128]{4,3,2,1,0:T(8,128)(2,1)}, u32[]{:S(2)}) copy-start(bf16[2,2,2,64,128]{4,3,2,1,0:T(8,128)(2,1)} %down_leaf_ref.1) | copy-start | bytes 393220
  81.5 26.6 %copy-start.1 = (bf16[3,3,3,3,128,128]{5,4,3,2,1,0:T(8,128)(2,1)S(1)}, bf16[3,3,3,3,128,128]{5,4,3,2,1,0:T(8,128)(2,1)}, u32[]{:S(2)}) copy-start(bf16[3,3,3,3,128,128]{5,4,3,2,1,0:T(8,128)(2,1)} %coarse_ref.3) | copy-start | bytes 7962628
  81.5 26.6 %copy-start.2 = (bf16[2,2,2,2,128,128]{5,4,3,2,1,0:T(8,128)(2,1)S(1)}, bf16[2,2,2,2,128,128]{5,4,3,2,1,0:T(8,128)(2,1)}, u32[]{:S(2)}) copy-start(bf16[2,2,2,2,128,128]{5,4,3,2,1,0:T(8,128)(2,1)} %down_ref.3) | copy-start | bytes 1572868
  95.5 7.3 %collective-permute-start.5 = (bf16[128,128]{1,0:T(8,128)(2,1)S(1)}, bf16[128,128]{1,0:T(8,128)(2,1)S(1)}, u32[]{:S(2)}, u32[]{:S(2)}) collective-permute-start(bf16[128,128]{1,0:T(8,128)(2,1)S(1)} %get-tuple-element.43), channel_id=1, source_target_pairs={{0,8},{8,16},{16,24},{24,32},{32,40},{40,48},{48,56},{56,64},{64,7... | collective-permute-start | bytes 98312 | tf_op jit(solution)/shard_map/ppermute | solution.py:663
  95.6 7.2 %collective-permute-start.4 = (bf16[128,128]{1,0:T(8,128)(2,1)S(1)}, bf16[128,128]{1,0:T(8,128)(2,1)S(1)}, u32[]{:S(2)}, u32[]{:S(2)}) collective-permute-start(bf16[128,128]{1,0:T(8,128)(2,1)S(1)} %get-tuple-element.43), channel_id=1, source_target_pairs={{0,120},{8,0},{16,8},{24,16},{32,24},{40,32},{48,40},{56,48},{64,5... | collective-permute-start | bytes 98312 | tf_op jit(solution)/shard_map/ppermute | solution.py:663
  102.8 5.3 %collective-permute-start.7 = (bf16[3,128,128]{2,1,0:T(8,128)(2,1)S(1)}, bf16[3,128,128]{2,1,0:T(8,128)(2,1)S(1)}, u32[]{:S(2)}, u32[]{:S(2)}) collective-permute-start(bf16[3,128,128]{2,1,0:T(8,128)(2,1)S(1)} %pad_maximum_fusion.2.middle_ref), channel_id=1, source_target_pairs={{0,1},{1,2},{2,3},{3,4},{4,5},{5,6},{6,7},{7,0},{8,9},{9,10},{10,1... | collective-permute-start | bytes 294920 | tf_op jit(solution)/shard_map/ppermute | solution.py:663
  102.9 5.2 %collective-permute-start.6 = (bf16[3,128,128]{2,1,0:T(8,128)(2,1)S(1)}, bf16[3,128,128]{2,1,0:T(8,128)(2,1)S(1)}, u32[]{:S(2)}, u32[]{:S(2)}) collective-permute-start(bf16[3,128,128]{2,1,0:T(8,128)(2,1)S(1)} %pad_maximum_fusion.2.middle_ref), channel_id=1, source_target_pairs={{0,7},{1,0},{2,1},{3,2},{4,3},{5,4},{6,5},{7,6},{8,15},{9,8},{10,9... | collective-permute-start | bytes 294920 | tf_op jit(solution)/shard_map/ppermute | solution.py:663

commit v7 on v6

--- a/solution.py
+++ b/solution.py
@@ -84,76 +84,67 @@
 def scatter_kernel(
     msg_ref, coarse_ref, fine_ref, west_ref, east_ref, south_ref, north_ref, total_ref
 ):
-    step = pl.program_id(0)
-
-    @pl.when(step == 0)
-    def _():
-        total_ref[...] = jnp.zeros_like(total_ref)
-
+    total_ref[...] = jnp.zeros_like(total_ref)
     wide = 256
     lanes = lax.broadcasted_iota(jnp.int32, (wide, wide), 0).astype(jnp.bfloat16)
     zero = jnp.zeros((32, wide), jnp.bfloat16)
     left = lax.broadcasted_iota(jnp.int32, (8, 128), 1) < 64
-    for quad in range(BUCKETS // 4):
-        turned, ids = [], []
-        for pair in range(2):
-            first = quad * 4 + pair * 2
-            rows = jnp.concatenate([msg_ref[first, 0:64], msg_ref[first + 1, 0:64]], 0)
-            turned.append(jnp.transpose(rows))
-            ids.append(
-                jnp.where(
-                    left,
-                    msg_ref[first, 64:72].astype(jnp.float32),
-                    msg_ref[first + 1, 64:72].astype(jnp.float32),
+    @pl.loop(0, msg_ref.shape[0] // BUCKETS)
+    def _(step):
+        for quad in range(BUCKETS // 4):
+            turned, ids = [], []
+            for pair in range(2):
+                first = step * BUCKETS + quad * 4 + pair * 2
+                rows = jnp.concatenate([msg_ref[first, 0:64], msg_ref[first + 1, 0:64]], 0)
+                turned.append(jnp.transpose(rows))
+                ids.append(
+                    jnp.where(
+                        left,
+                        msg_ref[first, 64:72].astype(jnp.float32),
+                        msg_ref[first + 1, 64:72].astype(jnp.float32),
+                    )
                 )
-            )
-        turned = jnp.concatenate(turned, 1)
-        ids = jnp.concatenate(ids, 1)
-        for base in (0, 2):
-            spreads, hots = [], []
-            for quarter in (base, base + 1):
-                features = turned[quarter * 32 : quarter * 32 + 32]
-                high = jnp.broadcast_to(ids[quarter : quarter + 1], (wide, wide))
-                low = jnp.broadcast_to(ids[quarter + 4 : quarter + 5], (32, wide))
-                high, low = high.astype(jnp.bfloat16), low.astype(jnp.bfloat16)
-                hots.append(jnp.where(lanes == high, 1.0, 0.0).astype(jnp.bfloat16))
-                spreads += [
-                    jnp.concatenate(
-                        [jnp.where(low == jnp.bfloat16(i), features, zero) for i in range(32)], 0
-                    )
-                ]
-            total_ref[...] += lax.dot_general(
-                jnp.concatenate(spreads, 1),
-                jnp.concatenate(hots, 1),
-                (((1,), (1,)), ((), ())),
-                preferred_element_type=jnp.float32,
-            )
-
-    @pl.when(step == pl.num_programs(0) - 1)
-    def _():
-        for part in range(4):
-            summed = jnp.transpose(total_ref[part * wide : part * wide + wide])
-            coarse = summed.astype(jnp.bfloat16)
-            lanes = slice(part * wide, part * wide + wide)
-            coarse_ref[:, lanes] = coarse
-            fine_ref[:, lanes] = (summed - coarse.astype(jnp.float32)).astype(jnp.bfloat16)
-            west_ref[:, lanes] = coarse[:64]
-            east_ref[:, lanes] = coarse[192:]
-            if part == 0:
-                south_ref[...] = coarse
-            if part == 3:
-                north_ref[...] = coarse
+            turned = jnp.concatenate(turned, 1)
+            ids = jnp.concatenate(ids, 1)
+            for base in (0, 2):
+                spreads, hots = [], []
+                for quarter in (base, base + 1):
+                    features = turned[quarter * 32 : quarter * 32 + 32]
+                    high = jnp.broadcast_to(ids[quarter : quarter + 1], (wide, wide))
+                    low = jnp.broadcast_to(ids[quarter + 4 : quarter + 5], (32, wide))
+                    high, low = high.astype(jnp.bfloat16), low.astype(jnp.bfloat16)
+                    hots.append(jnp.where(lanes == high, 1.0, 0.0).astype(jnp.bfloat16))
+                    spreads += [
+                        jnp.concatenate(
+                            [jnp.where(low == jnp.bfloat16(i), features, zero) for i in range(32)], 0
+                        )
+                    ]
+                total_ref[...] += lax.dot_general(
+                    jnp.concatenate(spreads, 1),
+                    jnp.concatenate(hots, 1),
+                    (((1,), (1,)), ((), ())),
+                    preferred_element_type=jnp.float32,
+                )
+
+    for part in range(4):
+        summed = jnp.transpose(total_ref[part * wide : part * wide + wide])
+        coarse = summed.astype(jnp.bfloat16)
+        lanes = slice(part * wide, part * wide + wide)
+        coarse_ref[:, lanes] = coarse
+        fine_ref[:, lanes] = (summed - coarse.astype(jnp.float32)).astype(jnp.bfloat16)
+        west_ref[:, lanes] = coarse[:64]
+        east_ref[:, lanes] = coarse[192:]
+        if part == 0:
+            south_ref[...] = coarse
+        if part == 3:
+            north_ref[...] = coarse
 
 
 def scatter(messages):
-    sources, rows, width = messages.shape
     shapes = [(256, 1024)] * 2 + [(64, 1024)] * 2 + [(256, 256)] * 2
     return pl.pallas_call(
         scatter_kernel,
-        grid=(sources // BUCKETS,),
-        in_specs=[
-            pl.BlockSpec((BUCKETS, rows, width), lambda i: (i, 0, 0)),
-        ],
+        in_specs=[pl.BlockSpec(memory_space=pltpu.VMEM)],
         out_specs=[pl.BlockSpec(memory_space=pltpu.VMEM)] * 6,
         out_shape=[jax.ShapeDtypeStruct(shape, jnp.bfloat16) for shape in shapes],
         scratch_shapes=[pltpu.VMEM((1024, 256), jnp.float32)],
@@ -421,24 +412,10 @@
         pltpu.make_async_copy(one_z_middle_ref, one_z_ref.at[:, 512:2304], one_sem.at[1]),
         pltpu.make_async_copy(down_leaf_ref, down_leaf_vmem, leaf_sem),
     ]
-    copies = []
-    for dx in range(3):
-        for dz in range(3):
-            copies.append(
-                pltpu.make_async_copy(
-                    coarse_ref.at[0, dx, :, dz], coarse_vmem.at[dx, dz], coarse_sem.at[dx, dz]
-                )
-            )
-    for a in range(2):
-        for b in range(2):
-            for c in range(2):
-                copies.append(
-                    pltpu.make_async_copy(
-                        down_ref.at[0, a, b, c],
-                        down_vmem.at[a, b, :, c * 128 : c * 128 + 128],
-                        down_sem.at[a, b, c],
-                    )
-                )
+    copies = [
+        pltpu.make_async_copy(coarse_ref.at[0], coarse_vmem, coarse_sem),
+        pltpu.make_async_copy(down_ref.at[0], down_vmem, down_sem),
+    ]
     for copy in early + copies:
         copy.start()
     flags = grid_flags()
@@ -516,7 +493,8 @@
                 1,
             )
         )
-    taps = coarse_vmem[...].reshape(3456, 128)
+    taps = [coarse_vmem[dx, :, dz].reshape(384, 128) for dx in range(3) for dz in range(3)]
+    taps = jnp.concatenate(taps, 0)
     total = jnp.dot(jnp.concatenate(windows, 0), taps, preferred_element_type=jnp.float32)
     total = jnp.maximum(total, 0.0).reshape(8, 128, 128)
     masks = [leaf_mask_ref[1 + y // 4, 64:320].reshape(8, 2, 16, 128)[:, 0] for y in range(8)]
@@ -525,7 +503,12 @@
     merged = jnp.concatenate(
         [level[:, b, :, a].reshape(256, 128) for a in range(2) for b in range(2)], 1
     )
-    taps = down_vmem[...].reshape(512, 256)
+    taps = [
+        jnp.concatenate([down_vmem[a, b, c] for c in range(2)], 1)
+        for a in range(2)
+        for b in range(2)
+    ]
+    taps = jnp.concatenate(taps, 0)
     parts = jnp.dot(merged, taps, preferred_element_type=jnp.float32)
     parts_ref[0] = parts[:, :128]
     parts_ref[1] = parts[:, 128:]
@@ -554,12 +537,12 @@
             pltpu.VMEM((2, 256, 128), jnp.float32),
             pltpu.VMEM((2, 2, 2, 64, 128), jnp.bfloat16),
             pltpu.VMEM((3, 3, 3, 128, 128), jnp.bfloat16),
-            pltpu.VMEM((2, 2, 128, 256), jnp.bfloat16),
+            pltpu.VMEM((2, 2, 2, 128, 128), jnp.bfloat16),
             pltpu.VMEM((4, 384, 128), jnp.float32),
             pltpu.SemaphoreType.DMA((2,)),
             pltpu.SemaphoreType.DMA,
-            pltpu.SemaphoreType.DMA((3, 3)),
-            pltpu.SemaphoreType.DMA((2, 2, 2)),
+            pltpu.SemaphoreType.DMA,
+            pltpu.SemaphoreType.DMA,
         ],
         compiler_params=pltpu.CompilerParams(vmem_limit_bytes=32 << 20),
         name="leaf_border",

time: 111 us -> 111 us (level)
  no operation moved by 1% of the time
where the time goes in v7:
time: 111 us; the launch traced here: 110 us
  Pallas kernels  48.3 us (44%)
  waiting for transfers between devices  35.2 us (32%)
  starting transfers between devices  25.5 us (23%)
    all_to_all x1, waiting for transfers between devices, per_device(): lax.all_to_all(messages, ('gx', 'gy'), split_axis=0, concat_axis=0, tiled...  29.3 us
    pallas_call x1, Pallas kernels, scatter(): pl.pallas_call(scatter_kernel, in_specs=[pl.BlockSpec(memory_space=pltpu....  18.2 us
    ppermute x8, starting transfers between devices, ring(): lax.ppermute(values, axis, [(i, (i + step) % count) for i in range(count)])  14.4 us
    pallas_call x1, Pallas kernels, border_part(): pl.pallas_call(border_kernel, out_shape=[jax.ShapeDtypeStruct((16, 16, 16...  13.8 us
    all_to_all x1, starting transfers between devices, per_device(): lax.all_to_all(messages, ('gx', 'gy'), split_axis=0, concat_axis=0, tiled...  11.1 us
    ppermute x8, waiting for transfers between devices, ring(): lax.ppermute(values, axis, [(i, (i + step) % count) for i in range(count)])  5.89 us
    pallas_call x1, Pallas kernels, middle_part(): pl.pallas_call(middle_kernel, out_shape=[jax.ShapeDtypeStruct((352, 1792)...  5.11 us
    pallas_call x1, Pallas kernels, pack_messages(): pl.pallas_call(pack_kernel, in_specs=[pl.BlockSpec(memory_space=pltpu.HBM...  3.51 us
  transfers between devices with their start and end apart: 9, of which 5 were waited for; matrix products, arithmetic and copies ran while one was open for 0% of the time, Pallas kernels for 9%

profile of v7, /device:TPU:0, one launch (start us, length us, event | category | flops | bytes accessed | tf_op | source)
XLA Modules:
  0.0 110.3 jit_solution(11058920002576631218)
XLA Ops:
  0.6 3.5 %pack.1 = bf16[128,72,128]{2,1,0:T(8,128)(2,1)} custom-call(bf16[128,64,128]{2,1,0:T(8,128)(2,1)} %bitcast.8, s32[128,256]{1,0:T(8,128)} %bitcast.9, s32[2,2,4]{2,1,0:T(2,128)} %bricks_ref.1), custom_call_target="tpu_custom_call" | custom-call | tf_op jit(solution)/shard_map/pack/pallas_call | solution.py:66
  4.1 0.0 copy-start.4
  4.2 11.1 %all-to-all-start = ((bf16[128,72,128]{2,1,0:T(8,128)(2,1)}), bf16[128,72,128]{2,1,0:T(8,128)(2,1)S(1)}, u32[]{:S(2)}, u32[]{:S(2)}) async-start(bf16[128,72,128]{2,1,0:T(8,128)(2,1)} %pack.1), calls=%async_computation | async-start | bytes 4718592 | tf_op jit(solution)/shard_map/all_to_all | solution.py:653
  15.3 0.1 broadcast_multiply_fusion
  15.4 0.3 mul.27.lift_ref
  15.8 3.5 %leaf_taps.1.taps_ref = bf16[2,3,1024,256]{3,2,1,0:T(8,128)(2,1)} custom-call(bf16[2,3,3,3,64,64]{5,4,3,2,1,0:T(8,128)(2,1)} %convs_ref.1), custom_call_target="tpu_custom_call" | custom-call | tf_op jit(solution)/shard_map/leaf_taps/pallas_call | solution.py:180
  19.2 29.3 %all-to-all-done.msg_ref.arrived_ref = bf16[128,72,128]{2,1,0:T(8,128)(2,1)S(1)} async-done(((bf16[128,72,128]{2,1,0:T(8,128)(2,1)}), bf16[128,72,128]{2,1,0:T(8,128)(2,1)S(1)}, u32[]{:S(2)}, u32[]{:S(2)}) %all-to-all-start) | async-done | bytes 2359328 | tf_op jit(solution)/shard_map/all_to_all | solution.py:653
  48.5 18.2 %scatter.1 = (bf16[256,1024]{1,0:T(8,128)(2,1)S(1)}, bf16[256,1024]{1,0:T(8,128)(2,1)S(1)}, bf16[64,1024]{1,0:T(8,128)(2,1)S(1)}, bf16[64,1024]{1,0:T(8,128)(2,1...) custom-call(bf16[128,72,128]{2,1,0:T(8,128)(2,1)S(1)} %all-to-all-done.msg_ref.arrived_ref), custom_call_target="tpu_custom_call" | custom-call | tf_op jit(solution)/shard_map/scatter/pallas_call | solution.py:145
  66.7 0.8 collective-permute-start
  67.6 4.6 %collective-permute-start.1 = (bf16[64,1024]{1,0:T(8,128)(2,1)S(1)}, bf16[64,1024]{1,0:T(8,128)(2,1)S(1)}, u32[]{:S(2)}, u32[]{:S(2)}) collective-permute-start(bf16[64,1024]{1,0:T(8,128)(2,1)S(1)} %get-tuple-element.29), channel_id=1, source_target_pairs={{0,120},{8,0},{16,8},{24,16},{32,24},{40,32},{48,40},{56,48},{64,5... | collective-permute-start | bytes 393224 | tf_op jit(solution)/shard_map/ppermute | solution.py:646
  72.1 1.8 %leaf_own.1 = (bf16[256,2048]{1,0:T(8,128)(2,1)S(1)}, bf16[256,2048]{1,0:T(8,128)(2,1)S(1)}, f32[16,8,128]{2,1,0:T(8,128)S(1)}) custom-call(bf16[256,1024]{1,0:T(8,128)(2,1)S(1)} %get-tuple-element.24.coarse_ref, bf16[256,1024]{1,0:T(8,128)(2,1)S(1)} %get-tuple-element.25.fine_ref, bf16[256,512]{1,0:T(8,128)(2,1)S(1)} %mul.27.lift_ref, ...), custom_call_target="tpu_custom_call" | custom-call | tf_op jit(solution)/shard_map/leaf_own/pallas_call | solution.py:296
  74.0 1.1 collective-permute-done.west_ref
  75.1 0.0 collective-permute-start.2
  75.2 0.5 collective-permute-start.3
  75.7 5.1 %leaf_middle.1 = (bf16[352,1792]{1,0:T(8,128)(2,1)S(1)}, bf16[352,1792]{1,0:T(8,128)(2,1)S(1)}, bf16[384,256]{1,0:T(8,128)(2,1)S(1)}, bf16[384,256]{1,0:T(8,128)(2,1)S(1)}) custom-call(bf16[256,2048]{1,0:T(8,128)(2,1)S(1)} %get-tuple-element.27.cells_ref, bf16[64,1024]{1,0:T(8,128)(2,1)S(1)} %collective-permute-done.west_ref, ...), custom_call_target="tpu_custom_call" | custom-call | tf_op jit(solution)/shard_map/leaf_middle/pallas_call | solution.py:360
  80.8 0.7 collective-permute-done.3.south_ref
  81.5 13.8 %leaf_border.1 = (bf16[16,16,16,128]{3,2,1,0:T(8,128)(2,1)}, bf16[128,128]{1,0:T(8,128)(2,1)S(1)}) custom-call(bf16[384,256]{1,0:T(8,128)(2,1)S(1)} %get-tuple-element.36.low_ref, bf16[384,256]{1,0:T(8,128)(2,1)S(1)} %get-tuple-element.37.high_ref, bf16[384,256]{1,0:T(8,128)(2,1)S(1)} %collective-permute-done.2.north_ref, ...), custom_call_target="tpu_custom_call" | custom-call | tf_op jit(solution)/shard_map/leaf_border/pallas_call | solution.py:522
  95.3 0.1 collective-permute-start.5
  95.4 5.4 %collective-permute-start.4 = (bf16[128,128]{1,0:T(8,128)(2,1)S(1)}, bf16[128,128]{1,0:T(8,128)(2,1)S(1)}, u32[]{:S(2)}, u32[]{:S(2)}) collective-permute-start(bf16[128,128]{1,0:T(8,128)(2,1)S(1)} %get-tuple-element.43), channel_id=1, source_target_pairs={{0,120},{8,0},{16,8},{24,16},{32,24},{40,32},{48,40},{56,48},{64,5... | collective-permute-start | bytes 98312 | tf_op jit(solution)/shard_map/ppermute | solution.py:646
  100.8 1.8 %collective-permute-done.5 = bf16[128,128]{1,0:T(8,128)(2,1)S(1)} collective-permute-done((bf16[128,128]{1,0:T(8,128)(2,1)S(1)}, bf16[128,128]{1,0:T(8,128)(2,1)S(1)}, u32[]{:S(2)}, u32[]{:S(2)}) %collective-permute-start.5) | collective-permute-done | bytes 32800 | tf_op jit(solution)/shard_map/ppermute | solution.py:646
  102.6 0.0 collective-permute-start.7
  102.7 2.9 %collective-permute-start.6 = (bf16[3,128,128]{2,1,0:T(8,128)(2,1)S(1)}, bf16[3,128,128]{2,1,0:T(8,128)(2,1)S(1)}, u32[]{:S(2)}, u32[]{:S(2)}) collective-permute-start(bf16[3,128,128]{2,1,0:T(8,128)(2,1)S(1)} %pad_maximum_fusion.2.middle_ref), channel_id=1, source_target_pairs={{0,7},{1,0},{2,1},{3,2},{4,3},{5,4},{6,5},{7,6},{8,15},{9,8},{10,9... | collective-permute-start | bytes 294920 | tf_op jit(solution)/shard_map/ppermute | solution.py:646
  105.6 2.3 %collective-permute-done.7.south_ref = bf16[3,128,128]{2,1,0:T(8,128)(2,1)S(1)} collective-permute-done((bf16[3,128,128]{2,1,0:T(8,128)(2,1)S(1)}, bf16[3,128,128]{2,1,0:T(8,128)(2,1)S(1)}, u32[]{:S(2)}, u32[]{:S(2)}) %collective-permute-start.7) | collective-permute-done | bytes 98336 | tf_op jit(solution)/shard_map/ppermute | solution.py:646
  107.9 2.4 %coarse_levels.1 = bf16[2,2,4,128]{3,2,1,0:T(4,128)(2,1)} custom-call(bf16[3,128,128]{2,1,0:T(8,128)(2,1)S(1)} %collective-permute-done.6.north_ref, bf16[3,128,128]{2,1,0:T(8,128)(2,1)S(1)} %pad_maximum_fusion.2.middle_ref, bf16[3,128,128]{2,1,0:T(8,128)(2,1)S(1)} %collective-permute-done.7.south_ref, bf16[3,3,3,3,128,128]{5,4,3,2,1,0:T(8,128)(2,1)S(1)} %copy-done.1, ...), custom_call_target="tpu_custom_call" | custom-call | tf_op jit(solution)/shard_map/coarse_levels/pallas_call | solution.py:634
  (18 shorter events, 0.1 us)
Async XLA Ops:
  4.1 11.2 %copy-start.4 = (bf16[32,64]{1,0:T(8,128)(2,1)S(1)}, bf16[32,64]{1,0:T(8,128)(2,1)}, u32[]{:S(2)}) copy-start(bf16[32,64]{1,0:T(8,128)(2,1)} %param.11) | copy-start | bytes 12292
  4.2 44.4 %all-to-all-start = ((bf16[128,72,128]{2,1,0:T(8,128)(2,1)}), bf16[128,72,128]{2,1,0:T(8,128)(2,1)S(1)}, u32[]{:S(2)}, u32[]{:S(2)}) async-start(bf16[128,72,128]{2,1,0:T(8,128)(2,1)} %pack.1), calls=%async_computation | async-start | bytes 4718592 | tf_op jit(solution)/shard_map/all_to_all | solution.py:653
  66.7 8.4 %collective-permute-start = (bf16[64,1024]{1,0:T(8,128)(2,1)S(1)}, bf16[64,1024]{1,0:T(8,128)(2,1)S(1)}, u32[]{:S(2)}, u32[]{:S(2)}) collective-permute-start(bf16[64,1024]{1,0:T(8,128)(2,1)S(1)} %get-tuple-element.28), channel_id=1, source_target_pairs={{0,8},{8,16},{16,24},{24,32},{32,40},{40,48},{48,56},{56,64},{64,7... | collective-permute-start | bytes 393224 | tf_op jit(solution)/shard_map/ppermute | solution.py:646
  67.6 7.5 %collective-permute-start.1 = (bf16[64,1024]{1,0:T(8,128)(2,1)S(1)}, bf16[64,1024]{1,0:T(8,128)(2,1)S(1)}, u32[]{:S(2)}, u32[]{:S(2)}) collective-permute-start(bf16[64,1024]{1,0:T(8,128)(2,1)S(1)} %get-tuple-element.29), channel_id=1, source_target_pairs={{0,120},{8,0},{16,8},{24,16},{32,24},{40,32},{48,40},{56,48},{64,5... | collective-permute-start | bytes 393224 | tf_op jit(solution)/shard_map/ppermute | solution.py:646
  72.1 3.5 %copy-start = (bf16[2,3,1024,256]{3,2,1,0:T(8,128)(2,1)S(1)}, bf16[2,3,1024,256]{3,2,1,0:T(8,128)(2,1)}, u32[]{:S(2)}) copy-start(bf16[2,3,1024,256]{3,2,1,0:T(8,128)(2,1)} %leaf_taps.1.taps_ref) | copy-start | bytes 9437188
  75.1 5.7 %collective-permute-start.2 = (bf16[384,256]{1,0:T(8,128)(2,1)S(1)}, bf16[384,256]{1,0:T(8,128)(2,1)S(1)}, u32[]{:S(2)}, u32[]{:S(2)}) collective-permute-start(bf16[384,256]{1,0:T(8,128)(2,1)S(1)} %pad_maximum_fusion), channel_id=1, source_target_pairs={{0,7},{1,0},{2,1},{3,2},{4,3},{5,4},{6,5},{7,6},{8,15},{9,8},{10,9... | collective-permute-start | bytes 589832 | tf_op jit(solution)/shard_map/ppermute | solution.py:646
  75.2 6.3 %collective-permute-start.3 = (bf16[384,256]{1,0:T(8,128)(2,1)S(1)}, bf16[384,256]{1,0:T(8,128)(2,1)S(1)}, u32[]{:S(2)}, u32[]{:S(2)}) collective-permute-start(bf16[384,256]{1,0:T(8,128)(2,1)S(1)} %pad_maximum_fusion.1), channel_id=1, source_target_pairs={{0,1},{1,2},{2,3},{3,4},{4,5},{5,6},{6,7},{7,0},{8,9},{9,10},{10,1... | collective-permute-start | bytes 589832 | tf_op jit(solution)/shard_map/ppermute | solution.py:646
  75.7 5.8 %copy-start.3 = (bf16[2,2,2,64,128]{4,3,2,1,0:T(8,128)(2,1)S(1)}, bf16[2,2,2,64,128]{4,3,2,1,0:T(8,128)(2,1)}, u32[]{:S(2)}) copy-start(bf16[2,2,2,64,128]{4,3,2,1,0:T(8,128)(2,1)} %down_leaf_ref.1) | copy-start | bytes 393220
  81.5 26.4 %copy-start.1 = (bf16[3,3,3,3,128,128]{5,4,3,2,1,0:T(8,128)(2,1)S(1)}, bf16[3,3,3,3,128,128]{5,4,3,2,1,0:T(8,128)(2,1)}, u32[]{:S(2)}) copy-start(bf16[3,3,3,3,128,128]{5,4,3,2,1,0:T(8,128)(2,1)} %coarse_ref.3) | copy-start | bytes 7962628
  81.5 26.4 %copy-start.2 = (bf16[2,2,2,2,128,128]{5,4,3,2,1,0:T(8,128)(2,1)S(1)}, bf16[2,2,2,2,128,128]{5,4,3,2,1,0:T(8,128)(2,1)}, u32[]{:S(2)}) copy-start(bf16[2,2,2,2,128,128]{5,4,3,2,1,0:T(8,128)(2,1)} %down_ref.3) | copy-start | bytes 1572868
  95.3 7.3 %collective-permute-start.5 = (bf16[128,128]{1,0:T(8,128)(2,1)S(1)}, bf16[128,128]{1,0:T(8,128)(2,1)S(1)}, u32[]{:S(2)}, u32[]{:S(2)}) collective-permute-start(bf16[128,128]{1,0:T(8,128)(2,1)S(1)} %get-tuple-element.43), channel_id=1, source_target_pairs={{0,8},{8,16},{16,24},{24,32},{32,40},{40,48},{48,56},{56,64},{64,7... | collective-permute-start | bytes 98312 | tf_op jit(solution)/shard_map/ppermute | solution.py:646
  95.4 7.2 %collective-permute-start.4 = (bf16[128,128]{1,0:T(8,128)(2,1)S(1)}, bf16[128,128]{1,0:T(8,128)(2,1)S(1)}, u32[]{:S(2)}, u32[]{:S(2)}) collective-permute-start(bf16[128,128]{1,0:T(8,128)(2,1)S(1)} %get-tuple-element.43), channel_id=1, source_target_pairs={{0,120},{8,0},{16,8},{24,16},{32,24},{40,32},{48,40},{56,48},{64,5... | collective-permute-start | bytes 98312 | tf_op jit(solution)/shard_map/ppermute | solution.py:646
  102.6 5.3 %collective-permute-start.7 = (bf16[3,128,128]{2,1,0:T(8,128)(2,1)S(1)}, bf16[3,128,128]{2,1,0:T(8,128)(2,1)S(1)}, u32[]{:S(2)}, u32[]{:S(2)}) collective-permute-start(bf16[3,128,128]{2,1,0:T(8,128)(2,1)S(1)} %pad_maximum_fusion.2.middle_ref), channel_id=1, source_target_pairs={{0,1},{1,2},{2,3},{3,4},{4,5},{5,6},{6,7},{7,0},{8,9},{9,10},{10,1... | collective-permute-start | bytes 294920 | tf_op jit(solution)/shard_map/ppermute | solution.py:646
  102.7 5.2 %collective-permute-start.6 = (bf16[3,128,128]{2,1,0:T(8,128)(2,1)S(1)}, bf16[3,128,128]{2,1,0:T(8,128)(2,1)S(1)}, u32[]{:S(2)}, u32[]{:S(2)}) collective-permute-start(bf16[3,128,128]{2,1,0:T(8,128)(2,1)S(1)} %pad_maximum_fusion.2.middle_ref), channel_id=1, source_target_pairs={{0,7},{1,0},{2,1},{3,2},{4,3},{5,4},{6,5},{7,6},{8,15},{9,8},{10,9... | collective-permute-start | bytes 294920 | tf_op jit(solution)/shard_map/ppermute | solution.py:646

commit v8 on v6

--- a/solution.py
+++ b/solution.py
@@ -421,24 +421,10 @@
         pltpu.make_async_copy(one_z_middle_ref, one_z_ref.at[:, 512:2304], one_sem.at[1]),
         pltpu.make_async_copy(down_leaf_ref, down_leaf_vmem, leaf_sem),
     ]
-    copies = []
-    for dx in range(3):
-        for dz in range(3):
-            copies.append(
-                pltpu.make_async_copy(
-                    coarse_ref.at[0, dx, :, dz], coarse_vmem.at[dx, dz], coarse_sem.at[dx, dz]
-                )
-            )
-    for a in range(2):
-        for b in range(2):
-            for c in range(2):
-                copies.append(
-                    pltpu.make_async_copy(
-                        down_ref.at[0, a, b, c],
-                        down_vmem.at[a, b, :, c * 128 : c * 128 + 128],
-                        down_sem.at[a, b, c],
-                    )
-                )
+    copies = [
+        pltpu.make_async_copy(coarse_ref.at[0], coarse_vmem, coarse_sem),
+        pltpu.make_async_copy(down_ref.at[0], down_vmem, down_sem),
+    ]
     for copy in early + copies:
         copy.start()
     flags = grid_flags()
@@ -516,7 +502,8 @@
                 1,
             )
         )
-    taps = coarse_vmem[...].reshape(3456, 128)
+    taps = [coarse_vmem[dx, :, dz].reshape(384, 128) for dx in range(3) for dz in range(3)]
+    taps = jnp.concatenate(taps, 0)
     total = jnp.dot(jnp.concatenate(windows, 0), taps, preferred_element_type=jnp.float32)
     total = jnp.maximum(total, 0.0).reshape(8, 128, 128)
     masks = [leaf_mask_ref[1 + y // 4, 64:320].reshape(8, 2, 16, 128)[:, 0] for y in range(8)]
@@ -525,7 +512,12 @@
     merged = jnp.concatenate(
         [level[:, b, :, a].reshape(256, 128) for a in range(2) for b in range(2)], 1
     )
-    taps = down_vmem[...].reshape(512, 256)
+    taps = [
+        jnp.concatenate([down_vmem[a, b, c] for c in range(2)], 1)
+        for a in range(2)
+        for b in range(2)
+    ]
+    taps = jnp.concatenate(taps, 0)
     parts = jnp.dot(merged, taps, preferred_element_type=jnp.float32)
     parts_ref[0] = parts[:, :128]
     parts_ref[1] = parts[:, 128:]
@@ -554,12 +546,12 @@
             pltpu.VMEM((2, 256, 128), jnp.float32),
             pltpu.VMEM((2, 2, 2, 64, 128), jnp.bfloat16),
             pltpu.VMEM((3, 3, 3, 128, 128), jnp.bfloat16),
-            pltpu.VMEM((2, 2, 128, 256), jnp.bfloat16),
+            pltpu.VMEM((2, 2, 2, 128, 128), jnp.bfloat16),
             pltpu.VMEM((4, 384, 128), jnp.float32),
             pltpu.SemaphoreType.DMA((2,)),
             pltpu.SemaphoreType.DMA,
-            pltpu.SemaphoreType.DMA((3, 3)),
-            pltpu.SemaphoreType.DMA((2, 2, 2)),
+            pltpu.SemaphoreType.DMA,
+            pltpu.SemaphoreType.DMA,
         ],
         compiler_params=pltpu.CompilerParams(vmem_limit_bytes=32 << 20),
         name="leaf_border",

time: 111 us -> 111 us (level)
  no operation moved by 1% of the time
where the time goes in v8:
time: 111 us; the launch traced here: 110 us
  Pallas kernels  48.4 us (44%)
  waiting for transfers between devices  35.2 us (32%)
  starting transfers between devices  25.5 us (23%)
    all_to_all x1, waiting for transfers between devices, per_device(): lax.all_to_all(messages, ('gx', 'gy'), split_axis=0, concat_axis=0, tiled...  29.3 us
    pallas_call x1, Pallas kernels, scatter(): pl.pallas_call(scatter_kernel, grid=(sources // BUCKETS,), in_specs=[pl.B...  18.2 us
    ppermute x8, starting transfers between devices, ring(): lax.ppermute(values, axis, [(i, (i + step) % count) for i in range(count)])  14.4 us
    pallas_call x1, Pallas kernels, border_part(): pl.pallas_call(border_kernel, out_shape=[jax.ShapeDtypeStruct((16, 16, 16...  13.8 us
    all_to_all x1, starting transfers between devices, per_device(): lax.all_to_all(messages, ('gx', 'gy'), split_axis=0, concat_axis=0, tiled...  11.1 us
    ppermute x8, waiting for transfers between devices, ring(): lax.ppermute(values, axis, [(i, (i + step) % count) for i in range(count)])  5.88 us
    pallas_call x1, Pallas kernels, middle_part(): pl.pallas_call(middle_kernel, out_shape=[jax.ShapeDtypeStruct((352, 1792)...  5.11 us
    pallas_call x1, Pallas kernels, pack_messages(): pl.pallas_call(pack_kernel, in_specs=[pl.BlockSpec(memory_space=pltpu.HBM...  3.51 us
  transfers between devices with their start and end apart: 9, of which 5 were waited for; matrix products, arithmetic and copies ran while one was open for 0% of the time, Pallas kernels for 9%

profile of v8, /device:TPU:0, one launch (start us, length us, event | category | flops | bytes accessed | tf_op | source)
XLA Modules:
  0.0 110.4 jit_solution(2975350107426388283)
XLA Ops:
  0.6 3.5 %pack.1 = bf16[128,72,128]{2,1,0:T(8,128)(2,1)} custom-call(bf16[128,64,128]{2,1,0:T(8,128)(2,1)} %bitcast.8, s32[128,256]{1,0:T(8,128)} %bitcast.9, s32[2,2,4]{2,1,0:T(2,128)} %bricks_ref.1), custom_call_target="tpu_custom_call" | custom-call | tf_op jit(solution)/shard_map/pack/pallas_call | solution.py:66
  4.1 0.0 copy-start.4
  4.2 11.1 %all-to-all-start = ((bf16[128,72,128]{2,1,0:T(8,128)(2,1)}), bf16[128,72,128]{2,1,0:T(8,128)(2,1)S(1)}, u32[]{:S(2)}, u32[]{:S(2)}) async-start(bf16[128,72,128]{2,1,0:T(8,128)(2,1)} %pack.1), calls=%async_computation | async-start | bytes 4718592 | tf_op jit(solution)/shard_map/all_to_all | solution.py:662
  15.3 0.1 broadcast_multiply_fusion
  15.4 0.3 mul.27.lift_ref
  15.8 3.5 %leaf_taps.1.taps_ref = bf16[2,3,1024,256]{3,2,1,0:T(8,128)(2,1)} custom-call(bf16[2,3,3,3,64,64]{5,4,3,2,1,0:T(8,128)(2,1)} %convs_ref.1), custom_call_target="tpu_custom_call" | custom-call | tf_op jit(solution)/shard_map/leaf_taps/pallas_call | solution.py:189
  19.2 29.3 %all-to-all-done.msg_ref.arrived_ref = bf16[128,72,128]{2,1,0:T(8,128)(2,1)S(1)} async-done(((bf16[128,72,128]{2,1,0:T(8,128)(2,1)}), bf16[128,72,128]{2,1,0:T(8,128)(2,1)S(1)}, u32[]{:S(2)}, u32[]{:S(2)}) %all-to-all-start) | async-done | bytes 2359328 | tf_op jit(solution)/shard_map/all_to_all | solution.py:662
  48.5 18.2 %scatter.1 = (bf16[256,1024]{1,0:T(8,128)(2,1)S(1)}, bf16[256,1024]{1,0:T(8,128)(2,1)S(1)}, bf16[64,1024]{1,0:T(8,128)(2,1)S(1)}, bf16[64,1024]{1,0:T(8,128)(2,1...) custom-call(bf16[128,72,128]{2,1,0:T(8,128)(2,1)S(1)} %all-to-all-done.msg_ref.arrived_ref), custom_call_target="tpu_custom_call" | custom-call | tf_op jit(solution)/shard_map/scatter/pallas_call | solution.py:151
  66.8 0.8 collective-permute-start
  67.6 4.6 %collective-permute-start.1 = (bf16[64,1024]{1,0:T(8,128)(2,1)S(1)}, bf16[64,1024]{1,0:T(8,128)(2,1)S(1)}, u32[]{:S(2)}, u32[]{:S(2)}) collective-permute-start(bf16[64,1024]{1,0:T(8,128)(2,1)S(1)} %get-tuple-element.29), channel_id=1, source_target_pairs={{0,120},{8,0},{16,8},{24,16},{32,24},{40,32},{48,40},{56,48},{64,5... | collective-permute-start | bytes 393224 | tf_op jit(solution)/shard_map/ppermute | solution.py:655
  72.2 1.8 %leaf_own.1 = (bf16[256,2048]{1,0:T(8,128)(2,1)S(1)}, bf16[256,2048]{1,0:T(8,128)(2,1)S(1)}, f32[16,8,128]{2,1,0:T(8,128)S(1)}) custom-call(bf16[256,1024]{1,0:T(8,128)(2,1)S(1)} %get-tuple-element.24.coarse_ref, bf16[256,1024]{1,0:T(8,128)(2,1)S(1)} %get-tuple-element.25.fine_ref, bf16[256,512]{1,0:T(8,128)(2,1)S(1)} %mul.27.lift_ref, ...), custom_call_target="tpu_custom_call" | custom-call | tf_op jit(solution)/shard_map/leaf_own/pallas_call | solution.py:305
  74.0 1.1 collective-permute-done.west_ref
  75.2 0.0 collective-permute-start.2
  75.2 0.5 collective-permute-start.3
  75.7 5.1 %leaf_middle.1 = (bf16[352,1792]{1,0:T(8,128)(2,1)S(1)}, bf16[352,1792]{1,0:T(8,128)(2,1)S(1)}, bf16[384,256]{1,0:T(8,128)(2,1)S(1)}, bf16[384,256]{1,0:T(8,128)(2,1)S(1)}) custom-call(bf16[256,2048]{1,0:T(8,128)(2,1)S(1)} %get-tuple-element.27.cells_ref, bf16[64,1024]{1,0:T(8,128)(2,1)S(1)} %collective-permute-done.west_ref, ...), custom_call_target="tpu_custom_call" | custom-call | tf_op jit(solution)/shard_map/leaf_middle/pallas_call | solution.py:369
  80.8 0.7 collective-permute-done.3.south_ref
  81.5 13.8 %leaf_border.1 = (bf16[16,16,16,128]{3,2,1,0:T(8,128)(2,1)}, bf16[128,128]{1,0:T(8,128)(2,1)S(1)}) custom-call(bf16[384,256]{1,0:T(8,128)(2,1)S(1)} %get-tuple-element.36.low_ref, bf16[384,256]{1,0:T(8,128)(2,1)S(1)} %get-tuple-element.37.high_ref, bf16[384,256]{1,0:T(8,128)(2,1)S(1)} %collective-permute-done.2.north_ref, ...), custom_call_target="tpu_custom_call" | custom-call | tf_op jit(solution)/shard_map/leaf_border/pallas_call | solution.py:531
  95.3 0.1 collective-permute-start.5
  95.4 5.4 %collective-permute-start.4 = (bf16[128,128]{1,0:T(8,128)(2,1)S(1)}, bf16[128,128]{1,0:T(8,128)(2,1)S(1)}, u32[]{:S(2)}, u32[]{:S(2)}) collective-permute-start(bf16[128,128]{1,0:T(8,128)(2,1)S(1)} %get-tuple-element.43), channel_id=1, source_target_pairs={{0,120},{8,0},{16,8},{24,16},{32,24},{40,32},{48,40},{56,48},{64,5... | collective-permute-start | bytes 98312 | tf_op jit(solution)/shard_map/ppermute | solution.py:655
  100.8 1.8 %collective-permute-done.5 = bf16[128,128]{1,0:T(8,128)(2,1)S(1)} collective-permute-done((bf16[128,128]{1,0:T(8,128)(2,1)S(1)}, bf16[128,128]{1,0:T(8,128)(2,1)S(1)}, u32[]{:S(2)}, u32[]{:S(2)}) %collective-permute-start.5) | collective-permute-done | bytes 32800 | tf_op jit(solution)/shard_map/ppermute | solution.py:655
  102.7 0.0 collective-permute-start.7
  102.7 2.9 %collective-permute-start.6 = (bf16[3,128,128]{2,1,0:T(8,128)(2,1)S(1)}, bf16[3,128,128]{2,1,0:T(8,128)(2,1)S(1)}, u32[]{:S(2)}, u32[]{:S(2)}) collective-permute-start(bf16[3,128,128]{2,1,0:T(8,128)(2,1)S(1)} %pad_maximum_fusion.2.middle_ref), channel_id=1, source_target_pairs={{0,7},{1,0},{2,1},{3,2},{4,3},{5,4},{6,5},{7,6},{8,15},{9,8},{10,9... | collective-permute-start | bytes 294920 | tf_op jit(solution)/shard_map/ppermute | solution.py:655
  105.6 2.3 %collective-permute-done.7.south_ref = bf16[3,128,128]{2,1,0:T(8,128)(2,1)S(1)} collective-permute-done((bf16[3,128,128]{2,1,0:T(8,128)(2,1)S(1)}, bf16[3,128,128]{2,1,0:T(8,128)(2,1)S(1)}, u32[]{:S(2)}, u32[]{:S(2)}) %collective-permute-start.7) | collective-permute-done | bytes 98336 | tf_op jit(solution)/shard_map/ppermute | solution.py:655
  108.0 2.4 %coarse_levels.1 = bf16[2,2,4,128]{3,2,1,0:T(4,128)(2,1)} custom-call(bf16[3,128,128]{2,1,0:T(8,128)(2,1)S(1)} %collective-permute-done.6.north_ref, bf16[3,128,128]{2,1,0:T(8,128)(2,1)S(1)} %pad_maximum_fusion.2.middle_ref, bf16[3,128,128]{2,1,0:T(8,128)(2,1)S(1)} %collective-permute-done.7.south_ref, bf16[3,3,3,3,128,128]{5,4,3,2,1,0:T(8,128)(2,1)S(1)} %copy-done.1, ...), custom_call_target="tpu_custom_call" | custom-call | tf_op jit(solution)/shard_map/coarse_levels/pallas_call | solution.py:643
  (18 shorter events, 0.1 us)
Async XLA Ops:
  4.1 11.2 %copy-start.4 = (bf16[32,64]{1,0:T(8,128)(2,1)S(1)}, bf16[32,64]{1,0:T(8,128)(2,1)}, u32[]{:S(2)}) copy-start(bf16[32,64]{1,0:T(8,128)(2,1)} %param.11) | copy-start | bytes 12292
  4.2 44.4 %all-to-all-start = ((bf16[128,72,128]{2,1,0:T(8,128)(2,1)}), bf16[128,72,128]{2,1,0:T(8,128)(2,1)S(1)}, u32[]{:S(2)}, u32[]{:S(2)}) async-start(bf16[128,72,128]{2,1,0:T(8,128)(2,1)} %pack.1), calls=%async_computation | async-start | bytes 4718592 | tf_op jit(solution)/shard_map/all_to_all | solution.py:662
  66.8 8.4 %collective-permute-start = (bf16[64,1024]{1,0:T(8,128)(2,1)S(1)}, bf16[64,1024]{1,0:T(8,128)(2,1)S(1)}, u32[]{:S(2)}, u32[]{:S(2)}) collective-permute-start(bf16[64,1024]{1,0:T(8,128)(2,1)S(1)} %get-tuple-element.28), channel_id=1, source_target_pairs={{0,8},{8,16},{16,24},{24,32},{32,40},{40,48},{48,56},{56,64},{64,7... | collective-permute-start | bytes 393224 | tf_op jit(solution)/shard_map/ppermute | solution.py:655
  67.6 7.5 %collective-permute-start.1 = (bf16[64,1024]{1,0:T(8,128)(2,1)S(1)}, bf16[64,1024]{1,0:T(8,128)(2,1)S(1)}, u32[]{:S(2)}, u32[]{:S(2)}) collective-permute-start(bf16[64,1024]{1,0:T(8,128)(2,1)S(1)} %get-tuple-element.29), channel_id=1, source_target_pairs={{0,120},{8,0},{16,8},{24,16},{32,24},{40,32},{48,40},{56,48},{64,5... | collective-permute-start | bytes 393224 | tf_op jit(solution)/shard_map/ppermute | solution.py:655
  72.2 3.5 %copy-start = (bf16[2,3,1024,256]{3,2,1,0:T(8,128)(2,1)S(1)}, bf16[2,3,1024,256]{3,2,1,0:T(8,128)(2,1)}, u32[]{:S(2)}) copy-start(bf16[2,3,1024,256]{3,2,1,0:T(8,128)(2,1)} %leaf_taps.1.taps_ref) | copy-start | bytes 9437188
  75.2 5.7 %collective-permute-start.2 = (bf16[384,256]{1,0:T(8,128)(2,1)S(1)}, bf16[384,256]{1,0:T(8,128)(2,1)S(1)}, u32[]{:S(2)}, u32[]{:S(2)}) collective-permute-start(bf16[384,256]{1,0:T(8,128)(2,1)S(1)} %pad_maximum_fusion), channel_id=1, source_target_pairs={{0,7},{1,0},{2,1},{3,2},{4,3},{5,4},{6,5},{7,6},{8,15},{9,8},{10,9... | collective-permute-start | bytes 589832 | tf_op jit(solution)/shard_map/ppermute | solution.py:655
  75.2 6.3 %collective-permute-start.3 = (bf16[384,256]{1,0:T(8,128)(2,1)S(1)}, bf16[384,256]{1,0:T(8,128)(2,1)S(1)}, u32[]{:S(2)}, u32[]{:S(2)}) collective-permute-start(bf16[384,256]{1,0:T(8,128)(2,1)S(1)} %pad_maximum_fusion.1), channel_id=1, source_target_pairs={{0,1},{1,2},{2,3},{3,4},{4,5},{5,6},{6,7},{7,0},{8,9},{9,10},{10,1... | collective-permute-start | bytes 589832 | tf_op jit(solution)/shard_map/ppermute | solution.py:655
  75.7 5.8 %copy-start.3 = (bf16[2,2,2,64,128]{4,3,2,1,0:T(8,128)(2,1)S(1)}, bf16[2,2,2,64,128]{4,3,2,1,0:T(8,128)(2,1)}, u32[]{:S(2)}) copy-start(bf16[2,2,2,64,128]{4,3,2,1,0:T(8,128)(2,1)} %down_leaf_ref.1) | copy-start | bytes 393220
  81.5 26.4 %copy-start.1 = (bf16[3,3,3,3,128,128]{5,4,3,2,1,0:T(8,128)(2,1)S(1)}, bf16[3,3,3,3,128,128]{5,4,3,2,1,0:T(8,128)(2,1)}, u32[]{:S(2)}) copy-start(bf16[3,3,3,3,128,128]{5,4,3,2,1,0:T(8,128)(2,1)} %coarse_ref.3) | copy-start | bytes 7962628
  81.5 26.4 %copy-start.2 = (bf16[2,2,2,2,128,128]{5,4,3,2,1,0:T(8,128)(2,1)S(1)}, bf16[2,2,2,2,128,128]{5,4,3,2,1,0:T(8,128)(2,1)}, u32[]{:S(2)}) copy-start(bf16[2,2,2,2,128,128]{5,4,3,2,1,0:T(8,128)(2,1)} %down_ref.3) | copy-start | bytes 1572868
  95.3 7.3 %collective-permute-start.5 = (bf16[128,128]{1,0:T(8,128)(2,1)S(1)}, bf16[128,128]{1,0:T(8,128)(2,1)S(1)}, u32[]{:S(2)}, u32[]{:S(2)}) collective-permute-start(bf16[128,128]{1,0:T(8,128)(2,1)S(1)} %get-tuple-element.43), channel_id=1, source_target_pairs={{0,8},{8,16},{16,24},{24,32},{32,40},{40,48},{48,56},{56,64},{64,7... | collective-permute-start | bytes 98312 | tf_op jit(solution)/shard_map/ppermute | solution.py:655
  95.4 7.2 %collective-permute-start.4 = (bf16[128,128]{1,0:T(8,128)(2,1)S(1)}, bf16[128,128]{1,0:T(8,128)(2,1)S(1)}, u32[]{:S(2)}, u32[]{:S(2)}) collective-permute-start(bf16[128,128]{1,0:T(8,128)(2,1)S(1)} %get-tuple-element.43), channel_id=1, source_target_pairs={{0,120},{8,0},{16,8},{24,16},{32,24},{40,32},{48,40},{56,48},{64,5... | collective-permute-start | bytes 98312 | tf_op jit(solution)/shard_map/ppermute | solution.py:655
  102.7 5.3 %collective-permute-start.7 = (bf16[3,128,128]{2,1,0:T(8,128)(2,1)S(1)}, bf16[3,128,128]{2,1,0:T(8,128)(2,1)S(1)}, u32[]{:S(2)}, u32[]{:S(2)}) collective-permute-start(bf16[3,128,128]{2,1,0:T(8,128)(2,1)S(1)} %pad_maximum_fusion.2.middle_ref), channel_id=1, source_target_pairs={{0,1},{1,2},{2,3},{3,4},{4,5},{5,6},{6,7},{7,0},{8,9},{9,10},{10,1... | collective-permute-start | bytes 294920 | tf_op jit(solution)/shard_map/ppermute | solution.py:655
  102.7 5.2 %collective-permute-start.6 = (bf16[3,128,128]{2,1,0:T(8,128)(2,1)S(1)}, bf16[3,128,128]{2,1,0:T(8,128)(2,1)S(1)}, u32[]{:S(2)}, u32[]{:S(2)}) collective-permute-start(bf16[3,128,128]{2,1,0:T(8,128)(2,1)S(1)} %pad_maximum_fusion.2.middle_ref), channel_id=1, source_target_pairs={{0,7},{1,0},{2,1},{3,2},{4,3},{5,4},{6,5},{7,6},{8,15},{9,8},{10,9... | collective-permute-start | bytes 294920 | tf_op jit(solution)/shard_map/ppermute | solution.py:655
